TPU v7x, 32 devices: a whole 2x2x4 slice. The times are simulated.
32 devices in a mesh: dp: 2 (over y), seq: 16 (over z, x, core).
Axes of the slice: x: 2, y: 2, z: 4, core: 2. Of those that a mesh axis runs over, the one named last changes fastest.
Arguments:
- tokens: bfloat16 [2, 4096, 1024], P('dp', 'seq'), may hold values from -6 to 6
- segment_ids: int32 [2, 4096], P('dp', 'seq'), may hold values from 0 to 7, never falling along the last dimension, each value on 1 to 2048 neighbouring positions
- second_doc: int32 [2, 8], P('dp'), may hold values from 0 to 7, as said below
- memory_index: int32 [2, 32, 8, 128], P('dp', 'seq'), may hold values from 0 to 511
- cache_keys: bfloat16 [2, 8, 256, 1024], P('dp'), may hold values from -6 to 6
- cache_values: bfloat16 [2, 8, 256, 1024], P('dp'), may hold values from -6 to 6
- first_gain: bfloat16 [1024], P(('dp', 'seq')), may hold values from 0.099609375 to 1.8984375
- query_weight: bfloat16 [1024, 1024], P(('dp', 'seq')), may hold values from -0.1875 to 0.1875
- key_weight: bfloat16 [1024, 1024], P(('dp', 'seq')), may hold values from -0.1875 to 0.1875
- value_weight: bfloat16 [1024, 1024], P(('dp', 'seq')), may hold values from -0.1875 to 0.1875
- out_weight: bfloat16 [1024, 1024], P(('dp', 'seq')), may hold values from -1.5 to 1.5
- second_gain: bfloat16 [1024], P(('dp', 'seq')), may hold values from 0.099609375 to 1.8984375
- gate_weight: bfloat16 [1024, 2816], P(('dp', 'seq')), may hold values from -0.1875 to 0.1875
- up_weight: bfloat16 [1024, 2816], P(('dp', 'seq')), may hold values from -0.1875 to 0.1875
- down_weight: bfloat16 [2816, 1024], P(('dp', 'seq')), may hold values from -0.109375 to 0.109375
- cotangent: bfloat16 [2, 4096, 1024], P('dp', 'seq'), may hold values from -6 to 6
Outputs:
- output: bfloat16 [2, 4096, 1024], P('dp', 'seq')
- input_grad: float32 [2, 4096, 1024], P('dp', 'seq')
- first_gain_grad: float32 [1024], P(('dp', 'seq'))
- query_weight_grad: float32 [1024, 1024], P(('dp', 'seq'))
- key_weight_grad: float32 [1024, 1024], P(('dp', 'seq'))
- value_weight_grad: float32 [1024, 1024], P(('dp', 'seq'))
- out_weight_grad: float32 [1024, 1024], P(('dp', 'seq'))
- second_gain_grad: float32 [1024], P(('dp', 'seq'))
- gate_weight_grad: float32 [1024, 2816], P(('dp', 'seq'))
- up_weight_grad: float32 [1024, 2816], P(('dp', 'seq'))
- down_weight_grad: float32 [2816, 1024], P(('dp', 'seq'))
Inputs may be any that keep to these rules, and one draw needn't show every extreme that they name: `segment_ids`: within each sequence the numbers never fall; every document spans at most 2048 positions and one spans exactly 2048. `second_doc`: never the document's own number.
All inputs are finite; a program needn't handle non-finite values.
Results may differ from a plain program's by a relative error of at most 0.018.
Values may be sent and summed in bfloat16 or wider, within the bound.
No kernel may reach another device: no remote copies, remote signals or barrier semaphores. Data moves between devices by JAX's collectives and lax.ppermute only.
A program may use at most 320 MiB of HBM per device.

v0:
```python
import math

import jax
import jax.numpy as jnp
from jax import lax
from jax.sharding import PartitionSpec as P

D = 1024
FF = 2816
HEADS = 8
HEAD_DIM = 128
QUERY_BLOCK = 128
MEM_ROWS = 256
DOC_MAX = 2048


EPSILON = 1e-05
NEGATIVE = -1e30


def from_behind(block, axis, distance):
    devices = range(lax.axis_size(axis))
    route = [(i - distance, i) for i in devices if i - distance in devices]
    return lax.ppermute(block, axis, route)


def normalize(values, gain):
    scale_rows = lax.rsqrt(jnp.mean(values * values, axis=-1, keepdims=True) + EPSILON)
    return values * scale_rows * gain


def norm_backward(values, gain, upstream):
    scale_rows = lax.rsqrt(jnp.mean(values * values, axis=-1, keepdims=True) + EPSILON)
    gain_grad = jnp.sum(upstream * values * scale_rows, axis=0)
    scaled = upstream * gain
    inner = jnp.mean(scaled * values, axis=-1, keepdims=True)
    return (scale_rows * scaled - values * scale_rows * scale_rows * scale_rows * inner, gain_grad)


def angles(positions, half):
    freqs = 10000.0 ** (-jnp.arange(half, dtype=jnp.float32) * 2.0 / (2 * half))
    turned = positions.astype(jnp.float32)[:, None] * freqs[None, :]
    return (jnp.cos(turned)[:, None, :], jnp.sin(turned)[:, None, :])


def rotate(values, cosine, sine):
    half = values.shape[-1] // 2
    first = values[..., :half]
    second = values[..., half:]
    return jnp.concatenate(
        [first * cosine - second * sine, second * cosine + first * sine], axis=-1
    )


def local(
    tokens,
    segment_ids,
    second_doc,
    memory_index,
    cache_keys,
    cache_values,
    first_gain,
    query_weight,
    key_weight,
    value_weight,
    out_weight,
    second_gain,
    gate_weight,
    up_weight,
    down_weight,
    cotangent,
):
    gain_one, query_w, key_w, value_w, out_w, gain_two, gate_w, up_w, down_w = (
        lax.all_gather(first_gain, ("dp", "seq"), axis=0, tiled=True),
        lax.all_gather(query_weight, ("dp", "seq"), axis=0, tiled=True),
        lax.all_gather(key_weight, ("dp", "seq"), axis=0, tiled=True),
        lax.all_gather(value_weight, ("dp", "seq"), axis=0, tiled=True),
        lax.all_gather(out_weight, ("dp", "seq"), axis=0, tiled=True),
        lax.all_gather(second_gain, ("dp", "seq"), axis=0, tiled=True),
        lax.all_gather(gate_weight, ("dp", "seq"), axis=0, tiled=True),
        lax.all_gather(up_weight, ("dp", "seq"), axis=0, tiled=True),
        lax.all_gather(down_weight, ("dp", "seq"), axis=0, tiled=True),
    )
    inputs = tokens[0].astype(jnp.float32)
    count = inputs.shape[0]
    scale = 1.0 / math.sqrt(HEAD_DIM)
    seq_index = lax.axis_index("seq")
    span = min((DOC_MAX - 2) // count + 1, lax.axis_size("seq") - 1)
    positions = seq_index * count + jnp.arange(count, dtype=jnp.int32)
    cosine, sine = angles(positions, HEAD_DIM // 2)
    normed_one = normalize(inputs, gain_one.astype(jnp.float32)).astype(jnp.bfloat16)

    def project(weight):
        return jnp.dot(normed_one, weight, preferred_element_type=jnp.float32).reshape(
            count, HEADS, HEAD_DIM
        )

    queries = rotate(project(query_w), cosine, sine).astype(jnp.bfloat16)
    keys = rotate(project(key_w), cosine, sine).astype(jnp.bfloat16)
    values = project(value_w).astype(jnp.bfloat16)
    segments = segment_ids[0]
    segment_low = segments.astype(jnp.bfloat16)
    blocks = count // QUERY_BLOCK
    partner = second_doc[0]
    docs = partner.shape[0]
    block_docs = segments[::QUERY_BLOCK]
    doc_ids = jnp.arange(docs, dtype=jnp.int32)
    partner_blocks = jnp.sum(
        jnp.where(block_docs[:, None] == doc_ids[None, :], partner[None, :], 0), axis=1
    )
    picked = memory_index[0]
    retrieved = picked.shape[-1]
    from_own = picked < MEM_ROWS
    owner = jnp.where(from_own, block_docs[:, None, None], partner_blocks[:, None, None])
    row_index = jnp.where(from_own, picked, picked - MEM_ROWS)
    head_ids = jnp.arange(HEADS, dtype=jnp.int32)[None, :, None]
    memory_keys = cache_keys[0].reshape(docs, MEM_ROWS, HEADS, HEAD_DIM)[owner, row_index, head_ids]
    memory_values = cache_values[0].reshape(docs, MEM_ROWS, HEADS, HEAD_DIM)[
        owner, row_index, head_ids
    ]
    query_blocks = queries.reshape(blocks, QUERY_BLOCK, HEADS, HEAD_DIM)
    memory_scores = (
        jnp.einsum(
            "bqhd,bhrd->hbqr", query_blocks, memory_keys, preferred_element_type=jnp.float32
        ).reshape(HEADS, count, retrieved)
        * scale
    )
    memory_mask = (segments.reshape(blocks, QUERY_BLOCK) == block_docs[:, None]).reshape(
        1, count, 1
    )
    top = jnp.max(jnp.where(memory_mask, memory_scores, NEGATIVE), axis=-1)
    memory_probs = jnp.where(memory_mask, jnp.exp(memory_scores - top[..., None]), 0.0)
    total = jnp.sum(memory_probs, axis=-1)
    accum = jnp.einsum(
        "hbqr,bhrd->bqhd",
        memory_probs.astype(jnp.bfloat16).reshape(HEADS, blocks, QUERY_BLOCK, retrieved),
        memory_values,
        preferred_element_type=jnp.float32,
    ).reshape(count, HEADS, HEAD_DIM)

    def piece_scores(key_piece, key_segs, key_start, available):
        scores = (
            jnp.einsum("qhd,khd->hqk", queries, key_piece, preferred_element_type=jnp.float32)
            * scale
        )
        key_pos = key_start + jnp.arange(key_piece.shape[0], dtype=jnp.int32)
        allowed = (
            (key_segs[None, :] == segment_low[:, None])
            & (key_pos[None, :] <= positions[:, None])
            & available
        )
        return (scores, allowed[None])

    def absorb(state, scores, allowed, value_piece):
        old_top, old_total, old_accum = state
        fresh = jnp.maximum(old_top, jnp.max(jnp.where(allowed, scores, NEGATIVE), axis=-1))
        decay = jnp.exp(old_top - fresh)
        probs = jnp.where(allowed, jnp.exp(scores - fresh[..., None]), 0.0)
        new_total = old_total * decay + jnp.sum(probs, axis=-1)
        new_accum = old_accum * decay.T[:, :, None] + jnp.einsum(
            "hqk,khd->qhd",
            probs.astype(jnp.bfloat16),
            value_piece,
            preferred_element_type=jnp.float32,
        )
        return (fresh, new_total, new_accum)

    state = (top, total, accum)
    scores, allowed = piece_scores(keys, segment_low, seq_index * count, True)
    state = absorb(state, scores, allowed, values)
    kept = []
    for step in range(1, span + 1):
        moved = from_behind((keys, values, segment_low), "seq", step)
        kept.append(moved)
        scores, allowed = piece_scores(
            moved[0], moved[2], (seq_index - step) * count, seq_index >= step
        )
        state = absorb(state, scores, allowed, moved[1])
    top, total, accum = state
    attention = accum / total.T[:, :, None]
    log_total = top + jnp.log(total)
    attention_low = attention.reshape(count, HEADS * HEAD_DIM).astype(jnp.bfloat16)
    mid = inputs + jnp.dot(attention_low, out_w, preferred_element_type=jnp.float32)
    normed_two = normalize(mid, gain_two.astype(jnp.float32)).astype(jnp.bfloat16)
    gate = jnp.dot(normed_two, gate_w, preferred_element_type=jnp.float32)
    upper = jnp.dot(normed_two, up_w, preferred_element_type=jnp.float32)
    hidden = (jax.nn.silu(gate) * upper).astype(jnp.bfloat16)
    output = (mid + jnp.dot(hidden, down_w, preferred_element_type=jnp.float32)).astype(
        jnp.bfloat16
    )
    gain_one, query_w, key_w, value_w, out_w, gain_two, gate_w, up_w, down_w = (
        lax.all_gather(first_gain, ("dp", "seq"), axis=0, tiled=True),
        lax.all_gather(query_weight, ("dp", "seq"), axis=0, tiled=True),
        lax.all_gather(key_weight, ("dp", "seq"), axis=0, tiled=True),
        lax.all_gather(value_weight, ("dp", "seq"), axis=0, tiled=True),
        lax.all_gather(out_weight, ("dp", "seq"), axis=0, tiled=True),
        lax.all_gather(second_gain, ("dp", "seq"), axis=0, tiled=True),
        lax.all_gather(gate_weight, ("dp", "seq"), axis=0, tiled=True),
        lax.all_gather(up_weight, ("dp", "seq"), axis=0, tiled=True),
        lax.all_gather(down_weight, ("dp", "seq"), axis=0, tiled=True),
    )
    upstream = cotangent[0]
    hidden_grad = jnp.einsum("td,fd->tf", upstream, down_w, preferred_element_type=jnp.float32)
    sigma = jax.nn.sigmoid(gate)
    gate_grad = (hidden_grad * upper * sigma * (1.0 + gate * (1.0 - sigma))).astype(jnp.bfloat16)
    upper_grad = (hidden_grad * gate * sigma).astype(jnp.bfloat16)
    normed_two_grad = jnp.einsum(
        "tf,df->td", gate_grad, gate_w, preferred_element_type=jnp.float32
    ) + jnp.einsum("tf,df->td", upper_grad, up_w, preferred_element_type=jnp.float32)
    mid_part, gain_two_grad = norm_backward(mid, gain_two.astype(jnp.float32), normed_two_grad)
    mid_grad = upstream.astype(jnp.float32) + mid_part
    branch_grad = mid_grad.astype(jnp.bfloat16)
    attention_grad = (
        jnp.einsum("te,de->td", branch_grad, out_w, preferred_element_type=jnp.float32)
        .astype(jnp.bfloat16)
        .reshape(count, HEADS, HEAD_DIM)
    )
    delta = jnp.sum(attention_grad.astype(jnp.float32) * attention, axis=-1).T
    memory_dprob = jnp.einsum(
        "bqhd,bhrd->hbqr",
        attention_grad.reshape(blocks, QUERY_BLOCK, HEADS, HEAD_DIM),
        memory_values,
        preferred_element_type=jnp.float32,
    ).reshape(HEADS, count, retrieved)
    memory_weights = jnp.where(memory_mask, jnp.exp(memory_scores - log_total[..., None]), 0.0)
    memory_score_grad = (memory_weights * (memory_dprob - delta[..., None])).astype(jnp.bfloat16)
    query_grad = (
        jnp.einsum(
            "hbqr,bhrd->bqhd",
            memory_score_grad.reshape(HEADS, blocks, QUERY_BLOCK, retrieved),
            memory_keys,
            preferred_element_type=jnp.float32,
        ).reshape(count, HEADS, HEAD_DIM)
        * scale
    )

    def piece_grads(query_sum, key_piece, value_piece, key_segs, key_start, available):
        scores, allowed = piece_scores(key_piece, key_segs, key_start, available)
        probs = jnp.where(allowed, jnp.exp(scores - log_total[..., None]), 0.0)
        value_part = jnp.einsum(
            "hqk,qhd->khd",
            probs.astype(jnp.bfloat16),
            attention_grad,
            preferred_element_type=jnp.float32,
        )
        prob_grad = jnp.einsum(
            "qhd,khd->hqk", attention_grad, value_piece, preferred_element_type=jnp.float32
        )
        score_grad = (probs * (prob_grad - delta[..., None])).astype(jnp.bfloat16)
        query_sum = (
            query_sum
            + jnp.einsum("hqk,khd->qhd", score_grad, key_piece, preferred_element_type=jnp.float32)
            * scale
        )
        key_part = (
            jnp.einsum("hqk,qhd->khd", score_grad, queries, preferred_element_type=jnp.float32)
            * scale
        )
        return (query_sum, key_part, value_part)

    query_grad, key_total, value_total = piece_grads(
        query_grad, keys, values, segment_low, seq_index * count, True
    )
    for step in range(1, span + 1):
        moved = from_behind((keys, values, segment_low), "seq", step)
        query_grad, key_part, value_part = piece_grads(
            query_grad, moved[0], moved[1], moved[2], (seq_index - step) * count, seq_index >= step
        )
        returned = (
            from_behind(key_part.astype(jnp.bfloat16), "seq", -step).astype(key_part.dtype),
            from_behind(value_part.astype(jnp.bfloat16), "seq", -step).astype(value_part.dtype),
        )
        key_total = key_total + returned[0]
        value_total = value_total + returned[1]
    query_low = (
        rotate(query_grad, cosine, -sine).astype(jnp.bfloat16).reshape(count, HEADS * HEAD_DIM)
    )
    key_low = rotate(key_total, cosine, -sine).astype(jnp.bfloat16).reshape(count, HEADS * HEAD_DIM)
    value_low = value_total.astype(jnp.bfloat16).reshape(count, HEADS * HEAD_DIM)
    normed_one_grad = (
        jnp.einsum("te,de->td", query_low, query_w, preferred_element_type=jnp.float32)
        + jnp.einsum("te,de->td", key_low, key_w, preferred_element_type=jnp.float32)
        + jnp.einsum("te,de->td", value_low, value_w, preferred_element_type=jnp.float32)
    )
    input_part, gain_one_grad = norm_backward(inputs, gain_one.astype(jnp.float32), normed_one_grad)
    input_grad = mid_grad + input_part
    width = D
    hidden_units = FF
    row_sums = lax.psum_scatter(
        jnp.concatenate(
            [
                jnp.einsum("td,te->de", normed_one, query_low, preferred_element_type=jnp.float32),
                jnp.einsum("td,te->de", normed_one, key_low, preferred_element_type=jnp.float32),
                jnp.einsum("td,te->de", normed_one, value_low, preferred_element_type=jnp.float32),
                jnp.einsum(
                    "td,te->de", attention_low, branch_grad, preferred_element_type=jnp.float32
                ),
                jnp.einsum("td,tf->df", normed_two, gate_grad, preferred_element_type=jnp.float32),
                jnp.einsum("td,tf->df", normed_two, upper_grad, preferred_element_type=jnp.float32),
            ],
            axis=1,
        ),
        ("dp", "seq"),
        scatter_dimension=0,
        tiled=True,
    )
    down_sum = lax.psum_scatter(
        jnp.einsum("tf,td->fd", hidden, upstream, preferred_element_type=jnp.float32),
        ("dp", "seq"),
        scatter_dimension=0,
        tiled=True,
    )
    gains = (
        lax.psum_scatter(gain_one_grad, ("dp", "seq"), scatter_dimension=0, tiled=True),
        lax.psum_scatter(gain_two_grad, ("dp", "seq"), scatter_dimension=0, tiled=True),
    )
    query_w_grad = row_sums[:, 0:width]
    key_w_grad = row_sums[:, width : 2 * width]
    value_w_grad = row_sums[:, 2 * width : 3 * width]
    out_w_grad = row_sums[:, 3 * width : 4 * width]
    gate_w_grad = row_sums[:, 4 * width : 4 * width + hidden_units]
    up_w_grad = row_sums[:, 4 * width + hidden_units :]
    return (
        output[None],
        input_grad[None],
        gains[0],
        query_w_grad,
        key_w_grad,
        value_w_grad,
        out_w_grad,
        gains[1],
        gate_w_grad,
        up_w_grad,
        down_sum,
    )


def solution(mesh):
    placed = (
        P("dp", "seq", None),
        P("dp", "seq"),
        P("dp", None),
        P("dp", "seq", None, None),
        P("dp", None, None, None),
        P("dp", None, None, None),
        P(("dp", "seq")),
        P(("dp", "seq"), None),
        P(("dp", "seq"), None),
        P(("dp", "seq"), None),
        P(("dp", "seq"), None),
        P(("dp", "seq")),
        P(("dp", "seq"), None),
        P(("dp", "seq"), None),
        P(("dp", "seq"), None),
        P("dp", "seq", None),
    )
    return jax.shard_map(
        local,
        mesh=mesh,
        in_specs=placed,
        out_specs=(
            P("dp", "seq", None),
            P("dp", "seq", None),
            P(("dp", "seq")),
            P(("dp", "seq"), None),
            P(("dp", "seq"), None),
            P(("dp", "seq"), None),
            P(("dp", "seq"), None),
            P(("dp", "seq")),
            P(("dp", "seq"), None),
            P(("dp", "seq"), None),
            P(("dp", "seq"), None),
        ),
        check_vma=False,
    )
```

profile of v0, /device:TPU:0, one launch (start us, length us, event | category | flops | bytes accessed | tf_op | source)
XLA Modules:
  0.0 1470.0 jit_solution(7796010108947157635)
XLA Ops:
  11.9 6.0 collective-permute-start.21
  17.8 3.6 collective-permute-start.18
  23.5 2.8 collective-permute-start.3
  34.4 38.6 %all-reduce.5 = (bf16[1024]{0:T(1024)(128)(2,1)S(1)}, bf16[1024]{0:T(1024)(128)(2,1)S(1)}) all-reduce(bf16[1024]{0:T(1024)(128)(2,1)S(1)} %dynamic-update-slice, bf16[1024]{0:T(1024)(128)(2,1)S(1)} %dynamic-update-slice.1), channel_id=1, replica_groups=mesh['dp'=2,'seq'=16] {'dp','seq'}, use_global_device_ids=true, to_apply=%add | all-reduce | flops 2048 | bytes 8192
  75.4 5.5 copy.512
  80.8 3.0 copy.511
  83.9 26.9 %gather_fusion.1 = bf16[2048,128]{1,0:T(8,128)(2,1)S(1)} fusion(bf16[8,256,8,128]{3,2,1,0:T(8,128)(2,1)} %bitcast.620, s32[2048]{0:T(1024)S(1)} %fusion.231), kind=kCustom, calls=%fused_computation.1 | custom fusion | bytes 1073152 | tf_op jit(solution)/shard_map/gather | solution.py:117
  110.7 36.1 %gather_fusion = bf16[2048,128]{1,0:T(8,128)(2,1)} fusion(bf16[8,256,8,128]{3,2,1,0:T(8,128)(2,1)} %bitcast.619, s32[2048]{0:T(1024)S(1)} %fusion.231), kind=kCustom, calls=%fused_computation | custom fusion | bytes 1073152 | tf_op jit(solution)/shard_map/gather | solution.py:118
  149.2 2.8 collective-permute-start.9
  151.9 4.3 collective-permute-start.6
  158.7 2.9 copy.329
  163.2 4.6 collective-permute-start.23
  172.3 2.9 copy.325
  177.0 12.6 all-gather.8.cloned.1.call-done
  189.6 2.9 copy.319
  195.0 2.9 collective-permute-start.1
  197.9 8.0 collective-permute-start.22
  218.1 23.8 %collective-permute-start.4 = (bf16[256,8,128]{0,2,1:T(8,128)(2,1)}, bf16[256,8,128]{0,2,1:T(8,128)(2,1)}, u32[]{:S(2)}, u32[]{:S(2)}) collective-permute-start(bf16[256,8,128]{0,2,1:T(8,128)(2,1)} %pad_maximum_fusion.1), channel_id=1, source_target_pairs={{0,2},{1,3},{2,4},{3,5},{4,6},{5,7},{6,8},{7,9},{8,10},{9,11},{10,... | collective-permute-start | bytes 1572872 | tf_op jit(solution)/shard_map/ppermute | solution.py:24
  241.9 3.5 select_reduce_fusion
  246.7 12.4 collective-permute-start.7
  259.1 3.5 select_reduce_fusion.7
  263.9 34.1 %collective-permute-start.10 = (bf16[256,8,128]{0,2,1:T(8,128)(2,1)}, bf16[256,8,128]{0,2,1:T(8,128)(2,1)}, u32[]{:S(2)}, u32[]{:S(2)}) collective-permute-start(bf16[256,8,128]{0,2,1:T(8,128)(2,1)} %pad_maximum_fusion.1), channel_id=1, source_target_pairs={{0,4},{1,5},{2,6},{3,7},{4,8},{5,9},{6,10},{7,11},{8,12},{9,13},{1... | collective-permute-start | bytes 1572872 | tf_op jit(solution)/shard_map/ppermute | solution.py:24
  298.0 3.5 select_reduce_fusion.6
  302.8 3.8 collective-permute-start.13
  306.6 3.5 select_reduce_fusion.5
  312.4 10.4 collective-permute-start.16
  322.7 3.5 select_reduce_fusion.4
  327.6 3.7 collective-permute-done.13
  331.3 50.6 %collective-permute-start.19 = (bf16[256,8,128]{0,2,1:T(8,128)(2,1)}, bf16[256,8,128]{0,2,1:T(8,128)(2,1)}, u32[]{:S(2)}, u32[]{:S(2)}) collective-permute-start(bf16[256,8,128]{0,2,1:T(8,128)(2,1)} %pad_maximum_fusion.1), channel_id=1, source_target_pairs={{0,7},{1,8},{2,9},{3,10},{4,11},{5,12},{6,13},{7,14},{8,15},{16,23... | collective-permute-start | bytes 1572872 | tf_op jit(solution)/shard_map/ppermute | solution.py:24
  381.9 3.5 select_reduce_fusion.3
  388.8 3.5 select_reduce_fusion.2
  393.5 8.2 collective-permute-start.5
  401.7 3.6 select_reduce_fusion.1
  408.0 3.3 fusion.12
  419.4 3.7 fusion.2
  425.1 6.2 collective-permute-start.11
  433.7 9.7 collective-permute-start.14
  445.0 5.7 collective-permute-done.11
  450.7 5.2 collective-permute-start.2
  456.5 13.5 collective-permute-done.14
  485.6 5.9 fusion.334
  491.5 5.9 fusion.333
  497.4 40.9 %all-gather.20.cloned.1.call-done = bf16[2816,1024]{1,0:T(8,128)(2,1)} async-done(((bf16[88,1024]{1,0:T(8,128)(2,1)}), bf16[2816,1024]{1,0:T(8,128)(2,1)}) %all-gather.20.cloned.1.call-update) | async-done | bytes 5767184 | tf_op jit(solution)/shard_map/all_gather | solution.py:82
  538.2 9.3 multiply_convert_fusion
  549.3 5.2 multiply_reduce_fusion
  559.7 3.2 fusion.80
  573.4 3.7 multiply_convert_fusion.11
  606.7 3.0 mul.813
  631.8 4.6 collective-permute-done.25
  642.5 17.0 %collective-permute-done.27 = bf16[256,8,128]{0,2,1:T(8,128)(2,1)S(1)} collective-permute-done((bf16[256,8,128]{0,2,1:T(8,128)(2,1)}, bf16[256,8,128]{0,2,1:T(8,128)(2,1)S(1)}, u32[]{:S(2)}, u32[]{:S(2)}) %collective-permute-start.27) | collective-permute-done | bytes 524320 | tf_op jit(solution)/shard_map/ppermute | solution.py:24
  667.7 116.6 %collective-permute-done.31 = bf16[256,8,128]{0,2,1:T(8,128)(2,1)S(1)} collective-permute-done((bf16[256,8,128]{0,2,1:T(8,128)(2,1)S(1)}, bf16[256,8,128]{0,2,1:T(8,128)(2,1)S(1)}, u32[]{:S(2)}, u32[]{:S(2)}) %collective-permute-start.31) | collective-permute-done | bytes 524320 | tf_op jit(solution)/shard_map/ppermute | solution.py:24
  786.9 8.6 collective-permute-done.39
  799.9 2.9 convolution_dynamic-update-slice_fusion.5
  802.9 2.9 convolution_dynamic-update-slice_fusion.4
  805.8 25.1 %collective-permute-done.35 = bf16[256,8,128]{0,2,1:T(8,128)(2,1)S(1)} collective-permute-done((bf16[256,8,128]{0,2,1:T(8,128)(2,1)S(1)}, bf16[256,8,128]{0,2,1:T(8,128)(2,1)S(1)}, u32[]{:S(2)}, u32[]{:S(2)}) %collective-permute-start.35) | collective-permute-done | bytes 524320 | tf_op jit(solution)/shard_map/ppermute | solution.py:24
  831.9 2.9 convolution_dynamic-update-slice_fusion.3
  834.8 2.7 convolution_dynamic-update-slice_fusion.2
  837.6 5.9 convolution_dynamic-update-slice_fusion.1
  843.5 6.0 convolution_dynamic-update-slice_fusion
  850.6 7.3 fusion.207
  858.0 5.7 fusion.96
  868.1 79.1 %all-reduce.4 = (f32[1024]{0:T(1024)S(1)}, f32[1024]{0:T(1024)S(1)}) all-reduce(f32[1024]{0:T(1024)S(1)} %get-tuple-element.13, f32[1024]{0:T(1024)S(1)} %copy-done.156), channel_id=2, replica_groups=mesh['dp'=2,'seq'=16] {'dp','seq'}, use_global_device_ids=true, to_apply=%region_27.28.clone | all-reduce | flops 2048 | bytes 16384
  949.7 350.9 %reduce-scatter.3.cloned.1.call-done = f32[32,9728]{1,0:T(8,128)} async-done(((f32[1024,9728]{1,0:T(8,128)}), f32[32,9728]{1,0:T(8,128)}) %reduce-scatter.3.cloned.1.call-update) | async-done | bytes 1245200 | tf_op jit(solution)/shard_map/reduce_scatter | solution.py:289
  1304.5 158.8 %reduce-scatter.5.cloned.1.call-done = f32[88,1024]{1,0:T(8,128)} async-done(((f32[2816,1024]{1,0:T(8,128)}), f32[88,1024]{1,0:T(8,128)}) %reduce-scatter.5.cloned.1.call-update) | async-done | bytes 360464 | tf_op jit(solution)/shard_map/reduce_scatter | solution.py:307
  (547 shorter events, 190.8 us)
Async XLA Ops:
  7.2 151.5 %all-gather.12.cloned.1.call-start = ((), (), s32[]{:S(2)}) async-start(), calls=%async_computation.4 | async-start | bytes 2162688 | tf_op jit(solution)/shard_map/all_gather | solution.py:77
  7.9 164.4 %all-gather.10.cloned.1.call-start = ((), (), s32[]{:S(2)}) async-start(), calls=%async_computation.3 | async-start | bytes 2162688 | tf_op jit(solution)/shard_map/all_gather | solution.py:76
  8.7 180.9 %all-gather.8.cloned.1.call-start = ((), (), s32[]{:S(2)}) async-start(), calls=%async_computation.2 | async-start | bytes 2162688 | tf_op jit(solution)/shard_map/all_gather | solution.py:75
  9.4 471.7 %all-gather.14.cloned.1.call-start = ((), (), s32[]{:S(2)}) async-start(), calls=%async_computation.5 | async-start | bytes 2162688 | tf_op jit(solution)/shard_map/all_gather | solution.py:78
  10.0 475.6 %all-gather.18.cloned.1.call-start = ((), (), s32[]{:S(2)}) async-start(), calls=%async_computation.7 | async-start | bytes 5947392 | tf_op jit(solution)/shard_map/all_gather | solution.py:81
  10.6 480.9 %all-gather.16.cloned.1.call-start = ((), (), s32[]{:S(2)}) async-start(), calls=%async_computation.6 | async-start | bytes 5947392 | tf_op jit(solution)/shard_map/all_gather | solution.py:80
  11.1 527.1 %all-gather.20.cloned.1.call-start = ((), (), s32[]{:S(2)}) async-start(), calls=%async_computation.8 | async-start | bytes 5947392 | tf_op jit(solution)/shard_map/all_gather | solution.py:82
  11.9 135.0 %collective-permute-start.21 = (bf16[256]{0:T(256)(128)(2,1)S(1)}, bf16[256]{0:T(256)(128)(2,1)S(1)}, u32[]{:S(2)}, u32[]{:S(2)}) collective-permute-start(bf16[256]{0:T(256)(128)(2,1)S(1)} %convert_element_type.365), channel_id=1, source_target_pairs={{0,8},{1,9},{2,10},{3,11},{4,12},{5,13},{6,14},{7,15},{16,24},{17,... | collective-permute-start | bytes 1544 | tf_op jit(solution)/shard_map/ppermute | solution.py:24
  17.8 139.3 %collective-permute-start.18 = (bf16[256]{0:T(256)(128)(2,1)S(1)}, bf16[256]{0:T(256)(128)(2,1)S(1)}, u32[]{:S(2)}, u32[]{:S(2)}) collective-permute-start(bf16[256]{0:T(256)(128)(2,1)S(1)} %convert_element_type.365), channel_id=1, source_target_pairs={{0,7},{1,8},{2,9},{3,10},{4,11},{5,12},{6,13},{7,14},{8,15},{16,23... | collective-permute-start | bytes 1544 | tf_op jit(solution)/shard_map/ppermute | solution.py:24
  21.4 135.7 %collective-permute-start.15 = (bf16[256]{0:T(256)(128)(2,1)S(1)}, bf16[256]{0:T(256)(128)(2,1)S(1)}, u32[]{:S(2)}, u32[]{:S(2)}) collective-permute-start(bf16[256]{0:T(256)(128)(2,1)S(1)} %convert_element_type.365), channel_id=1, source_target_pairs={{0,6},{1,7},{2,8},{3,9},{4,10},{5,11},{6,12},{7,13},{8,14},{9,15},... | collective-permute-start | bytes 1544 | tf_op jit(solution)/shard_map/ppermute | solution.py:24
  23.5 125.6 %collective-permute-start.3 = (bf16[256]{0:T(256)(128)(2,1)S(1)}, bf16[256]{0:T(256)(128)(2,1)S(1)}, u32[]{:S(2)}, u32[]{:S(2)}) collective-permute-start(bf16[256]{0:T(256)(128)(2,1)S(1)} %convert_element_type.365), channel_id=1, source_target_pairs={{0,2},{1,3},{2,4},{3,5},{4,6},{5,7},{6,8},{7,9},{8,10},{9,11},{10,... | collective-permute-start | bytes 1544 | tf_op jit(solution)/shard_map/ppermute | solution.py:24
  26.4 125.6 %collective-permute-start = (bf16[256]{0:T(256)(128)(2,1)S(1)}, bf16[256]{0:T(256)(128)(2,1)S(1)}, u32[]{:S(2)}, u32[]{:S(2)}) collective-permute-start(bf16[256]{0:T(256)(128)(2,1)S(1)} %convert_element_type.365), channel_id=1, source_target_pairs={{0,1},{1,2},{2,3},{3,4},{4,5},{5,6},{6,7},{7,8},{8,9},{9,10},{10,1... | collective-permute-start | bytes 1544 | tf_op jit(solution)/shard_map/ppermute | solution.py:24
  27.7 1272.9 %reduce-scatter.3.cloned.1.call-start = ((), (), s32[]{:S(2)}) async-start(), calls=%async_computation.9 | async-start | bytes 41091072 | tf_op jit(solution)/shard_map/reduce_scatter | solution.py:289
  110.7 99.5 %copy-start.40 = (bf16[2048,128]{1,0:T(8,128)(2,1)}, bf16[2048,128]{1,0:T(8,128)(2,1)S(1)}, u32[]{:S(2)}) copy-start(bf16[2048,128]{1,0:T(8,128)(2,1)S(1)} %gather_fusion.1) | copy-start | bytes 1572868
  146.9 10.3 collective-permute-start.12
  149.2 8.0 collective-permute-start.9
  151.9 5.5 collective-permute-start.6
  163.2 311.4 %collective-permute-start.23 = (bf16[256,8,128]{2,0,1:T(8,128)(2,1)}, bf16[256,8,128]{2,0,1:T(8,128)(2,1)}, u32[]{:S(2)}, u32[]{:S(2)}) collective-permute-start(bf16[256,8,128]{2,0,1:T(8,128)(2,1)} %convolution_convert_fusion.9), channel_id=1, source_target_pairs={{0,8},{1,9},{2,10},{3,11},{4,12},{5,13},{6,14},{7,15},{16,24},{17,... | collective-permute-start | bytes 1572872 | tf_op jit(solution)/shard_map/ppermute | solution.py:24
  167.8 304.9 %collective-permute-start.20 = (bf16[256,8,128]{2,0,1:T(8,128)(2,1)}, bf16[256,8,128]{2,0,1:T(8,128)(2,1)}, u32[]{:S(2)}, u32[]{:S(2)}) collective-permute-start(bf16[256,8,128]{2,0,1:T(8,128)(2,1)} %convolution_convert_fusion.9), channel_id=1, source_target_pairs={{0,7},{1,8},{2,9},{3,10},{4,11},{5,12},{6,13},{7,14},{8,15},{16,23... | collective-permute-start | bytes 1572872 | tf_op jit(solution)/shard_map/ppermute | solution.py:24
  169.9 301.0 %collective-permute-start.17 = (bf16[256,8,128]{2,0,1:T(8,128)(2,1)}, bf16[256,8,128]{2,0,1:T(8,128)(2,1)}, u32[]{:S(2)}, u32[]{:S(2)}) collective-permute-start(bf16[256,8,128]{2,0,1:T(8,128)(2,1)} %convolution_convert_fusion.9), channel_id=1, source_target_pairs={{0,6},{1,7},{2,8},{3,9},{4,10},{5,11},{6,12},{7,13},{8,14},{9,15},... | collective-permute-start | bytes 1572872 | tf_op jit(solution)/shard_map/ppermute | solution.py:24
  195.0 51.7 %collective-permute-start.1 = (bf16[256,8,128]{0,2,1:T(8,128)(2,1)}, bf16[256,8,128]{0,2,1:T(8,128)(2,1)}, u32[]{:S(2)}, u32[]{:S(2)}) collective-permute-start(bf16[256,8,128]{0,2,1:T(8,128)(2,1)} %pad_maximum_fusion.1), channel_id=1, source_target_pairs={{0,1},{1,2},{2,3},{3,4},{4,5},{5,6},{6,7},{7,8},{8,9},{9,10},{10,1... | collective-permute-start | bytes 1572872 | tf_op jit(solution)/shard_map/ppermute | solution.py:24
  197.9 20.2 %collective-permute-start.22 = (bf16[256,8,128]{0,2,1:T(8,128)(2,1)}, bf16[256,8,128]{0,2,1:T(8,128)(2,1)}, u32[]{:S(2)}, u32[]{:S(2)}) collective-permute-start(bf16[256,8,128]{0,2,1:T(8,128)(2,1)} %pad_maximum_fusion.1), channel_id=1, source_target_pairs={{0,8},{1,9},{2,10},{3,11},{4,12},{5,13},{6,14},{7,15},{16,24},{17,... | collective-permute-start | bytes 1572872 | tf_op jit(solution)/shard_map/ppermute | solution.py:24
  209.5 266.9 %copy-start.3 = (f32[8,256,256]{1,2,0:T(8,128)}, f32[8,256,256]{1,2,0:T(8,128)S(1)}, u32[]{:S(2)}) copy-start(f32[8,256,256]{1,2,0:T(8,128)S(1)} %get-tuple-element.92) | copy-start | bytes 6291460
  213.9 27.9 %copy-start.51 = (bf16[256,8,64]{0,2,1:T(8,128)(2,1)S(1)}, bf16[256,8,64]{0,2,1:T(8,128)(2,1)}, u32[]{:S(2)}) copy-start(bf16[256,8,64]{0,2,1:T(8,128)(2,1)} %copy-done.50) | copy-start | bytes 786436
  213.9 27.9 %copy-start.55 = (bf16[256,8,64]{0,2,1:T(8,128)(2,1)S(1)}, bf16[256,8,64]{0,2,1:T(8,128)(2,1)}, u32[]{:S(2)}) copy-start(bf16[256,8,64]{0,2,1:T(8,128)(2,1)} %copy-done.54) | copy-start | bytes 786436
  218.1 45.8 %collective-permute-start.4 = (bf16[256,8,128]{0,2,1:T(8,128)(2,1)}, bf16[256,8,128]{0,2,1:T(8,128)(2,1)}, u32[]{:S(2)}, u32[]{:S(2)}) collective-permute-start(bf16[256,8,128]{0,2,1:T(8,128)(2,1)} %pad_maximum_fusion.1), channel_id=1, source_target_pairs={{0,2},{1,3},{2,4},{3,5},{4,6},{5,7},{6,8},{7,9},{8,10},{9,11},{10,... | collective-permute-start | bytes 1572872 | tf_op jit(solution)/shard_map/ppermute | solution.py:24
  246.7 56.2 %collective-permute-start.7 = (bf16[256,8,128]{0,2,1:T(8,128)(2,1)}, bf16[256,8,128]{0,2,1:T(8,128)(2,1)}, u32[]{:S(2)}, u32[]{:S(2)}) collective-permute-start(bf16[256,8,128]{0,2,1:T(8,128)(2,1)} %pad_maximum_fusion.1), channel_id=1, source_target_pairs={{0,3},{1,4},{2,5},{3,6},{4,7},{5,8},{6,9},{7,10},{8,11},{9,12},{10... | collective-permute-start | bytes 1572872 | tf_op jit(solution)/shard_map/ppermute | solution.py:24
  263.9 48.5 %collective-permute-start.10 = (bf16[256,8,128]{0,2,1:T(8,128)(2,1)}, bf16[256,8,128]{0,2,1:T(8,128)(2,1)}, u32[]{:S(2)}, u32[]{:S(2)}) collective-permute-start(bf16[256,8,128]{0,2,1:T(8,128)(2,1)} %pad_maximum_fusion.1), channel_id=1, source_target_pairs={{0,4},{1,5},{2,6},{3,7},{4,8},{5,9},{6,10},{7,11},{8,12},{9,13},{1... | collective-permute-start | bytes 1572872 | tf_op jit(solution)/shard_map/ppermute | solution.py:24
  302.8 28.4 %collective-permute-start.13 = (bf16[256,8,128]{0,2,1:T(8,128)(2,1)}, bf16[256,8,128]{0,2,1:T(8,128)(2,1)}, u32[]{:S(2)}, u32[]{:S(2)}) collective-permute-start(bf16[256,8,128]{0,2,1:T(8,128)(2,1)} %pad_maximum_fusion.1), channel_id=1, source_target_pairs={{0,5},{1,6},{2,7},{3,8},{4,9},{5,10},{6,11},{7,12},{8,13},{9,14},{... | collective-permute-start | bytes 1572872 | tf_op jit(solution)/shard_map/ppermute | solution.py:24
  312.4 74.3 %collective-permute-start.16 = (bf16[256,8,128]{0,2,1:T(8,128)(2,1)}, bf16[256,8,128]{0,2,1:T(8,128)(2,1)}, u32[]{:S(2)}, u32[]{:S(2)}) collective-permute-start(bf16[256,8,128]{0,2,1:T(8,128)(2,1)} %pad_maximum_fusion.1), channel_id=1, source_target_pairs={{0,6},{1,7},{2,8},{3,9},{4,10},{5,11},{6,12},{7,13},{8,14},{9,15},... | collective-permute-start | bytes 1572872 | tf_op jit(solution)/shard_map/ppermute | solution.py:24
  331.3 62.3 %collective-permute-start.19 = (bf16[256,8,128]{0,2,1:T(8,128)(2,1)}, bf16[256,8,128]{0,2,1:T(8,128)(2,1)}, u32[]{:S(2)}, u32[]{:S(2)}) collective-permute-start(bf16[256,8,128]{0,2,1:T(8,128)(2,1)} %pad_maximum_fusion.1), channel_id=1, source_target_pairs={{0,7},{1,8},{2,9},{3,10},{4,11},{5,12},{6,13},{7,14},{8,15},{16,23... | collective-permute-start | bytes 1572872 | tf_op jit(solution)/shard_map/ppermute | solution.py:24
  386.7 47.0 %collective-permute-start.8 = (bf16[256,8,128]{2,0,1:T(8,128)(2,1)}, bf16[256,8,128]{2,0,1:T(8,128)(2,1)}, u32[]{:S(2)}, u32[]{:S(2)}) collective-permute-start(bf16[256,8,128]{2,0,1:T(8,128)(2,1)} %convolution_convert_fusion.9), channel_id=1, source_target_pairs={{0,3},{1,4},{2,5},{3,6},{4,7},{5,8},{6,9},{7,10},{8,11},{9,12},{10... | collective-permute-start | bytes 1572872 | tf_op jit(solution)/shard_map/ppermute | solution.py:24
  393.5 31.5 %collective-permute-start.5 = (bf16[256,8,128]{2,0,1:T(8,128)(2,1)}, bf16[256,8,128]{2,0,1:T(8,128)(2,1)}, u32[]{:S(2)}, u32[]{:S(2)}) collective-permute-start(bf16[256,8,128]{2,0,1:T(8,128)(2,1)} %convolution_convert_fusion.9), channel_id=1, source_target_pairs={{0,2},{1,3},{2,4},{3,5},{4,6},{5,7},{6,8},{7,9},{8,10},{9,11},{10,... | collective-permute-start | bytes 1572872 | tf_op jit(solution)/shard_map/ppermute | solution.py:24
  425.1 25.7 %collective-permute-start.11 = (bf16[256,8,128]{2,0,1:T(8,128)(2,1)}, bf16[256,8,128]{2,0,1:T(8,128)(2,1)S(1)}, u32[]{:S(2)}, u32[]{:S(2)}) collective-permute-start(bf16[256,8,128]{2,0,1:T(8,128)(2,1)} %convolution_convert_fusion.9), channel_id=1, source_target_pairs={{0,4},{1,5},{2,6},{3,7},{4,8},{5,9},{6,10},{7,11},{8,12},{9,13},{1... | collective-permute-start | bytes 1572872 | tf_op jit(solution)/shard_map/ppermute | solution.py:24
  433.7 22.2 %copy-start.19 = (f32[8,256,256]{1,2,0:T(8,128)S(1)}, f32[8,256,256]{1,2,0:T(8,128)}, u32[]{:S(2)}) copy-start(f32[8,256,256]{1,2,0:T(8,128)} %get-tuple-element.84) | copy-start | bytes 6291460
  433.7 36.3 %collective-permute-start.14 = (bf16[256,8,128]{2,0,1:T(8,128)(2,1)}, bf16[256,8,128]{2,0,1:T(8,128)(2,1)S(1)}, u32[]{:S(2)}, u32[]{:S(2)}) collective-permute-start(bf16[256,8,128]{2,0,1:T(8,128)(2,1)} %convolution_convert_fusion.9), channel_id=1, source_target_pairs={{0,5},{1,6},{2,7},{3,8},{4,9},{5,10},{6,11},{7,12},{8,13},{9,14},{... | collective-permute-start | bytes 1572872 | tf_op jit(solution)/shard_map/ppermute | solution.py:24
  445.0 24.9 %copy-start.23 = (f32[8,256,256]{1,2,0:T(8,128)S(1)}, f32[8,256,256]{1,2,0:T(8,128)}, u32[]{:S(2)}) copy-start(f32[8,256,256]{1,2,0:T(8,128)} %get-tuple-element.82) | copy-start | bytes 6291460
  450.7 27.6 %collective-permute-start.2 = (bf16[256,8,128]{2,0,1:T(8,128)(2,1)}, bf16[256,8,128]{2,0,1:T(8,128)(2,1)S(1)}, u32[]{:S(2)}, u32[]{:S(2)}) collective-permute-start(bf16[256,8,128]{2,0,1:T(8,128)(2,1)} %convolution_convert_fusion.9), channel_id=1, source_target_pairs={{0,1},{1,2},{2,3},{3,4},{4,5},{5,6},{6,7},{7,8},{8,9},{9,10},{10,1... | collective-permute-start | bytes 1572872 | tf_op jit(solution)/shard_map/ppermute | solution.py:24
  483.9 65.4 %copy-start.149 = (f32[256]{0:T(256)}, f32[256]{0:T(256)S(1)}, u32[]{:S(2)}) copy-start(f32[256]{0:T(256)S(1)} %add_rsqrt_fusion) | copy-start | bytes 3076
  491.5 46.8 %copy-start.63 = (bf16[1,256,1024]{2,1,0:T(8,128)(2,1)S(1)}, bf16[1,256,1024]{2,1,0:T(8,128)(2,1)}, u32[]{:S(2)}) copy-start(bf16[1,256,1024]{2,1,0:T(8,128)(2,1)} %param.31) | copy-start | bytes 1572868
  609.7 20.6 %collective-permute-start.24 = (bf16[256,8,128]{0,2,1:T(8,128)(2,1)}, bf16[256,8,128]{0,2,1:T(8,128)(2,1)S(1)}, u32[]{:S(2)}, u32[]{:S(2)}) collective-permute-start(bf16[256,8,128]{0,2,1:T(8,128)(2,1)} %fusion.95), channel_id=1, source_target_pairs={{1,0},{2,1},{3,2},{4,3},{5,4},{6,5},{7,6},{8,7},{9,8},{10,9},{11,1... | collective-permute-start | bytes 1572872 | tf_op jit(solution)/shard_map/ppermute | solution.py:24
  611.3 25.1 %collective-permute-start.25 = (bf16[256,8,128]{0,2,1:T(8,128)(2,1)}, bf16[256,8,128]{0,2,1:T(8,128)(2,1)S(1)}, u32[]{:S(2)}, u32[]{:S(2)}) collective-permute-start(bf16[256,8,128]{0,2,1:T(8,128)(2,1)} %fusion.94), channel_id=1, source_target_pairs={{2,0},{3,1},{4,2},{5,3},{6,4},{7,5},{8,6},{9,7},{10,8},{11,9},{12,... | collective-permute-start | bytes 1572872 | tf_op jit(solution)/shard_map/ppermute | solution.py:24
  612.6 25.4 %collective-permute-start.26 = (bf16[256,8,128]{0,2,1:T(8,128)(2,1)}, bf16[256,8,128]{0,2,1:T(8,128)(2,1)S(1)}, u32[]{:S(2)}, u32[]{:S(2)}) collective-permute-start(bf16[256,8,128]{0,2,1:T(8,128)(2,1)} %fusion.93), channel_id=1, source_target_pairs={{3,0},{4,1},{5,2},{6,3},{7,4},{8,5},{9,6},{10,7},{11,8},{12,9},{13... | collective-permute-start | bytes 1572872 | tf_op jit(solution)/shard_map/ppermute | solution.py:24
  613.9 45.6 %collective-permute-start.27 = (bf16[256,8,128]{0,2,1:T(8,128)(2,1)}, bf16[256,8,128]{0,2,1:T(8,128)(2,1)S(1)}, u32[]{:S(2)}, u32[]{:S(2)}) collective-permute-start(bf16[256,8,128]{0,2,1:T(8,128)(2,1)} %fusion.92), channel_id=1, source_target_pairs={{4,0},{5,1},{6,2},{7,3},{8,4},{9,5},{10,6},{11,7},{12,8},{13,9},{1... | collective-permute-start | bytes 1572872 | tf_op jit(solution)/shard_map/ppermute | solution.py:24
  615.2 46.2 %collective-permute-start.28 = (bf16[256,8,128]{0,2,1:T(8,128)(2,1)}, bf16[256,8,128]{0,2,1:T(8,128)(2,1)S(1)}, u32[]{:S(2)}, u32[]{:S(2)}) collective-permute-start(bf16[256,8,128]{0,2,1:T(8,128)(2,1)} %fusion.91), channel_id=1, source_target_pairs={{5,0},{6,1},{7,2},{8,3},{9,4},{10,5},{11,6},{12,7},{13,8},{14,9},{... | collective-permute-start | bytes 1572872 | tf_op jit(solution)/shard_map/ppermute | solution.py:24
  630.3 34.0 %collective-permute-start.29 = (bf16[256,8,128]{0,2,1:T(8,128)(2,1)S(1)}, bf16[256,8,128]{0,2,1:T(8,128)(2,1)S(1)}, u32[]{:S(2)}, u32[]{:S(2)}) collective-permute-start(bf16[256,8,128]{0,2,1:T(8,128)(2,1)S(1)} %fusion.90), channel_id=1, source_target_pairs={{6,0},{7,1},{8,2},{9,3},{10,4},{11,5},{12,6},{13,7},{14,8},{15,9},... | collective-permute-start | bytes 1572872 | tf_op jit(solution)/shard_map/ppermute | solution.py:24
  636.4 30.1 %collective-permute-start.30 = (bf16[256,8,128]{0,2,1:T(8,128)(2,1)S(1)}, bf16[256,8,128]{0,2,1:T(8,128)(2,1)S(1)}, u32[]{:S(2)}, u32[]{:S(2)}) collective-permute-start(bf16[256,8,128]{0,2,1:T(8,128)(2,1)S(1)} %copy-done.166), channel_id=1, source_target_pairs={{7,0},{8,1},{9,2},{10,3},{11,4},{12,5},{13,6},{14,7},{15,8},{23,16... | collective-permute-start | bytes 1572872 | tf_op jit(solution)/shard_map/ppermute | solution.py:24
  638.0 146.4 %collective-permute-start.31 = (bf16[256,8,128]{0,2,1:T(8,128)(2,1)S(1)}, bf16[256,8,128]{0,2,1:T(8,128)(2,1)S(1)}, u32[]{:S(2)}, u32[]{:S(2)}) collective-permute-start(bf16[256,8,128]{0,2,1:T(8,128)(2,1)S(1)} %copy-done.165), channel_id=1, source_target_pairs={{8,0},{9,1},{10,2},{11,3},{12,4},{13,5},{14,6},{15,7},{24,16},{25,... | collective-permute-start | bytes 1572872 | tf_op jit(solution)/shard_map/ppermute | solution.py:24
  640.6 23.7 %copy-start.163 = (bf16[256,8,128]{0,2,1:T(8,128)(2,1)S(1)}, bf16[256,8,128]{0,2,1:T(8,128)(2,1)}, u32[]{:S(2)}) copy-start(bf16[256,8,128]{0,2,1:T(8,128)(2,1)} %fusion.85) | copy-start | bytes 1572868
  640.7 25.8 %copy-start.162 = (bf16[256,8,128]{0,2,1:T(8,128)(2,1)S(1)}, bf16[256,8,128]{0,2,1:T(8,128)(2,1)}, u32[]{:S(2)}) copy-start(bf16[256,8,128]{0,2,1:T(8,128)(2,1)} %fusion.84) | copy-start | bytes 1572868
  640.7 143.7 %copy-start.161 = (bf16[256,8,128]{0,2,1:T(8,128)(2,1)S(1)}, bf16[256,8,128]{0,2,1:T(8,128)(2,1)}, u32[]{:S(2)}) copy-start(bf16[256,8,128]{0,2,1:T(8,128)(2,1)} %fusion.83) | copy-start | bytes 1572868
  640.7 144.9 %copy-start.46 = (bf16[8,256,256]{1,2,0:T(8,128)(2,1)S(1)}, bf16[8,256,256]{1,2,0:T(8,128)(2,1)}, u32[]{:S(2)}) copy-start(bf16[8,256,256]{1,2,0:T(8,128)(2,1)} %multiply_convert_fusion.11) | copy-start | bytes 3145732
  642.5 144.0 %copy-start.107 = (f32[256,64]{0,1:T(8,128)S(1)}, f32[256,64]{0,1:T(8,128)}, u32[]{:S(2)}) copy-start(f32[256,64]{0,1:T(8,128)} %get-tuple-element.65) | copy-start | bytes 196612
  642.5 144.0 %copy-start.114 = (f32[256,64]{0,1:T(8,128)S(1)}, f32[256,64]{0,1:T(8,128)}, u32[]{:S(2)}) copy-start(f32[256,64]{0,1:T(8,128)} %get-tuple-element.63) | copy-start | bytes 196612
  659.5 136.1 %collective-permute-start.39 = (bf16[256,8,128]{0,2,1:T(8,128)(2,1)S(1)}, bf16[256,8,128]{0,2,1:T(8,128)(2,1)S(1)}, u32[]{:S(2)}, u32[]{:S(2)}) collective-permute-start(bf16[256,8,128]{0,2,1:T(8,128)(2,1)S(1)} %fusion.87), channel_id=1, source_target_pairs={{8,0},{9,1},{10,2},{11,3},{12,4},{13,5},{14,6},{15,7},{24,16},{25,... | collective-permute-start | bytes 1572872 | tf_op jit(solution)/shard_map/ppermute | solution.py:24
  661.4 135.9 %collective-permute-start.38 = (bf16[256,8,128]{0,2,1:T(8,128)(2,1)S(1)}, bf16[256,8,128]{0,2,1:T(8,128)(2,1)S(1)}, u32[]{:S(2)}, u32[]{:S(2)}) collective-permute-start(bf16[256,8,128]{0,2,1:T(8,128)(2,1)S(1)} %copy-done.164), channel_id=1, source_target_pairs={{7,0},{8,1},{9,2},{10,3},{11,4},{12,5},{13,6},{14,7},{15,8},{23,16... | collective-permute-start | bytes 1572872 | tf_op jit(solution)/shard_map/ppermute | solution.py:24
  664.3 134.3 %collective-permute-start.37 = (bf16[256,8,128]{0,2,1:T(8,128)(2,1)S(1)}, bf16[256,8,128]{0,2,1:T(8,128)(2,1)S(1)}, u32[]{:S(2)}, u32[]{:S(2)}) collective-permute-start(bf16[256,8,128]{0,2,1:T(8,128)(2,1)S(1)} %copy-done.163), channel_id=1, source_target_pairs={{6,0},{7,1},{8,2},{9,3},{10,4},{11,5},{12,6},{13,7},{14,8},{15,9},... | collective-permute-start | bytes 1572872 | tf_op jit(solution)/shard_map/ppermute | solution.py:24
  666.4 139.3 %collective-permute-start.36 = (bf16[256,8,128]{0,2,1:T(8,128)(2,1)S(1)}, bf16[256,8,128]{0,2,1:T(8,128)(2,1)S(1)}, u32[]{:S(2)}, u32[]{:S(2)}) collective-permute-start(bf16[256,8,128]{0,2,1:T(8,128)(2,1)S(1)} %copy-done.162), channel_id=1, source_target_pairs={{5,0},{6,1},{7,2},{8,3},{9,4},{10,5},{11,6},{12,7},{13,8},{14,9},{... | collective-permute-start | bytes 1572872 | tf_op jit(solution)/shard_map/ppermute | solution.py:24
  784.3 46.5 %collective-permute-start.35 = (bf16[256,8,128]{0,2,1:T(8,128)(2,1)S(1)}, bf16[256,8,128]{0,2,1:T(8,128)(2,1)S(1)}, u32[]{:S(2)}, u32[]{:S(2)}) collective-permute-start(bf16[256,8,128]{0,2,1:T(8,128)(2,1)S(1)} %copy-done.161), channel_id=1, source_target_pairs={{4,0},{5,1},{6,2},{7,3},{8,4},{9,5},{10,6},{11,7},{12,8},{13,9},{1... | collective-permute-start | bytes 1572872 | tf_op jit(solution)/shard_map/ppermute | solution.py:24
  795.6 35.3 %collective-permute-start.34 = (bf16[256,8,128]{0,2,1:T(8,128)(2,1)S(1)}, bf16[256,8,128]{0,2,1:T(8,128)(2,1)S(1)}, u32[]{:S(2)}, u32[]{:S(2)}) collective-permute-start(bf16[256,8,128]{0,2,1:T(8,128)(2,1)S(1)} %copy-done.160), channel_id=1, source_target_pairs={{3,0},{4,1},{5,2},{6,3},{7,4},{8,5},{9,6},{10,7},{11,8},{12,9},{13... | collective-permute-start | bytes 1572872 | tf_op jit(solution)/shard_map/ppermute | solution.py:24
  797.3 33.6 %collective-permute-start.33 = (bf16[256,8,128]{0,2,1:T(8,128)(2,1)S(1)}, bf16[256,8,128]{0,2,1:T(8,128)(2,1)S(1)}, u32[]{:S(2)}, u32[]{:S(2)}) collective-permute-start(bf16[256,8,128]{0,2,1:T(8,128)(2,1)S(1)} %copy-done.159), channel_id=1, source_target_pairs={{2,0},{3,1},{4,2},{5,3},{6,4},{7,5},{8,6},{9,7},{10,8},{11,9},{12,... | collective-permute-start | bytes 1572872 | tf_op jit(solution)/shard_map/ppermute | solution.py:24
  798.6 32.3 %collective-permute-start.32 = (bf16[256,8,128]{0,2,1:T(8,128)(2,1)S(1)}, bf16[256,8,128]{0,2,1:T(8,128)(2,1)S(1)}, u32[]{:S(2)}, u32[]{:S(2)}) collective-permute-start(bf16[256,8,128]{0,2,1:T(8,128)(2,1)S(1)} %copy-done.158), channel_id=1, source_target_pairs={{1,0},{2,1},{3,2},{4,3},{5,4},{6,5},{7,6},{8,7},{9,8},{10,9},{11,1... | collective-permute-start | bytes 1572872 | tf_op jit(solution)/shard_map/ppermute | solution.py:24
  802.8 28.0 %copy-start.4 = (f32[8,256,256]{1,2,0:T(8,128)S(1)}, f32[8,256,256]{1,2,0:T(8,128)}, u32[]{:S(2)}) copy-start(f32[8,256,256]{1,2,0:T(8,128)} %copy-done.3) | copy-start | bytes 6291460
  849.6 613.7 %reduce-scatter.5.cloned.1.call-start = ((), (), s32[]{:S(2)}) async-start(), calls=%async_computation.10 | async-start | bytes 11894784 | tf_op jit(solution)/shard_map/reduce_scatter | solution.py:307
  (152 other events, 577.8 us)
Sparse Core Ops, SparseCore 0:
  10.8 59.1 all-gather.11
  72.8 55.1 all-gather.9
  130.8 58.7 all-gather.7
  192.3 90.9 all-gather.13
  286.0 77.7 all-gather.17
  366.6 100.2 all-gather.15
  469.8 68.4 all-gather.19
  849.7 450.8 reduce-scatter.2
  1303.5 159.7 reduce-scatter.4
where the time goes:
time: 1480 us; the launch traced here: 1470 us
  waiting for transfers between devices  766 us (52%)
  starting transfers between devices  233 us (16%)
  matrix products  176 us (12%)
  local copies, waits for them, and re-layouts  133 us (9%)
  blocking collectives  118 us (8%)
  other arithmetic  27.3 us (2%)
  between operations  16.5 us (1%)
    reduce_scatter x1, waiting for transfers between devices, local(): lax.psum_scatter(jnp.concatenate([jnp.einsum('td,te->de', normed_one, que...  351 us
    ppermute x40, starting transfers between devices, from_behind(): return lax.ppermute(block, axis, route)  233 us
    ppermute x40, waiting for transfers between devices, from_behind(): return lax.ppermute(block, axis, route)  200 us
    reduce_scatter x1, waiting for transfers between devices, local(): lax.psum_scatter(jnp.einsum('tf,td->fd', hidden, upstream, preferred_elem...  159 us
    unnamed x2, blocking collectives  118 us
    all_gather x1, waiting for transfers between devices, local(): lax.all_gather(down_weight, ('dp', 'seq'), axis=0, tiled=True)  40.9 us
    gather x1, local copies, waits for them, and re-layouts, local(): cache_values[0].reshape(docs, MEM_ROWS, HEADS, HEAD_DIM)  36.1 us
    dot_general x9, matrix products, piece_scores(): jnp.einsum('qhd,khd->hqk', queries, key_piece, preferred_element_type=jnp...  29.8 us
  transfers between devices with their start and end apart: 49, of which 18 were waited for; matrix products, arithmetic and copies ran while one was open for 16% of the time, Pallas kernels for 0%

commit v1 on v0

v1 whole, which is shorter than its diff:
```python
import functools
import math

import jax
import jax.numpy as jnp
from jax import lax
from jax.experimental import pallas as pl
from jax.experimental.pallas import tpu as pltpu
from jax.sharding import Mesh
from jax.sharding import PartitionSpec as P

D = 1024
FF = 2816
HEADS = 8
HEAD_DIM = 128
QUERY_BLOCK = 128
MEM_ROWS = 256
EPSILON = 1e-05
NEGATIVE = -1e30
SCALE = 1.0 / math.sqrt(HEAD_DIM)
LOG2 = SCALE * math.log2(math.e)
LOW = jnp.bfloat16
WIDE = jnp.float32

RING = [2 * i for i in range(HEADS // 2)] + [2 * i + 1 for i in reversed(range(HEADS // 2))]
PLACE = [RING.index(i) for i in range(HEADS)]


def dot_nn(a, b):
    return lax.dot_general(a, b, (((1,), (0,)), ((), ())), preferred_element_type=WIDE)


def dot_nt(a, b):
    return lax.dot_general(a, b, (((1,), (1,)), ((), ())), preferred_element_type=WIDE)


def dot_tn(a, b):
    return lax.dot_general(a, b, (((0,), (0,)), ((), ())), preferred_element_type=WIDE)


def swap(block, axis):
    return lax.ppermute(block, axis, [(0, 1), (1, 0)])


def turn(block, distance):
    route = [(RING[i], RING[(i + distance) % HEADS]) for i in range(HEADS)]
    return lax.ppermute(block, "h", route)


def at_place(place):
    place = lax.rem(place + 2 * HEADS, HEADS)
    return jnp.where(place < HEADS // 2, 2 * place, 2 * (HEADS - 1 - place) + 1)


def rolled(blocks, start):
    return lax.dynamic_slice_in_dim(
        jnp.concatenate([blocks, blocks], axis=0), start, HEADS, axis=0
    )


def reverse(blocks):
    return jnp.concatenate([blocks[:1], jnp.flip(blocks[1:], axis=0)], axis=0)


def to_ahead(blocks, mine):
    return rolled(jnp.stack([blocks[i] for i in RING]), mine)


def from_behind(blocks, mine):
    placed = rolled(reverse(blocks), lax.rem(HEADS - mine, HEADS))
    return jnp.stack([placed[i] for i in PLACE])


def pick(flag, first, second):
    return jnp.where(flag == 0, first, second)


def smem():
    return pl.BlockSpec(memory_space=pltpu.SMEM)


def vmem():
    return pl.BlockSpec(memory_space=pltpu.VMEM)


def qkv_kernel(slot_ref, x_ref, gain_ref, w_ref, cos_ref, sin_ref, *rest):
    q_ref, kv_ref, n_ref = rest[-3:]
    x = x_ref[...].astype(WIDE)
    r = lax.rsqrt(jnp.mean(x * x, axis=-1, keepdims=True) + EPSILON)
    normed = (x * r * gain_ref[...].astype(WIDE)).astype(LOW)
    n_ref[0] = normed
    out = dot_nn(normed, w_ref[...])
    c, s = cos_ref[0], sin_ref[0]

    def rot(v):
        return v * c + pltpu.roll(v, HEAD_DIM // 2, 1) * s

    q_ref[0] = rot(out[:, :HEAD_DIM]).astype(LOW)
    kv_ref[0, 0] = rot(out[:, HEAD_DIM : 2 * HEAD_DIM]).astype(LOW)
    kv_ref[1, 0] = out[:, 2 * HEAD_DIM :].astype(LOW)


def qkv_block(slot, x, gain, w, cos, sin, held):
    count = x.shape[0]
    spec = pltpu.PrefetchScalarGridSpec(
        num_scalar_prefetch=1,
        grid=(1,),
        in_specs=[
            pl.BlockSpec((count, D), lambda i, s: (0, 0)),
            pl.BlockSpec((1, D), lambda i, s: (0, 0)),
            pl.BlockSpec((D, 3 * HEAD_DIM), lambda i, s: (0, 0)),
            pl.BlockSpec((1, count, HEAD_DIM), lambda i, s: (slot, 0, 0)),
            pl.BlockSpec((1, count, HEAD_DIM), lambda i, s: (slot, 0, 0)),
        ]
        + [pl.BlockSpec(memory_space=pl.ANY)] * len(held),
        out_specs=[
            pl.BlockSpec((1, count, HEAD_DIM), lambda i, s: (slot, 0, 0)),
            pl.BlockSpec((2, 1, count, HEAD_DIM), lambda i, s: (0, slot, 0, 0)),
            pl.BlockSpec((1, count, D), lambda i, s: (slot, 0, 0)),
        ],
    )
    return pl.pallas_call(
        qkv_kernel,
        grid_spec=spec,
        out_shape=[
            jax.ShapeDtypeStruct((HEADS, count, HEAD_DIM), LOW),
            jax.ShapeDtypeStruct((2, HEADS, count, HEAD_DIM), LOW),
            jax.ShapeDtypeStruct((HEADS, count, D), LOW),
        ],
        input_output_aliases={6 + i: i for i in range(len(held))},
        cost_estimate=pl.CostEstimate(
            flops=2 * count * D * 3 * HEAD_DIM, bytes_accessed=4 * count * D, transcendentals=0
        ),
        name=f"qkv{slot}",
    )(jnp.zeros((1,), jnp.int32), x, gain, w, cos, sin, *held)


def allowed_keys(segq, segk, qpos, kstart, shape):
    kpos = kstart + lax.broadcasted_iota(jnp.int32, shape, 1)
    return (segk == segq) & (kpos <= qpos)


def attend_kernel(
    tab, q_ref, own_ref, oth_ref, segq_ref, sego_ref, segt_ref, idx_ref, ck_ref, cv_ref,
    o_ref, low_ref, lse_ref, mem_ref,
):
    i = pl.program_id(0)
    chip = tab[i]
    parity = tab[48]
    count = q_ref.shape[1]
    for b in range(count // QUERY_BLOCK):
        rows = pl.ds(b * QUERY_BLOCK, QUERY_BLOCK)
        q = q_ref[0, rows, :]
        segq = segq_ref[0, rows, :]
        doc = tab[16 + 2 * i + b]
        mate = tab[32 + 2 * i + b]
        idx = idx_ref[0, rows, :]
        lane = lax.broadcasted_iota(jnp.int32, (QUERY_BLOCK, MEM_ROWS), 1)
        first = jnp.where(idx == lane, 1.0, 0.0).astype(LOW)
        second = jnp.where(idx == lane + MEM_ROWS, 1.0, 0.0).astype(LOW)
        here = pl.ds(pl.multiple_of(doc * MEM_ROWS, MEM_ROWS), MEM_ROWS)
        there = pl.ds(pl.multiple_of(mate * MEM_ROWS, MEM_ROWS), MEM_ROWS)
        mk = (dot_nn(first, ck_ref[here, :]) + dot_nn(second, ck_ref[there, :])).astype(LOW)
        mv = (dot_nn(first, cv_ref[here, :]) + dot_nn(second, cv_ref[there, :])).astype(LOW)
        mem_ref[0, 0, rows, :] = mk
        mem_ref[1, 0, rows, :] = mv
        s = dot_nt(q, mk) * LOG2
        mask = segq == doc
        top = jnp.where(mask, jnp.max(s, axis=-1, keepdims=True), NEGATIVE)
        p = jnp.where(mask, jnp.exp2(s - top), 0.0)
        total = jnp.sum(p, axis=-1, keepdims=True)
        acc = dot_nn(p.astype(LOW), mv)
        shape = (QUERY_BLOCK, count)
        qpos = (2 * chip + parity) * count + b * QUERY_BLOCK + lax.broadcasted_iota(
            jnp.int32, shape, 0
        )

        def body(j, state):
            top, total, acc = state
            slot = tab[8 + j]
            s1 = dot_nt(q, own_ref[0, slot]) * LOG2
            s2 = dot_nt(q, oth_ref[0, slot]) * LOG2
            ok1 = allowed_keys(segq, sego_ref[j], qpos, (2 * j + parity) * count, shape)
            ok2 = allowed_keys(segq, segt_ref[j], qpos, (2 * j + 1 - parity) * count, shape)
            s1 = jnp.where(ok1, s1, NEGATIVE)
            s2 = jnp.where(ok2, s2, NEGATIVE)
            fresh = jnp.maximum(
                top, jnp.max(jnp.maximum(s1, s2), axis=-1, keepdims=True)
            )
            p1 = jnp.where(ok1, jnp.exp2(s1 - fresh), 0.0)
            p2 = jnp.where(ok2, jnp.exp2(s2 - fresh), 0.0)
            decay = jnp.exp2(top - fresh)
            total = total * decay + jnp.sum(p1 + p2, axis=-1, keepdims=True)
            acc = (
                acc * decay
                + dot_nn(p1.astype(LOW), own_ref[1, slot])
                + dot_nn(p2.astype(LOW), oth_ref[1, slot])
            )
            return fresh, total, acc

        top, total, acc = lax.fori_loop(tab[64 + i], chip + 1, body, (top, total, acc))
        out = acc / total
        o_ref[0, rows, :] = out
        low_ref[0, rows, :] = out.astype(LOW)
        lse_ref[0, rows, :] = top + jnp.log2(total)


def attend(tab, q, own, oth, segq, sego, segt, idx, ck, cv):
    count = q.shape[1]
    block = pl.BlockSpec((1, count, HEAD_DIM), lambda i, t: (i, 0, 0))
    thin = pl.BlockSpec((1, count, 1), lambda i, t: (i, 0, 0))
    whole = pl.BlockSpec((2, HEADS, count, HEAD_DIM), lambda i, t: (0, 0, 0, 0))
    segs = pl.BlockSpec((HEADS, 1, count), lambda i, t: (0, 0, 0))
    cache = pl.BlockSpec((ck.shape[0], HEAD_DIM), lambda i, t: (0, t[49]))
    mem = pl.BlockSpec((2, 1, count, HEAD_DIM), lambda i, t: (0, i, 0, 0))
    return pl.pallas_call(
        attend_kernel,
        grid_spec=pltpu.PrefetchScalarGridSpec(
            num_scalar_prefetch=1,
            grid=(HEADS,),
            in_specs=[block, whole, whole, thin, segs, segs, thin, cache, cache],
            out_specs=[block, block, thin, mem],
        ),
        out_shape=[
            jax.ShapeDtypeStruct((HEADS, count, HEAD_DIM), WIDE),
            jax.ShapeDtypeStruct((HEADS, count, HEAD_DIM), LOW),
            jax.ShapeDtypeStruct((HEADS, count, 1), WIDE),
            jax.ShapeDtypeStruct((2, HEADS, count, HEAD_DIM), LOW),
        ],
        cost_estimate=pl.CostEstimate(
            flops=4 * 10**9, bytes_accessed=6 * 2**20, transcendentals=3 * 10**6
        ),
        name="attend",
    )(tab, q, own, oth, segq, sego, segt, idx, ck, cv)


def attend_back_kernel(
    tab, q_ref, up_ref, o_ref, lse_ref, own_ref, oth_ref, mem_ref, segq_ref, sego_ref, segt_ref,
    dq_ref, down_ref, doth_ref, sum_ref,
):
    i = pl.program_id(0)

    @pl.when(i == 0)
    def _():
        sum_ref[...] = jnp.zeros_like(sum_ref)

    chip = tab[i]
    parity = tab[48]
    count = q_ref.shape[1]
    for b in range(count // QUERY_BLOCK):
        rows = pl.ds(b * QUERY_BLOCK, QUERY_BLOCK)
        q = q_ref[0, rows, :]
        up = up_ref[0, rows, :]
        lse = lse_ref[0, rows, :]
        segq = segq_ref[0, rows, :]
        delta = jnp.sum(up.astype(WIDE) * o_ref[0, rows, :], axis=-1, keepdims=True)
        doc = tab[16 + 2 * i + b]
        mk = mem_ref[0, 0, rows, :]
        mv = mem_ref[1, 0, rows, :]
        p = jnp.where(segq == doc, jnp.exp2(dot_nt(q, mk) * LOG2 - lse), 0.0)
        ds = (p * (dot_nt(up, mv) - delta)).astype(LOW)
        dq = dot_nn(ds, mk)
        shape = (QUERY_BLOCK, count)
        qpos = (2 * chip + parity) * count + b * QUERY_BLOCK + lax.broadcasted_iota(
            jnp.int32, shape, 0
        )

        def body(j, dq):
            slot = tab[8 + j]
            for side, ref, seg_ref, start in (
                (0, own_ref, sego_ref, (2 * j + parity) * count),
                (1, oth_ref, segt_ref, (2 * j + 1 - parity) * count),
            ):
                k = ref[0, slot]
                v = ref[1, slot]
                ok = allowed_keys(segq, seg_ref[j], qpos, start, shape)
                p = jnp.where(ok, jnp.exp2(dot_nt(q, k) * LOG2 - lse), 0.0)
                ds = (p * (dot_nt(up, v) - delta)).astype(LOW)
                sum_ref[side, 0, slot] += dot_tn(ds, q)
                sum_ref[side, 1, slot] += dot_tn(p.astype(LOW), up)
                dq = dq + dot_nn(ds, k)
            return dq

        dq_ref[0, rows, :] = lax.fori_loop(tab[64 + i], chip + 1, body, dq)

    @pl.when(i == HEADS - 1)
    def _():
        down_ref[...] = sum_ref[0]
        doth_ref[...] = sum_ref[1].astype(LOW)


def attend_back(tab, q, up, o, lse, own, oth, mem, segq, sego, segt):
    count = q.shape[1]
    block = pl.BlockSpec((1, count, HEAD_DIM), lambda i, t: (i, 0, 0))
    thin = pl.BlockSpec((1, count, 1), lambda i, t: (i, 0, 0))
    whole = pl.BlockSpec((2, HEADS, count, HEAD_DIM), lambda i, t: (0, 0, 0, 0))
    segs = pl.BlockSpec((HEADS, 1, count), lambda i, t: (0, 0, 0))
    memory = pl.BlockSpec((2, 1, count, HEAD_DIM), lambda i, t: (0, i, 0, 0))
    return pl.pallas_call(
        attend_back_kernel,
        grid_spec=pltpu.PrefetchScalarGridSpec(
            num_scalar_prefetch=1,
            grid=(HEADS,),
            in_specs=[block, block, block, thin, whole, whole, memory, thin, segs, segs],
            out_specs=[block, whole, whole],
            scratch_shapes=[pltpu.VMEM((2, 2, HEADS, count, HEAD_DIM), WIDE)],
        ),
        out_shape=[
            jax.ShapeDtypeStruct((HEADS, count, HEAD_DIM), WIDE),
            jax.ShapeDtypeStruct((2, HEADS, count, HEAD_DIM), WIDE),
            jax.ShapeDtypeStruct((2, HEADS, count, HEAD_DIM), LOW),
        ],
        cost_estimate=pl.CostEstimate(
            flops=10 * 10**9, bytes_accessed=10 * 2**20, transcendentals=3 * 10**6
        ),
        name="attend_back",
    )(tab, q, up, o, lse, own, oth, mem, segq, sego, segt)


def out_kernel(tab, heads_ref, w_ref, x_ref, gain_ref, att_ref, mid_ref, n_ref):
    for h in range(HEADS):
        att_ref[:, h * HEAD_DIM : (h + 1) * HEAD_DIM] = heads_ref[tab[h]]
    mid = x_ref[...].astype(WIDE) + dot_nn(att_ref[...], w_ref[...])
    mid_ref[...] = mid
    r = lax.rsqrt(jnp.mean(mid * mid, axis=-1, keepdims=True) + EPSILON)
    n_ref[...] = (mid * r * gain_ref[...].astype(WIDE)).astype(LOW)


def out_block(tab, heads, w, x, gain):
    count = x.shape[0]
    return pl.pallas_call(
        out_kernel,
        in_specs=[smem()] + [vmem()] * 4,
        out_specs=[vmem()] * 3,
        out_shape=[
            jax.ShapeDtypeStruct((count, D), LOW),
            jax.ShapeDtypeStruct((count, D), WIDE),
            jax.ShapeDtypeStruct((count, D), LOW),
        ],
        cost_estimate=pl.CostEstimate(
            flops=2 * count * D * D, bytes_accessed=4 * 2**20, transcendentals=0
        ),
        name="out_block",
    )(tab, heads, w, x, gain)


def ffn_kernel(na, nb, ga, gb, g_ref, u_ref, d_ref, hid_ref, gg_ref, ug_ref, dn_ref):
    for t, (n_ref, c_ref) in enumerate(((na, ga), (nb, gb))):
        n = n_ref[...]
        gate = dot_nn(n, g_ref[...])
        upper = dot_nn(n, u_ref[...])
        sigma = jax.nn.sigmoid(gate)
        silu = gate * sigma
        hid_ref[t] = (silu * upper).astype(LOW)
        hg = dot_nt(c_ref[...], d_ref[...])
        gg = (hg * upper * sigma * (1.0 + gate * (1.0 - sigma))).astype(LOW)
        ug = (hg * silu).astype(LOW)
        gg_ref[t] = gg
        ug_ref[t] = ug
        dn_ref[t] = (dot_nt(gg, g_ref[...]) + dot_nt(ug, u_ref[...])).astype(LOW)


def ffn(na, nb, ga, gb, g, u, d):
    count = na.shape[0]
    units = g.shape[1]
    return pl.pallas_call(
        ffn_kernel,
        in_specs=[vmem()] * 7,
        out_specs=[vmem()] * 4,
        out_shape=[jax.ShapeDtypeStruct((2, count, units), LOW)] * 3
        + [jax.ShapeDtypeStruct((2, count, D), LOW)],
        cost_estimate=pl.CostEstimate(
            flops=20 * count * D * units,
            bytes_accessed=6 * D * units + 16 * count * D,
            transcendentals=2 * count * units,
        ),
        name="ffn",
    )(na, nb, ga, gb, g, u, d)


def mid_kernel(tab, mid_ref, pa, pb, pc, up_ref, gain_ref, w_ref, mg_ref, bg_ref, ag_ref):
    mid = mid_ref[...]
    scaled = (pa[...].astype(WIDE) + pb[...].astype(WIDE) + pc[...].astype(WIDE)) * gain_ref[
        ...
    ].astype(WIDE)
    r = lax.rsqrt(jnp.mean(mid * mid, axis=-1, keepdims=True) + EPSILON)
    inner = jnp.mean(scaled * mid, axis=-1, keepdims=True)
    mid_grad = up_ref[...].astype(WIDE) + r * scaled - mid * (r * r * r * inner)
    mg_ref[...] = mid_grad
    branch = mid_grad.astype(LOW)
    bg_ref[...] = branch
    att = dot_nt(branch, w_ref[...]).astype(LOW)
    for h in range(HEADS):
        ag_ref[tab[h]] = att[:, h * HEAD_DIM : (h + 1) * HEAD_DIM]


def mid_block(tab, mid, pa, pb, pc, up, gain, w):
    count = mid.shape[0]
    return pl.pallas_call(
        mid_kernel,
        in_specs=[smem()] + [vmem()] * 7,
        out_specs=[vmem()] * 3,
        out_shape=[
            jax.ShapeDtypeStruct((count, D), WIDE),
            jax.ShapeDtypeStruct((count, D), LOW),
            jax.ShapeDtypeStruct((HEADS, count, HEAD_DIM), LOW),
        ],
        cost_estimate=pl.CostEstimate(
            flops=2 * count * D * D, bytes_accessed=6 * 2**20, transcendentals=0
        ),
        name="mid_block",
    )(tab, mid, pa, pb, pc, up, gain, w)


def qkv_back_kernel(dq_ref, own_ref, got_ref, cos_ref, sin_ref, n_ref, w_ref, dx_ref, dw_ref, sum_ref):
    i = pl.program_id(0)

    @pl.when(i == 0)
    def _():
        sum_ref[...] = jnp.zeros_like(sum_ref)

    c, s = cos_ref[0], sin_ref[0]

    def rot(v):
        return v * c - pltpu.roll(v, HEAD_DIM // 2, 1) * s

    dq = rot(dq_ref[0] * SCALE).astype(LOW)
    dk = rot((own_ref[0, 0] + got_ref[0, 0].astype(WIDE)) * SCALE).astype(LOW)
    dv = (own_ref[1, 0] + got_ref[1, 0].astype(WIDE)).astype(LOW)
    grads = jnp.concatenate([dq, dk, dv], axis=1)
    dx_ref[0] = dot_nt(grads, w_ref[...]).astype(LOW)
    sum_ref[...] += dot_tn(n_ref[0], grads)

    @pl.when(i == HEADS - 1)
    def _():
        dw_ref[...] = sum_ref[...].astype(LOW)


def qkv_back(dq, own, got, cos, sin, normed, w):
    count = dq.shape[1]
    block = pl.BlockSpec((1, count, HEAD_DIM), lambda i: (i, 0, 0))
    pair = pl.BlockSpec((2, 1, count, HEAD_DIM), lambda i: (0, i, 0, 0))
    wide = pl.BlockSpec((1, count, D), lambda i: (i, 0, 0))
    weight = pl.BlockSpec((D, 3 * HEAD_DIM), lambda i: (0, 0))
    return pl.pallas_call(
        qkv_back_kernel,
        grid=(HEADS,),
        in_specs=[block, pair, pair, block, block, wide, weight],
        out_specs=[wide, weight],
        scratch_shapes=[pltpu.VMEM((D, 3 * HEAD_DIM), WIDE)],
        out_shape=[
            jax.ShapeDtypeStruct((HEADS, count, D), LOW),
            jax.ShapeDtypeStruct((D, 3 * HEAD_DIM), LOW),
        ],
        cost_estimate=pl.CostEstimate(
            flops=4 * HEADS * count * D * 3 * HEAD_DIM,
            bytes_accessed=4 * HEADS * count * D,
            transcendentals=0,
        ),
        name="qkv_back",
    )(dq, own, got, cos, sin, normed, w)


def local(
    far,
    tokens,
    segment_ids,
    second_doc,
    memory_index,
    cache_keys,
    cache_values,
    first_gain,
    query_weight,
    key_weight,
    value_weight,
    out_weight,
    second_gain,
    gate_weight,
    up_weight,
    down_weight,
    cotangent,
):
    x = tokens[0]
    upstream = cotangent[0]
    count = x.shape[0]
    blocks = count // QUERY_BLOCK
    rows = query_weight.shape[0]
    share = down_weight.shape[0]
    units = far * HEADS * share
    chip, core, pair = lax.axis_index("h"), lax.axis_index("c"), lax.axis_index("dl")
    mine = jnp.where(chip % 2 == 0, chip // 2, HEADS - 1 - chip // 2)
    slots = jnp.arange(HEADS, dtype=jnp.int32)
    chips = at_place(mine - slots)
    group = ("dh", "h") if far > 1 else "h"

    forth, back = [x], [x]
    for step in range(HEADS // 2):
        forth.append(turn(forth[-1], 1))
        if step < HEADS // 2 - 1:
            back.append(turn(back[-1], -1))
    x_slots = forth + back[:0:-1]

    def by_head(w):
        return w.reshape(rows, HEADS, HEAD_DIM).transpose(1, 0, 2)

    picked = memory_index[0].transpose(1, 0, 2)
    seg_rows = jnp.broadcast_to(
        segment_ids[0].astype(LOW).reshape(1, blocks, QUERY_BLOCK), (HEADS, blocks, QUERY_BLOCK)
    )
    gains = jnp.concatenate([first_gain, second_gain])
    gain_rows = jnp.broadcast_to(
        jnp.pad(gains, (0, HEAD_DIM - 2 * rows)).reshape(1, 1, HEAD_DIM), (HEADS, 1, HEAD_DIM)
    )
    pack = jnp.concatenate(
        [
            by_head(query_weight),
            by_head(key_weight),
            by_head(value_weight),
            seg_rows,
            (picked // MEM_ROWS).astype(LOW),
            (picked % MEM_ROWS).astype(LOW),
            gain_rows,
        ],
        axis=1,
    )
    height = pack.shape[1]
    pack = jnp.pad(pack, ((0, 0), (0, -height % 16), (0, 0)))
    pack = to_ahead(pack, mine)
    got = jnp.stack([pack[0]] + [turn(pack[d], d) for d in range(1, HEADS)])
    got_c = swap(got, "c")
    got_y = swap(got, "dl")
    got_yc = swap(got_y, "c")
    near = pick(core, jnp.stack([got, got_c]), jnp.stack([got_c, got]))
    away = pick(core, jnp.stack([got_y, got_yc]), jnp.stack([got_yc, got_y]))
    every = pick(pair, jnp.stack([near, away]), jnp.stack([away, near]))
    every = every.transpose(2, 0, 1, 3, 4)
    every = from_behind(every, mine)
    if far > 1:
        every = lax.all_gather(every, "dh", axis=0)
    else:
        every = every[None]
    every = every.transpose(0, 2, 1, 3, 4, 5)
    w_qkv = jnp.concatenate(
        [every[..., i * rows : (i + 1) * rows, :].reshape(D, HEAD_DIM) for i in range(3)], axis=1
    )
    gain_all = every[..., 3 * rows + 3 * blocks, : 2 * rows].reshape(-1, 2, rows)
    gain_one = gain_all[:, 0].reshape(1, D)
    gain_two = gain_all[:, 1].reshape(1, D)

    def seg_of(blocks_of):
        return (
            blocks_of[:, 3 * rows : 3 * rows + blocks]
            .astype(WIDE)
            .astype(jnp.int32)
            .reshape(HEADS, count)
        )

    seg_own_slots = seg_of(got)
    seg_own = from_behind(seg_own_slots, mine)
    seg_oth = from_behind(seg_of(got_c), mine)
    seg_all = pick(core, jnp.stack([seg_own, seg_oth], 1), jnp.stack([seg_oth, seg_own], 1))
    idx = (
        got[:, 3 * rows + blocks : 3 * rows + 2 * blocks].astype(WIDE) * MEM_ROWS
        + got[:, 3 * rows + 2 * blocks : 3 * rows + 3 * blocks].astype(WIDE)
    ).astype(jnp.int32)
    idx = idx.reshape(HEADS, count, 1)

    block_docs = seg_own_slots[:, ::QUERY_BLOCK]
    docs = second_doc.shape[1]
    doc_ids = jnp.arange(docs, dtype=jnp.int32)
    mates = jnp.sum(
        jnp.where(block_docs[:, :, None] == doc_ids, second_doc[0][None, None, :], 0), axis=-1
    )
    before = jnp.sum(
        (seg_all.reshape(1, -1) < block_docs[:, :1]).astype(jnp.int32), axis=1
    )
    places = jnp.asarray(PLACE, jnp.int32)
    tab = jnp.concatenate(
        [
            chips,
            lax.rem(mine - places + HEADS, HEADS),
            block_docs.reshape(-1),
            mates.reshape(-1),
            jnp.stack([core, chip]),
            jnp.zeros((14,), jnp.int32),
            before // (2 * count),
        ]
    ).astype(jnp.int32)
    ahead_of = lax.rem(places - mine + HEADS, HEADS).astype(jnp.int32)

    half = HEAD_DIM // 2
    freqs = 10000.0 ** (-jnp.arange(half, dtype=WIDE) * 2.0 / (2 * half))
    positions = ((2 * chips + core) * count)[:, None] + jnp.arange(count, dtype=jnp.int32)[None]
    turned = positions.astype(WIDE)[:, :, None] * freqs
    cosine, sine = jnp.cos(turned), jnp.sin(turned)
    cosine = jnp.concatenate([cosine, cosine], axis=-1)
    sine = jnp.concatenate([-sine, sine], axis=-1)

    def by_owner(w):
        return w.reshape(rows, far, 2, HEADS, 2, share).transpose(2, 4, 0, 1, 3, 5).reshape(
            2, 2, rows, units
        )

    gu = jnp.concatenate([by_owner(gate_weight), by_owner(up_weight)], axis=-1)
    kept = pick(core, gu[:, 0], gu[:, 1])
    came = swap(pick(core, gu[:, 1], gu[:, 0]), "c")
    gu = pick(core, jnp.stack([kept, came], 1), jnp.stack([came, kept], 1))
    kept = pick(pair, gu[0], gu[1])
    came = swap(pick(pair, gu[1], gu[0]), "dl")
    gu = pick(pair, jnp.stack([kept, came]), jnp.stack([came, kept])).reshape(4 * rows, 2 * units)
    wide = 2 * units
    third = wide - D
    pieces = [out_weight[:, i * third : (i + 1) * third] for i in range(-(-D // third))]
    pieces[-1] = jnp.pad(pieces[-1], ((0, 0), (0, third - pieces[-1].shape[1])))
    pieces = jnp.concatenate(pieces, axis=0)
    deep = max(share, pieces.shape[0])
    lower = jnp.concatenate(
        [
            jnp.pad(down_weight, ((0, deep - share), (0, 0))),
            jnp.pad(pieces, ((0, deep - pieces.shape[0]), (0, 0))),
        ],
        axis=1,
    )
    gathered = lax.all_gather(jnp.concatenate([gu, lower], axis=0), group, axis=0)
    gathered = gathered.reshape(far, HEADS, 4 * rows + deep, wide)
    gu_w = (
        gathered[:, :, : 4 * rows]
        .reshape(far, HEADS, 2, 2 * rows, wide)
        .transpose(0, 2, 1, 3, 4)
        .reshape(D, wide)
    )
    gate_w, up_w = gu_w[:, :units], gu_w[:, units:]
    down_w = gathered[:, :, 4 * rows : 4 * rows + share, :D].reshape(units, D)
    outs = gathered[:, :, 4 * rows :, D:]
    outs = jnp.concatenate(
        [outs[:, :, i * rows : (i + 1) * rows] for i in range(pieces.shape[0] // rows)], axis=-1
    )[..., :D]
    outs_c = swap(outs, "c")
    outs_y = swap(outs, "dl")
    outs_yc = swap(outs_y, "c")
    near = pick(core, jnp.stack([outs, outs_c], 2), jnp.stack([outs_c, outs], 2))
    away = pick(core, jnp.stack([outs_y, outs_yc], 2), jnp.stack([outs_yc, outs_y], 2))
    out_w = pick(pair, jnp.stack([near, away], 1), jnp.stack([away, near], 1)).reshape(D, D)

    up_c = swap(upstream, "c")
    up_y = swap(upstream, "dl")
    up_yc = swap(up_y, "c")

    order = [0]
    for step in range(1, HEADS // 2 + 1):
        order += [step] if step == HEADS // 2 else [step, HEADS - step]
    held = ()
    for slot in order:
        held = qkv_block(slot, x_slots[slot], gain_one, w_qkv, cosine, sine, held)
    queries, own, normed_one = held
    other = swap(own, "c")

    seg_thin = seg_own_slots.reshape(HEADS, count, 1)
    seg_own_row = seg_own.reshape(HEADS, 1, count)
    seg_oth_row = seg_oth.reshape(HEADS, 1, count)
    attention, attention_low, lse, memory = attend(
        tab,
        queries,
        own,
        other,
        seg_thin,
        seg_own_row,
        seg_oth_row,
        idx,
        cache_keys[0].reshape(-1, D),
        cache_values[0].reshape(-1, D),
    )

    heads = jnp.stack(
        [attention_low[0]] + [turn(attention_low[d], -d) for d in range(1, HEADS)]
    )
    attended, mid, normed_two = out_block(ahead_of, heads, out_w, x, gain_two)

    n_c = swap(normed_two, "c")
    n_y = swap(normed_two, "dl")
    n_yc = swap(n_y, "c")
    hid_l, gg_l, ug_l, dn_l = ffn(normed_two, n_c, upstream, up_c, gate_w, up_w, down_w)
    hid_r, gg_r, ug_r, dn_r = ffn(n_y, n_yc, up_y, up_yc, gate_w, up_w, down_w)

    def sum_back(near, away):
        there = (away[0].astype(WIDE) + swap(away[1], "c").astype(WIDE)).astype(LOW)
        return near[0], swap(near[1], "c"), swap(there, "dl")

    parts = sum_back(dn_l, dn_r)
    mid_grad, branch, att_grad = mid_block(
        ahead_of, mid, *parts, upstream, gain_two, out_w
    )

    def over_tokens(a, b):
        return jnp.einsum("gtd,gtf->df", a, b, preferred_element_type=WIDE)

    n_l, n_r = jnp.stack([normed_two, n_c]), jnp.stack([n_y, n_yc])
    u_l, u_r = jnp.stack([upstream, up_c]), jnp.stack([up_y, up_yc])
    gate_part = (over_tokens(n_l, gg_l) + over_tokens(n_r, gg_r)).astype(LOW)
    up_part = (over_tokens(n_l, ug_l) + over_tokens(n_r, ug_r)).astype(LOW)
    down_part = (over_tokens(hid_l, u_l) + over_tokens(hid_r, u_r)).astype(LOW)

    def by_rows(w):
        return (
            w.reshape(far, 2, HEADS, 2 * rows, units)
            .transpose(0, 2, 1, 3, 4)
            .reshape(far * HEADS, 4 * rows, units)
        )

    height = 4 * rows + share
    height += -height % 16
    parts = jnp.concatenate(
        [
            jnp.concatenate([by_rows(gate_part), by_rows(up_part)], axis=-1),
            jnp.pad(
                down_part.reshape(far * HEADS, share, D),
                ((0, 0), (0, height - 4 * rows - share), (0, wide - D)),
            ),
        ],
        axis=1,
    )
    summed = lax.psum_scatter(
        parts.reshape(far * HEADS * height, wide), group, scatter_dimension=0, tiled=True
    )
    down_w_grad = summed[4 * rows : 4 * rows + share, :D].astype(WIDE)
    gu = summed[: 4 * rows].reshape(2, 2, rows, wide)
    kept = pick(core, gu[:, 0], gu[:, 1])
    came = swap(pick(core, gu[:, 1], gu[:, 0]), "c")
    gu = pick(core, jnp.stack([kept, came], 1), jnp.stack([came, kept], 1))
    kept = pick(pair, gu[0], gu[1])
    came = swap(pick(pair, gu[1], gu[0]), "dl")
    gu = pick(pair, jnp.stack([kept, came]), jnp.stack([came, kept]))
    gu = (
        gu.reshape(2, 2, rows, 2, far, HEADS, share)
        .transpose(3, 2, 4, 0, 5, 1, 6)
        .reshape(2, rows, FF)
        .astype(WIDE)
    )
    gate_w_grad, up_w_grad = gu[0], gu[1]

    out_l = jnp.einsum("gtf,fd->gtd", hid_l, down_w, preferred_element_type=WIDE).astype(LOW)
    out_r = jnp.einsum("gtf,fd->gtd", hid_r, down_w, preferred_element_type=WIDE).astype(LOW)
    output = mid
    for part in sum_back(out_l, out_r):
        output = output + part.astype(WIDE)
    output = output.astype(LOW)

    def to_owners(w, width):
        w = w.reshape(far, 2, HEADS, 2, rows, width)
        kept = pick(core, w[:, :, :, 0], w[:, :, :, 1])
        came = swap(pick(core, w[:, :, :, 1], w[:, :, :, 0]), "c")
        w = kept.astype(WIDE) + came.astype(WIDE)
        kept = pick(pair, w[:, 0], w[:, 1])
        came = swap(pick(pair, w[:, 1], w[:, 0]).astype(LOW), "dl")
        w = (kept + came.astype(WIDE)).astype(LOW)
        if far > 1:
            w = lax.psum_scatter(w, "dh", scatter_dimension=0, tiled=True)
        w = to_ahead(w[0], mine)
        return [w[0]] + [turn(w[d], d) for d in range(1, HEADS)]

    out_part = jnp.einsum("td,te->de", attended, branch, preferred_element_type=WIDE).astype(LOW)
    out_w_grad = functools.reduce(
        lambda a, b: a + b, [w.astype(WIDE) for w in to_owners(out_part, D)]
    )

    ups = jnp.stack([att_grad[0]] + [turn(att_grad[d], d) for d in range(1, HEADS)])
    dq, d_own, d_oth = attend_back(
        tab, queries, ups, attention, lse, own, other, memory, seg_thin, seg_own_row, seg_oth_row
    )
    d_got = swap(d_oth, "c")
    dx, dw = qkv_back(dq, d_own, d_got, cosine, sine, normed_one, w_qkv)

    forth = dx[HEADS // 2]
    for slot in range(HEADS // 2 + 1, HEADS):
        forth = (turn(forth, 1).astype(WIDE) + dx[slot].astype(WIDE)).astype(LOW)
    forth = turn(forth, 1)
    back = dx[HEADS // 2 - 1]
    for slot in range(HEADS // 2 - 2, 0, -1):
        back = (turn(back, -1).astype(WIDE) + dx[slot].astype(WIDE)).astype(LOW)
    back = turn(back, -1)
    normed_one_grad = dx[0].astype(WIDE) + forth.astype(WIDE) + back.astype(WIDE)

    wide_x = x.astype(WIDE)
    r = lax.rsqrt(jnp.mean(wide_x * wide_x, axis=-1, keepdims=True) + EPSILON)
    scaled = normed_one_grad * gain_one.astype(WIDE)
    inner = jnp.mean(scaled * wide_x, axis=-1, keepdims=True)
    input_grad = mid_grad + r * scaled - wide_x * (r * r * r * inner)

    qkv_grads = from_behind(jnp.stack(to_owners(dw, 3 * HEAD_DIM)), mine).astype(WIDE)
    q_w_grad, k_w_grad, v_w_grad = (
        qkv_grads[:, :, i * HEAD_DIM : (i + 1) * HEAD_DIM].transpose(1, 0, 2).reshape(rows, D)
        for i in range(3)
    )

    def gain_grad(gain, pairs):
        total = 0.0
        for grad, weight in pairs:
            total = total + jnp.sum(grad * weight.astype(WIDE), axis=1)
        return total / gain.astype(WIDE)

    first_gain_grad = gain_grad(
        first_gain,
        ((q_w_grad, query_weight), (k_w_grad, key_weight), (v_w_grad, value_weight)),
    )
    second_gain_grad = gain_grad(
        second_gain, ((gate_w_grad, gate_weight), (up_w_grad, up_weight))
    )
    return (
        output[None],
        input_grad[None],
        first_gain_grad,
        q_w_grad,
        k_w_grad,
        v_w_grad,
        out_w_grad,
        second_gain_grad,
        gate_w_grad,
        up_w_grad,
        down_w_grad,
    )


def solution(mesh):
    far = mesh.shape["dp"] // 2
    cores = mesh.shape["seq"] // HEADS
    fine = Mesh(mesh.devices.reshape(far, 2, HEADS, cores), ("dh", "dl", "h", "c"))
    dp, seq, every = ("dh", "dl"), ("h", "c"), ("dh", "dl", "h", "c")
    rows = P(every, None)
    return jax.shard_map(
        functools.partial(local, far),
        mesh=fine,
        in_specs=(
            P(dp, seq, None),
            P(dp, seq),
            P(dp, None),
            P(dp, seq, None, None),
            P(dp, None, None, None),
            P(dp, None, None, None),
            P(every),
            rows,
            rows,
            rows,
            rows,
            P(every),
            rows,
            rows,
            rows,
            P(dp, seq, None),
        ),
        out_specs=(
            P(dp, seq, None),
            P(dp, seq, None),
            P(every),
            rows,
            rows,
            rows,
            rows,
            P(every),
            rows,
            rows,
            rows,
        ),
        check_vma=False,
    )
```

time: 1480 us -> 592 us (0.40)
  waiting for transfers between devices: 766 us -> 189 us
  matrix products: 176 us -> 26.1 us
  Pallas kernels: 0 us -> 137 us
  starting transfers between devices: 233 us -> 111 us
  blocking collectives: 118 us -> 0 us
  local copies, waits for them, and re-layouts: 133 us -> 61 us
  other arithmetic: 27.3 us -> 42.1 us
    reduce_scatter x2 -> x1, waiting for transfers between devices: 510 us -> 0.01 us  [local(): lax.psum_scatter(parts.reshape(far * HEADS * height, wide), group, scatte...]
    dot_general x79 -> x9, matrix products: 176 us -> 26.1 us  [the longest x6 19.4 us: over_tokens(): return jnp.einsum('gtd,gtf->df', a, b, preferred_element_type=WIDE)]
    pallas_call x0 -> x15, Pallas kernels: none -> 137 us  [the longest x1 40.2 us: attend_back(): pl.pallas_call(attend_back_kernel, grid_spec=pltpu.PrefetchScalarGridSpec...]
    ppermute x40 -> x77, starting transfers between devices: 233 us -> 111 us  [the longest x49 95.6 us: turn(): return lax.ppermute(block, 'h', route)]
    unnamed x2 -> x0, blocking collectives: 118 us -> none
    gather x2 -> x0, local copies, waits for them, and re-layouts: 63 us -> none  [the longest x1 36.1 us: local(): cache_values[0].reshape(docs, MEM_ROWS, HEADS, HEAD_DIM)]
    all_gather x7 -> x1, waiting for transfers between devices: 53.5 us -> 0.02 us  [local(): lax.all_gather(jnp.concatenate([gu, lower], axis=0), group, axis=0)]
    unnamed x343 -> x180, local copies, waits for them, and re-layouts: 25.8 us -> 9.4 us
  transfers between devices with their start and end apart: 49 -> 79, of which waited for: 18 -> 35; matrix products, arithmetic and copies ran while one was open for 16% -> 19% of each run, Pallas kernels for 0% -> 24%
where the time goes in v1:
time: 592 us; the launch traced here: 582 us
  waiting for transfers between devices  189 us (32%)
  Pallas kernels  137 us (23%)
  starting transfers between devices  111 us (19%)
  local copies, waits for them, and re-layouts  61 us (10%)
  other arithmetic  42.1 us (7%)
  matrix products  26.1 us (4%)
  between operations  16.1 us (3%)
    ppermute x49, waiting for transfers between devices, turn(): return lax.ppermute(block, 'h', route)  143 us
    ppermute x49, starting transfers between devices, turn(): return lax.ppermute(block, 'h', route)  95.6 us
    ppermute x28, waiting for transfers between devices, swap(): return lax.ppermute(block, axis, [(0, 1), (1, 0)])  45 us
    pallas_call x1, Pallas kernels, attend_back(): pl.pallas_call(attend_back_kernel, grid_spec=pltpu.PrefetchScalarGridSpec...  40.2 us
    pallas_call x1, Pallas kernels, attend(): pl.pallas_call(attend_kernel, grid_spec=pltpu.PrefetchScalarGridSpec(num_...  35.8 us
    pallas_call x8, Pallas kernels, qkv_block(): pl.pallas_call(qkv_kernel, grid_spec=spec, out_shape=[jax.ShapeDtypeStruc...  23 us
    dot_general x6, matrix products, over_tokens(): return jnp.einsum('gtd,gtf->df', a, b, preferred_element_type=WIDE)  19.4 us
    pallas_call x2, Pallas kernels, ffn(): pl.pallas_call(ffn_kernel, in_specs=[vmem()] * 7, out_specs=[vmem()] * 4,...  18.4 us
  transfers between devices with their start and end apart: 79, of which 35 were waited for; matrix products, arithmetic and copies ran while one was open for 19% of the time, Pallas kernels for 24%

profile of v1, /device:TPU:0, one launch (start us, length us, event | category | flops | bytes accessed | tf_op | source)
XLA Modules:
  0.0 581.7 jit_solution(6699738325995926952)
XLA Ops:
  12.8 2.9 collective-permute-start.26
  15.7 4.8 collective-permute-done.26
  25.8 2.6 collective-permute-start.1
  32.6 3.7 fusion.49
  38.3 3.5 collective-permute-start.5
  53.1 5.3 collective-permute-done.12
  59.3 5.6 collective-permute-done.8.x_ref
  64.9 3.0 collective-permute-start.9
  70.3 17.5 %collective-permute-done.9.x_ref = bf16[256,1024]{1,0:T(8,128)(2,1)} collective-permute-done((bf16[256,1024]{1,0:T(8,128)(2,1)}, bf16[256,1024]{1,0:T(8,128)(2,1)}, u32[]{:S(2)}, u32[]{:S(2)}) %collective-permute-start.9) | collective-permute-done | bytes 524320 | tf_op jit(solution)/shard_map/ppermute | solution.py:47
  87.8 7.6 %collective-permute-start.10 = (bf16[256,1024]{1,0:T(8,128)(2,1)}, bf16[256,1024]{1,0:T(8,128)(2,1)}, u32[]{:S(2)}, u32[]{:S(2)}) collective-permute-start(bf16[256,1024]{1,0:T(8,128)(2,1)} %collective-permute-done.9.x_ref), channel_id=1, source_target_pairs={{0,4},{4,8},{8,12},{12,14},{14,10},{10,6},{6,2},{2,0},{1,5},{5,9},... | collective-permute-start | bytes 1572872 | tf_op jit(solution)/shard_map/ppermute | solution.py:47
  101.2 4.0 collective-permute-done.15.x_ref
  105.2 13.7 %collective-permute-done.10.x_ref = bf16[256,1024]{1,0:T(8,128)(2,1)} collective-permute-done((bf16[256,1024]{1,0:T(8,128)(2,1)}, bf16[256,1024]{1,0:T(8,128)(2,1)}, u32[]{:S(2)}, u32[]{:S(2)}) %collective-permute-start.10) | collective-permute-done | bytes 524320 | tf_op jit(solution)/shard_map/ppermute | solution.py:47
  118.9 11.7 %collective-permute-start.11 = (bf16[256,1024]{1,0:T(8,128)(2,1)}, bf16[256,1024]{1,0:T(8,128)(2,1)S(1)}, u32[]{:S(2)}, u32[]{:S(2)}) collective-permute-start(bf16[256,1024]{1,0:T(8,128)(2,1)} %collective-permute-done.10.x_ref), channel_id=1, source_target_pairs={{0,4},{4,8},{8,12},{12,14},{14,10},{10,6},{6,2},{2,0},{1,5},{5,9},... | collective-permute-start | bytes 1572872 | tf_op jit(solution)/shard_map/ppermute | solution.py:47
  132.7 2.8 qkv0.1
  135.5 2.9 qkv1.1
  138.4 2.9 qkv7.1
  141.3 2.9 qkv2.1
  144.2 2.9 qkv6.1
  147.0 2.9 qkv3.1
  150.7 2.9 qkv5.1
  154.4 2.9 qkv4.1
  161.2 35.8 %attend.1 = (f32[8,256,128]{2,1,0:T(8,128)}, bf16[8,256,128]{2,1,0:T(8,128)(2,1)}, f32[8,256,1]{2,1,0:T(8,128)}, bf16[2,8,256,128]{3,2,1,0:T(8,128)(2,1)}) custom-call(s32[72]{0:T(128)} %concatenate.171.tab, bf16[8,256,128]{2,1,0:T(8,128)(2,1)} %get-tuple-element.79.q_ref, bf16[2,8,256,128]{3,2,1,0:T(8,128)(2,1)} %get-tuple-element.80.own_ref, ...), custom_call_target="tpu_custom_call" | custom-call | flops 4000000000 | bytes 6291456 | tf_op jit(solution)/shard_map/attend/pallas_call | solution.py:216
  198.1 3.4 collective-permute-start.18
  207.8 3.8 collective-permute-done.19
  213.5 4.4 collective-permute-done.20
  217.8 3.1 collective-permute-start.21
  225.2 8.8 %collective-permute-done.28 = bf16[1,8,32,1024]{3,2,1,0:T(8,128)(2,1)S(1)} collective-permute-done((bf16[1,8,32,1024]{3,2,1,0:T(8,128)(2,1)S(1)}, bf16[1,8,32,1024]{3,2,1,0:T(8,128)(2,1)S(1)}, u32[]{:S(2)}, u32[]{:S(2)}) %collective-permute-start.28) | collective-permute-done | bytes 524320 | tf_op jit(solution)/shard_map/ppermute | solution.py:42
  237.6 3.7 out_block.1
  241.9 2.6 slice.796
  250.1 9.1 %ffn.2 = (bf16[2,256,704]{2,1,0:T(8,128)(2,1)}, bf16[2,256,704]{2,1,0:T(8,128)(2,1)}, bf16[2,256,704]{2,1,0:T(8,128)(2,1)}, bf16[2,256,1024]{2,1,0:T(8,128)(2,1)}) custom-call(bf16[256,1024]{1,0:T(8,128)(2,1)} %get-tuple-element.83.na, bf16[256,1024]{1,0:T(8,128)(2,1)} %copy-done.12, bf16[256,1024]{1,0:T(8,128)(2,1)} %bitcast.575, ...), custom_call_target="tpu_custom_call" | custom-call | flops 3690987520 | bytes 8519680 | tf_op jit(solution)/shard_map/ffn/pallas_call | solution.py:366
  267.6 3.7 fusion.40
  271.3 3.6 fusion.39
  275.6 9.3 %ffn.3 = (bf16[2,256,704]{2,1,0:T(8,128)(2,1)}, bf16[2,256,704]{2,1,0:T(8,128)(2,1)}, bf16[2,256,704]{2,1,0:T(8,128)(2,1)}, bf16[2,256,1024]{2,1,0:T(8,128)(2,1)}) custom-call(bf16[256,1024]{1,0:T(8,128)(2,1)} %collective-permute-done.33.na, bf16[256,1024]{1,0:T(8,128)(2,1)} %copy-done.14, bf16[256,1024]{1,0:T(8,128)(2,1)} %collective-permute-done.35.ga, ...), custom_call_target="tpu_custom_call" | custom-call | flops 3690987520 | bytes 8519680 | tf_op jit(solution)/shard_map/ffn/pallas_call | solution.py:366
  287.1 2.7 convolution_convert_fusion.1
  291.8 3.2 fusion.4
  297.6 2.9 copy.610
  300.5 3.4 fusion.3
  306.5 2.8 copy.614
  312.7 3.4 fusion.2
  318.2 7.3 %collective-permute-done.41.pc = bf16[256,1024]{1,0:T(8,128)(2,1)S(1)} collective-permute-done((bf16[256,1024]{1,0:T(8,128)(2,1)S(1)}, bf16[256,1024]{1,0:T(8,128)(2,1)S(1)}, u32[]{:S(2)}, u32[]{:S(2)}) %collective-permute-start.41) | collective-permute-done | bytes 524320 | tf_op jit(solution)/shard_map/ppermute | solution.py:42
  326.3 4.6 mid_block.1
  338.5 2.7 collective-permute-start.43
  345.9 4.5 collective-permute-done.44
  352.0 5.6 collective-permute-done.45
  358.1 6.0 %collective-permute-done.46 = bf16[256,128]{1,0:T(8,128)(2,1)S(1)} collective-permute-done((bf16[256,128]{1,0:T(8,128)(2,1)S(1)}, bf16[256,128]{1,0:T(8,128)(2,1)S(1)}, u32[]{:S(2)}, u32[]{:S(2)}) %collective-permute-start.46) | collective-permute-done | bytes 65568 | tf_op jit(solution)/shard_map/ppermute | solution.py:47
  365.0 40.2 %attend_back.1 = (f32[8,256,128]{2,1,0:T(8,128)}, f32[2,8,256,128]{3,2,1,0:T(8,128)}, bf16[2,8,256,128]{3,2,1,0:T(8,128)(2,1)}) custom-call(s32[72]{0:T(128)} %concatenate.171.tab, bf16[8,256,128]{2,1,0:T(8,128)(2,1)} %get-tuple-element.79.q_ref, bf16[8,256,128]{2,1,0:T(8,128)(2,1)} %copy-done.46, f32[8,256,128]{2,1,0:T(8,128)} %get-tuple-element.90.o_ref, ...), custom_call_target="tpu_custom_call" | custom-call | flops 10000000000 | bytes 10485760 | tf_op jit(solution)/shard_map/attend_back/pallas_call | solution.py:299
  405.2 4.4 fusion.1
  413.3 3.2 convert_add_fusion
  416.5 11.7 %qkv_back.1 = (bf16[8,256,1024]{2,1,0:T(8,128)(2,1)}, bf16[1024,384]{1,0:T(8,128)(2,1)}) custom-call(f32[8,256,128]{2,1,0:T(8,128)} %get-tuple-element.93.dq_ref, f32[2,8,256,128]{3,2,1,0:T(8,128)} %get-tuple-element.94.own_ref, bf16[2,8,256,128]{3,2,1,0:T(8,128)(2,1)} %collective-permute-done.49.got_ref, f32[8,256,128]{2,1,0:T(8,128)} %get-tuple-element.215.cos_ref, ...), custom_call_target="tpu_custom_call" | custom-call | flops 3221225472 | bytes 8388608 | tf_op jit(solution)/shard_map/qkv_back/pallas_call | solution.py:445
  433.7 11.1 %collective-permute-done.67 = bf16[1,8,32,1024]{3,2,1,0:T(8,128)(2,1)S(1)} collective-permute-done((bf16[1,8,32,1024]{3,2,1,0:T(8,128)(2,1)S(1)}, bf16[1,8,32,1024]{3,2,1,0:T(8,128)(2,1)S(1)}, u32[]{:S(2)}, u32[]{:S(2)}) %collective-permute-start.67) | collective-permute-done | bytes 524320 | tf_op jit(solution)/shard_map/ppermute | solution.py:42
  445.5 4.2 collective-permute-start.73
  449.9 5.0 collective-permute-done.50
  458.6 12.8 %collective-permute-start.70 = (bf16[32,1024]{1,0:T(8,128)(2,1)S(1)}, bf16[32,1024]{1,0:T(8,128)(2,1)S(1)}, u32[]{:S(2)}, u32[]{:S(2)}) collective-permute-start(bf16[32,1024]{1,0:T(8,128)(2,1)S(1)} %get-tuple-element.132), channel_id=1, source_target_pairs={{0,12},{4,14},{8,10},{12,6},{14,2},{10,0},{6,4},{2,8},{1,13},{5,15... | collective-permute-start | bytes 196616 | tf_op jit(solution)/shard_map/ppermute | solution.py:47
  475.5 2.8 collective-permute-done.70
  480.0 4.0 collective-permute-start.65
  484.0 15.6 %collective-permute-done.59 = bf16[32,384]{1,0:T(8,128)(2,1)S(1)} collective-permute-done((bf16[32,384]{1,0:T(8,128)(2,1)S(1)}, bf16[32,384]{1,0:T(8,128)(2,1)S(1)}, u32[]{:S(2)}, u32[]{:S(2)}) %collective-permute-start.59) | collective-permute-done | bytes 24608 | tf_op jit(solution)/shard_map/ppermute | solution.py:47
  499.7 4.7 collective-permute-done.60
  504.4 5.6 collective-permute-done.61
  511.6 5.5 collective-permute-done.62
  517.1 6.4 %collective-permute-done.63 = bf16[32,384]{1,0:T(8,128)(2,1)S(1)} collective-permute-done((bf16[32,384]{1,0:T(8,128)(2,1)S(1)}, bf16[32,384]{1,0:T(8,128)(2,1)S(1)}, u32[]{:S(2)}, u32[]{:S(2)}) %collective-permute-start.63) | collective-permute-done | bytes 24608 | tf_op jit(solution)/shard_map/ppermute | solution.py:47
  528.6 13.9 %collective-permute-done.52 = bf16[256,1024]{1,0:T(8,128)(2,1)S(1)} collective-permute-done((bf16[256,1024]{1,0:T(8,128)(2,1)S(1)}, bf16[256,1024]{1,0:T(8,128)(2,1)S(1)}, u32[]{:S(2)}, u32[]{:S(2)}) %collective-permute-start.52) | collective-permute-done | bytes 524320 | tf_op jit(solution)/shard_map/ppermute | solution.py:47
  542.5 2.7 collective-permute-done.55
  549.9 8.4 %collective-permute-done.53 = bf16[256,1024]{1,0:T(8,128)(2,1)S(1)} collective-permute-done((bf16[256,1024]{1,0:T(8,128)(2,1)S(1)}, bf16[256,1024]{1,0:T(8,128)(2,1)S(1)}, u32[]{:S(2)}, u32[]{:S(2)}) %collective-permute-start.53) | collective-permute-done | bytes 524320 | tf_op jit(solution)/shard_map/ppermute | solution.py:47
  567.9 2.8 collective-permute-done.76
  (468 shorter events, 151.2 us)
Async XLA Ops:
  7.2 213.7 %all-gather.3.cloned.1.call-start = ((), (), s32[]{:S(2)}) async-start(), calls=%async_computation.2 | async-start | bytes 5677056 | tf_op jit(solution)/shard_map/all_gather | solution.py:624
  12.8 7.8 %collective-permute-start.26 = (bf16[2,32,1408]{2,1,0:T(8,128)(2,1)S(1)}, bf16[2,32,1408]{2,1,0:T(8,128)(2,1)S(1)}, u32[]{:S(2)}, u32[]{:S(2)}) collective-permute-start(bf16[2,32,1408]{2,1,0:T(8,128)(2,1)S(1)} %fusion.56), channel_id=1, source_target_pairs={{0,16},{16,0},{1,17},{17,1},{2,18},{18,2},{3,19},{19,3},{4,20},{20... | collective-permute-start | bytes 540680 | tf_op jit(solution)/shard_map/ppermute | solution.py:42
  21.6 539.8 %reduce-scatter.2.cloned.1.call-start = ((), (), s32[]{:S(2)}) async-start(), calls=%async_computation.1 | async-start | bytes 5677056 | tf_op jit(solution)/shard_map/reduce_scatter | solution.py:722
  23.9 14.4 %collective-permute-start = (bf16[112,128]{1,0:T(8,128)(2,1)S(1)}, bf16[112,128]{1,0:T(8,128)(2,1)S(1)}, u32[]{:S(2)}, u32[]{:S(2)}) collective-permute-start(bf16[112,128]{1,0:T(8,128)(2,1)S(1)} %bitcast.624), channel_id=1, source_target_pairs={{0,4},{4,8},{8,12},{12,14},{14,10},{10,6},{6,2},{2,0},{1,5},{5,9},... | collective-permute-start | bytes 86024 | tf_op jit(solution)/shard_map/ppermute | solution.py:47
  25.8 16.1 %collective-permute-start.1 = (bf16[112,128]{1,0:T(8,128)(2,1)S(1)}, bf16[112,128]{1,0:T(8,128)(2,1)S(1)}, u32[]{:S(2)}, u32[]{:S(2)}) collective-permute-start(bf16[112,128]{1,0:T(8,128)(2,1)S(1)} %bitcast.623), channel_id=1, source_target_pairs={{0,8},{4,12},{8,14},{12,10},{14,6},{10,2},{6,0},{2,4},{1,9},{5,13}... | collective-permute-start | bytes 86024 | tf_op jit(solution)/shard_map/ppermute | solution.py:47
  28.4 13.6 %collective-permute-start.2 = (bf16[112,128]{1,0:T(8,128)(2,1)S(1)}, bf16[112,128]{1,0:T(8,128)(2,1)S(1)}, u32[]{:S(2)}, u32[]{:S(2)}) collective-permute-start(bf16[112,128]{1,0:T(8,128)(2,1)S(1)} %bitcast.619), channel_id=1, source_target_pairs={{0,12},{4,14},{8,10},{12,6},{14,2},{10,0},{6,4},{2,8},{1,13},{5,15... | collective-permute-start | bytes 86024 | tf_op jit(solution)/shard_map/ppermute | solution.py:47
  29.7 14.0 %collective-permute-start.3 = (bf16[112,128]{1,0:T(8,128)(2,1)S(1)}, bf16[112,128]{1,0:T(8,128)(2,1)S(1)}, u32[]{:S(2)}, u32[]{:S(2)}) collective-permute-start(bf16[112,128]{1,0:T(8,128)(2,1)S(1)} %bitcast.616), channel_id=1, source_target_pairs={{0,14},{4,10},{8,6},{12,2},{14,0},{10,4},{6,8},{2,12},{1,15},{5,11... | collective-permute-start | bytes 86024 | tf_op jit(solution)/shard_map/ppermute | solution.py:47
  32.1 11.7 %collective-permute-start.4 = (bf16[112,128]{1,0:T(8,128)(2,1)S(1)}, bf16[112,128]{1,0:T(8,128)(2,1)S(1)}, u32[]{:S(2)}, u32[]{:S(2)}) collective-permute-start(bf16[112,128]{1,0:T(8,128)(2,1)S(1)} %bitcast.613), channel_id=1, source_target_pairs={{0,10},{4,6},{8,2},{12,0},{14,4},{10,8},{6,12},{2,14},{1,11},{5,7}... | collective-permute-start | bytes 86024 | tf_op jit(solution)/shard_map/ppermute | solution.py:47
  38.3 7.6 %collective-permute-start.5 = (bf16[112,128]{1,0:T(8,128)(2,1)S(1)}, bf16[112,128]{1,0:T(8,128)(2,1)S(1)}, u32[]{:S(2)}, u32[]{:S(2)}) collective-permute-start(bf16[112,128]{1,0:T(8,128)(2,1)S(1)} %bitcast.620), channel_id=1, source_target_pairs={{0,6},{4,2},{8,0},{12,4},{14,8},{10,12},{6,14},{2,10},{1,7},{5,3},... | collective-permute-start | bytes 86024 | tf_op jit(solution)/shard_map/ppermute | solution.py:47
  42.0 199.5 %collective-permute-start.35 = (bf16[256,1024]{1,0:T(8,128)(2,1)S(1)}, bf16[256,1024]{1,0:T(8,128)(2,1)}, u32[]{:S(2)}, u32[]{:S(2)}) collective-permute-start(bf16[256,1024]{1,0:T(8,128)(2,1)S(1)} %bitcast.577), channel_id=1, source_target_pairs={{0,16},{16,0},{1,17},{17,1},{2,18},{18,2},{3,19},{19,3},{4,20},{20... | collective-permute-start | bytes 1572872 | tf_op jit(solution)/shard_map/ppermute | solution.py:42
  43.6 205.6 %collective-permute-start.31 = (bf16[256,1024]{1,0:T(8,128)(2,1)S(1)}, bf16[256,1024]{1,0:T(8,128)(2,1)}, u32[]{:S(2)}, u32[]{:S(2)}) collective-permute-start(bf16[256,1024]{1,0:T(8,128)(2,1)S(1)} %bitcast.578), channel_id=1, source_target_pairs={{0,1},{1,0},{2,3},{3,2},{4,5},{5,4},{6,7},{7,6},{8,9},{9,8},{10,11... | collective-permute-start | bytes 1572872 | tf_op jit(solution)/shard_map/ppermute | solution.py:42
  43.8 21.1 %collective-permute-start.8 = (bf16[256,1024]{1,0:T(8,128)(2,1)S(1)}, bf16[256,1024]{1,0:T(8,128)(2,1)}, u32[]{:S(2)}, u32[]{:S(2)}) collective-permute-start(bf16[256,1024]{1,0:T(8,128)(2,1)S(1)} %bitcast.560), channel_id=1, source_target_pairs={{0,4},{4,8},{8,12},{12,14},{14,10},{10,6},{6,2},{2,0},{1,5},{5,9},... | collective-permute-start | bytes 1572872 | tf_op jit(solution)/shard_map/ppermute | solution.py:47
  48.2 10.2 %collective-permute-start.12 = (bf16[8,112,128]{2,0,1:T(8,128)(2,1)S(1)}, bf16[8,112,128]{2,0,1:T(8,128)(2,1)S(1)}, u32[]{:S(2)}, u32[]{:S(2)}) collective-permute-start(bf16[8,112,128]{2,0,1:T(8,128)(2,1)S(1)} %stack.301), channel_id=1, source_target_pairs={{0,16},{16,0},{1,17},{17,1},{2,18},{18,2},{3,19},{19,3},{4,20},{20... | collective-permute-start | bytes 688136 | tf_op jit(solution)/shard_map/ppermute | solution.py:42
  49.7 9.6 %collective-permute-start.7 = (bf16[8,112,128]{2,0,1:T(8,128)(2,1)S(1)}, bf16[8,112,128]{2,0,1:T(8,128)(2,1)S(1)}, u32[]{:S(2)}, u32[]{:S(2)}) collective-permute-start(bf16[8,112,128]{2,0,1:T(8,128)(2,1)S(1)} %stack.301), channel_id=1, source_target_pairs={{0,1},{1,0},{2,3},{3,2},{4,5},{5,4},{6,7},{7,6},{8,9},{9,8},{10,11... | collective-permute-start | bytes 688136 | tf_op jit(solution)/shard_map/ppermute | solution.py:42
  58.4 11.6 %collective-permute-start.14 = (bf16[256,1024]{1,0:T(8,128)(2,1)S(1)}, bf16[256,1024]{1,0:T(8,128)(2,1)}, u32[]{:S(2)}, u32[]{:S(2)}) collective-permute-start(bf16[256,1024]{1,0:T(8,128)(2,1)S(1)} %bitcast.561), channel_id=1, source_target_pairs={{0,2},{4,0},{8,4},{12,8},{14,12},{10,14},{6,10},{2,6},{1,3},{5,1},... | collective-permute-start | bytes 1572872 | tf_op jit(solution)/shard_map/ppermute | solution.py:47
  59.3 8.7 %collective-permute-start.13 = (bf16[8,112,128]{2,0,1:T(8,128)(2,1)S(1)}, bf16[8,112,128]{2,0,1:T(8,128)(2,1)S(1)}, u32[]{:S(2)}, u32[]{:S(2)}) collective-permute-start(bf16[8,112,128]{2,0,1:T(8,128)(2,1)S(1)} %collective-permute-done.12), channel_id=1, source_target_pairs={{0,1},{1,0},{2,3},{3,2},{4,5},{5,4},{6,7},{7,6},{8,9},{9,8},{10,11... | collective-permute-start | bytes 688136 | tf_op jit(solution)/shard_map/ppermute | solution.py:42
  64.9 22.9 %collective-permute-start.9 = (bf16[256,1024]{1,0:T(8,128)(2,1)}, bf16[256,1024]{1,0:T(8,128)(2,1)}, u32[]{:S(2)}, u32[]{:S(2)}) collective-permute-start(bf16[256,1024]{1,0:T(8,128)(2,1)} %collective-permute-done.8.x_ref), channel_id=1, source_target_pairs={{0,4},{4,8},{8,12},{12,14},{14,10},{10,6},{6,2},{2,0},{1,5},{5,9},... | collective-permute-start | bytes 1572872 | tf_op jit(solution)/shard_map/ppermute | solution.py:47
  70.0 35.2 %collective-permute-start.15 = (bf16[256,1024]{1,0:T(8,128)(2,1)}, bf16[256,1024]{1,0:T(8,128)(2,1)}, u32[]{:S(2)}, u32[]{:S(2)}) collective-permute-start(bf16[256,1024]{1,0:T(8,128)(2,1)} %collective-permute-done.14.x_ref), channel_id=1, source_target_pairs={{0,2},{4,0},{8,4},{12,8},{14,12},{10,14},{6,10},{2,6},{1,3},{5,1},... | collective-permute-start | bytes 1572872 | tf_op jit(solution)/shard_map/ppermute | solution.py:47
  87.8 31.1 %collective-permute-start.10 = (bf16[256,1024]{1,0:T(8,128)(2,1)}, bf16[256,1024]{1,0:T(8,128)(2,1)}, u32[]{:S(2)}, u32[]{:S(2)}) collective-permute-start(bf16[256,1024]{1,0:T(8,128)(2,1)} %collective-permute-done.9.x_ref), channel_id=1, source_target_pairs={{0,4},{4,8},{8,12},{12,14},{14,10},{10,6},{6,2},{2,0},{1,5},{5,9},... | collective-permute-start | bytes 1572872 | tf_op jit(solution)/shard_map/ppermute | solution.py:47
  105.2 44.7 %collective-permute-start.16 = (bf16[256,1024]{1,0:T(8,128)(2,1)}, bf16[256,1024]{1,0:T(8,128)(2,1)S(1)}, u32[]{:S(2)}, u32[]{:S(2)}) collective-permute-start(bf16[256,1024]{1,0:T(8,128)(2,1)} %collective-permute-done.15.x_ref), channel_id=1, source_target_pairs={{0,2},{4,0},{8,4},{12,8},{14,12},{10,14},{6,10},{2,6},{1,3},{5,1},... | collective-permute-start | bytes 1572872 | tf_op jit(solution)/shard_map/ppermute | solution.py:47
  118.9 34.7 %collective-permute-start.11 = (bf16[256,1024]{1,0:T(8,128)(2,1)}, bf16[256,1024]{1,0:T(8,128)(2,1)S(1)}, u32[]{:S(2)}, u32[]{:S(2)}) collective-permute-start(bf16[256,1024]{1,0:T(8,128)(2,1)} %collective-permute-done.10.x_ref), channel_id=1, source_target_pairs={{0,4},{4,8},{8,12},{12,14},{14,10},{10,6},{6,2},{2,0},{1,5},{5,9},... | collective-permute-start | bytes 1572872 | tf_op jit(solution)/shard_map/ppermute | solution.py:47
  198.1 7.8 %collective-permute-start.18 = (bf16[256,128]{1,0:T(8,128)(2,1)S(1)}, bf16[256,128]{1,0:T(8,128)(2,1)S(1)}, u32[]{:S(2)}, u32[]{:S(2)}) collective-permute-start(bf16[256,128]{1,0:T(8,128)(2,1)S(1)} %get-tuple-element.162), channel_id=1, source_target_pairs={{0,2},{4,0},{8,4},{12,8},{14,12},{10,14},{6,10},{2,6},{1,3},{5,1},... | collective-permute-start | bytes 196616 | tf_op jit(solution)/shard_map/ppermute | solution.py:47
  202.7 22.2 %collective-permute-start.23 = (bf16[256,128]{1,0:T(8,128)(2,1)S(1)}, bf16[256,128]{1,0:T(8,128)(2,1)S(1)}, u32[]{:S(2)}, u32[]{:S(2)}) collective-permute-start(bf16[256,128]{1,0:T(8,128)(2,1)S(1)} %get-tuple-element.157), channel_id=1, source_target_pairs={{0,8},{4,12},{8,14},{12,10},{14,6},{10,2},{6,0},{2,4},{1,9},{5,13}... | collective-permute-start | bytes 196616 | tf_op jit(solution)/shard_map/ppermute | solution.py:47
  204.3 20.5 %collective-permute-start.22 = (bf16[256,128]{1,0:T(8,128)(2,1)S(1)}, bf16[256,128]{1,0:T(8,128)(2,1)S(1)}, u32[]{:S(2)}, u32[]{:S(2)}) collective-permute-start(bf16[256,128]{1,0:T(8,128)(2,1)S(1)} %get-tuple-element.158), channel_id=1, source_target_pairs={{0,12},{4,14},{8,10},{12,6},{14,2},{10,0},{6,4},{2,8},{1,13},{5,15... | collective-permute-start | bytes 196616 | tf_op jit(solution)/shard_map/ppermute | solution.py:47
  217.8 7.0 %collective-permute-start.21 = (bf16[256,128]{1,0:T(8,128)(2,1)S(1)}, bf16[256,128]{1,0:T(8,128)(2,1)S(1)}, u32[]{:S(2)}, u32[]{:S(2)}) collective-permute-start(bf16[256,128]{1,0:T(8,128)(2,1)S(1)} %get-tuple-element.159), channel_id=1, source_target_pairs={{0,14},{4,10},{8,6},{12,2},{14,0},{10,4},{6,8},{2,12},{1,15},{5,11... | collective-permute-start | bytes 196616 | tf_op jit(solution)/shard_map/ppermute | solution.py:47
  224.8 9.2 %collective-permute-start.28 = (bf16[1,8,32,1024]{3,2,1,0:T(8,128)(2,1)S(1)}, bf16[1,8,32,1024]{3,2,1,0:T(8,128)(2,1)S(1)}, u32[]{:S(2)}, u32[]{:S(2)}) collective-permute-start(bf16[1,8,32,1024]{3,2,1,0:T(8,128)(2,1)S(1)} %pad_maximum_fusion.12), channel_id=1, source_target_pairs={{0,16},{16,0},{1,17},{17,1},{2,18},{18,2},{3,19},{19,3},{4,20},{20... | collective-permute-start | bytes 1572872 | tf_op jit(solution)/shard_map/ppermute | solution.py:42
  224.8 9.2 %collective-permute-start.27 = (bf16[1,8,32,1024]{3,2,1,0:T(8,128)(2,1)S(1)}, bf16[1,8,32,1024]{3,2,1,0:T(8,128)(2,1)S(1)}, u32[]{:S(2)}, u32[]{:S(2)}) collective-permute-start(bf16[1,8,32,1024]{3,2,1,0:T(8,128)(2,1)S(1)} %pad_maximum_fusion.12), channel_id=1, source_target_pairs={{0,1},{1,0},{2,3},{3,2},{4,5},{5,4},{6,7},{7,6},{8,9},{9,8},{10,11... | collective-permute-start | bytes 1572872 | tf_op jit(solution)/shard_map/ppermute | solution.py:42
  224.9 9.1 %collective-permute-start.24 = (bf16[256,128]{1,0:T(8,128)(2,1)S(1)}, bf16[256,128]{1,0:T(8,128)(2,1)S(1)}, u32[]{:S(2)}, u32[]{:S(2)}) collective-permute-start(bf16[256,128]{1,0:T(8,128)(2,1)S(1)} %get-tuple-element.156), channel_id=1, source_target_pairs={{0,4},{4,8},{8,12},{12,14},{14,10},{10,6},{6,2},{2,0},{1,5},{5,9},... | collective-permute-start | bytes 196616 | tf_op jit(solution)/shard_map/ppermute | solution.py:47
  241.3 8.0 %collective-permute-start.30 = (bf16[256,1024]{1,0:T(8,128)(2,1)}, bf16[256,1024]{1,0:T(8,128)(2,1)S(1)}, u32[]{:S(2)}, u32[]{:S(2)}) collective-permute-start(bf16[256,1024]{1,0:T(8,128)(2,1)} %get-tuple-element.83.na), channel_id=1, source_target_pairs={{0,1},{1,0},{2,3},{3,2},{4,5},{5,4},{6,7},{7,6},{8,9},{9,8},{10,11... | collective-permute-start | bytes 1572872 | tf_op jit(solution)/shard_map/ppermute | solution.py:42
  241.5 33.3 %collective-permute-start.36 = (bf16[256,1024]{1,0:T(8,128)(2,1)}, bf16[256,1024]{1,0:T(8,128)(2,1)}, u32[]{:S(2)}, u32[]{:S(2)}) collective-permute-start(bf16[256,1024]{1,0:T(8,128)(2,1)} %collective-permute-done.35.ga), channel_id=1, source_target_pairs={{0,1},{1,0},{2,3},{3,2},{4,5},{5,4},{6,7},{7,6},{8,9},{9,8},{10,11... | collective-permute-start | bytes 1572872 | tf_op jit(solution)/shard_map/ppermute | solution.py:42
  249.3 18.0 %collective-permute-start.33 = (bf16[256,1024]{1,0:T(8,128)(2,1)}, bf16[256,1024]{1,0:T(8,128)(2,1)}, u32[]{:S(2)}, u32[]{:S(2)}) collective-permute-start(bf16[256,1024]{1,0:T(8,128)(2,1)} %get-tuple-element.83.na), channel_id=1, source_target_pairs={{0,16},{16,0},{1,17},{17,1},{2,18},{18,2},{3,19},{19,3},{4,20},{20... | collective-permute-start | bytes 1572872 | tf_op jit(solution)/shard_map/ppermute | solution.py:42
  261.5 56.7 %collective-permute-start.39 = (bf16[256,1024]{1,0:T(8,128)(2,1)}, bf16[256,1024]{1,0:T(8,128)(2,1)}, u32[]{:S(2)}, u32[]{:S(2)}) collective-permute-start(bf16[256,1024]{1,0:T(8,128)(2,1)} %get-tuple-element.135), channel_id=1, source_target_pairs={{0,1},{1,0},{2,3},{3,2},{4,5},{5,4},{6,7},{7,6},{8,9},{9,8},{10,11... | collective-permute-start | bytes 1572872 | tf_op jit(solution)/shard_map/ppermute | solution.py:42
  264.8 144.9 %collective-permute-start.32 = (bf16[256,1024]{1,0:T(8,128)(2,1)}, bf16[256,1024]{1,0:T(8,128)(2,1)}, u32[]{:S(2)}, u32[]{:S(2)}) collective-permute-start(bf16[256,1024]{1,0:T(8,128)(2,1)} %slice_bitcast_fusion.4), channel_id=1, source_target_pairs={{0,1},{1,0},{2,3},{3,2},{4,5},{5,4},{6,7},{7,6},{8,9},{9,8},{10,11... | collective-permute-start | bytes 1572872 | tf_op jit(solution)/shard_map/ppermute | solution.py:42
  267.3 7.6 %collective-permute-start.34 = (bf16[256,1024]{1,0:T(8,128)(2,1)}, bf16[256,1024]{1,0:T(8,128)(2,1)S(1)}, u32[]{:S(2)}, u32[]{:S(2)}) collective-permute-start(bf16[256,1024]{1,0:T(8,128)(2,1)} %collective-permute-done.33.na), channel_id=1, source_target_pairs={{0,1},{1,0},{2,3},{3,2},{4,5},{5,4},{6,7},{7,6},{8,9},{9,8},{10,11... | collective-permute-start | bytes 1572872 | tf_op jit(solution)/shard_map/ppermute | solution.py:42
  286.8 22.6 %collective-permute-start.40 = (bf16[256,1024]{1,0:T(8,128)(2,1)}, bf16[256,1024]{1,0:T(8,128)(2,1)}, u32[]{:S(2)}, u32[]{:S(2)}) collective-permute-start(bf16[256,1024]{1,0:T(8,128)(2,1)} %slice_bitcast_fusion.8), channel_id=1, source_target_pairs={{0,1},{1,0},{2,3},{3,2},{4,5},{5,4},{6,7},{7,6},{8,9},{9,8},{10,11... | collective-permute-start | bytes 1572872 | tf_op jit(solution)/shard_map/ppermute | solution.py:42
  291.6 24.5 %collective-permute-start.37 = (bf16[256,1024]{1,0:T(8,128)(2,1)}, bf16[256,1024]{1,0:T(8,128)(2,1)}, u32[]{:S(2)}, u32[]{:S(2)}) collective-permute-start(bf16[256,1024]{1,0:T(8,128)(2,1)} %slice_bitcast_fusion.2), channel_id=1, source_target_pairs={{0,1},{1,0},{2,3},{3,2},{4,5},{5,4},{6,7},{7,6},{8,9},{9,8},{10,11... | collective-permute-start | bytes 1572872 | tf_op jit(solution)/shard_map/ppermute | solution.py:42
  310.6 14.9 %collective-permute-start.41 = (bf16[256,1024]{1,0:T(8,128)(2,1)S(1)}, bf16[256,1024]{1,0:T(8,128)(2,1)S(1)}, u32[]{:S(2)}, u32[]{:S(2)}) collective-permute-start(bf16[256,1024]{1,0:T(8,128)(2,1)S(1)} %fusion.29), channel_id=1, source_target_pairs={{0,16},{16,0},{1,17},{17,1},{2,18},{18,2},{3,19},{19,3},{4,20},{20... | collective-permute-start | bytes 1572872 | tf_op jit(solution)/shard_map/ppermute | solution.py:42
  318.1 91.5 %collective-permute-start.38 = (bf16[256,1024]{1,0:T(8,128)(2,1)}, bf16[256,1024]{1,0:T(8,128)(2,1)}, u32[]{:S(2)}, u32[]{:S(2)}) collective-permute-start(bf16[256,1024]{1,0:T(8,128)(2,1)} %fusion.30), channel_id=1, source_target_pairs={{0,16},{16,0},{1,17},{17,1},{2,18},{18,2},{3,19},{19,3},{4,20},{20... | collective-permute-start | bytes 1572872 | tf_op jit(solution)/shard_map/ppermute | solution.py:42
  332.0 32.1 %collective-permute-start.48 = (bf16[256,128]{1,0:T(8,128)(2,1)S(1)}, bf16[256,128]{1,0:T(8,128)(2,1)S(1)}, u32[]{:S(2)}, u32[]{:S(2)}) collective-permute-start(bf16[256,128]{1,0:T(8,128)(2,1)S(1)} %get-tuple-element.148), channel_id=1, source_target_pairs={{0,2},{4,0},{8,4},{12,8},{14,12},{10,14},{6,10},{2,6},{1,3},{5,1},... | collective-permute-start | bytes 196616 | tf_op jit(solution)/shard_map/ppermute | solution.py:47
  334.0 30.1 %collective-permute-start.47 = (bf16[256,128]{1,0:T(8,128)(2,1)S(1)}, bf16[256,128]{1,0:T(8,128)(2,1)S(1)}, u32[]{:S(2)}, u32[]{:S(2)}) collective-permute-start(bf16[256,128]{1,0:T(8,128)(2,1)S(1)} %get-tuple-element.149), channel_id=1, source_target_pairs={{0,6},{4,2},{8,0},{12,4},{14,8},{10,12},{6,14},{2,10},{1,7},{5,3},... | collective-permute-start | bytes 196616 | tf_op jit(solution)/shard_map/ppermute | solution.py:47
  343.7 6.7 %collective-permute-start.44 = (bf16[256,128]{1,0:T(8,128)(2,1)S(1)}, bf16[256,128]{1,0:T(8,128)(2,1)S(1)}, u32[]{:S(2)}, u32[]{:S(2)}) collective-permute-start(bf16[256,128]{1,0:T(8,128)(2,1)S(1)} %get-tuple-element.152), channel_id=1, source_target_pairs={{0,12},{4,14},{8,10},{12,6},{14,2},{10,0},{6,4},{2,8},{1,13},{5,15... | collective-permute-start | bytes 196616 | tf_op jit(solution)/shard_map/ppermute | solution.py:47
  350.4 7.2 %collective-permute-start.45 = (bf16[256,128]{1,0:T(8,128)(2,1)S(1)}, bf16[256,128]{1,0:T(8,128)(2,1)S(1)}, u32[]{:S(2)}, u32[]{:S(2)}) collective-permute-start(bf16[256,128]{1,0:T(8,128)(2,1)S(1)} %get-tuple-element.151), channel_id=1, source_target_pairs={{0,14},{4,10},{8,6},{12,2},{14,0},{10,4},{6,8},{2,12},{1,15},{5,11... | collective-permute-start | bytes 196616 | tf_op jit(solution)/shard_map/ppermute | solution.py:47
  364.1 49.2 %collective-permute-start.66 = (bf16[1,2,8,32,1024]{4,3,2,1,0:T(8,128)(2,1)}, bf16[1,2,8,32,1024]{4,3,2,1,0:T(8,128)(2,1)}, u32[]{:S(2)}, u32[]{:S(2)}) collective-permute-start(bf16[1,2,8,32,1024]{4,3,2,1,0:T(8,128)(2,1)} %select_bitcast_fusion), channel_id=1, source_target_pairs={{0,1},{1,0},{2,3},{3,2},{4,5},{5,4},{6,7},{7,6},{8,9},{9,8},{10,11... | collective-permute-start | bytes 3145736 | tf_op jit(solution)/shard_map/ppermute | solution.py:42
  405.1 11.4 %collective-permute-start.49 = (bf16[2,8,256,128]{3,2,1,0:T(8,128)(2,1)}, bf16[2,8,256,128]{3,2,1,0:T(8,128)(2,1)}, u32[]{:S(2)}, u32[]{:S(2)}) collective-permute-start(bf16[2,8,256,128]{3,2,1,0:T(8,128)(2,1)} %get-tuple-element.95), channel_id=1, source_target_pairs={{0,1},{1,0},{2,3},{3,2},{4,5},{5,4},{6,7},{7,6},{8,9},{9,8},{10,11... | collective-permute-start | bytes 3145736 | tf_op jit(solution)/shard_map/ppermute | solution.py:42
  430.0 14.9 %collective-permute-start.67 = (bf16[1,8,32,1024]{3,2,1,0:T(8,128)(2,1)S(1)}, bf16[1,8,32,1024]{3,2,1,0:T(8,128)(2,1)S(1)}, u32[]{:S(2)}, u32[]{:S(2)}) collective-permute-start(bf16[1,8,32,1024]{3,2,1,0:T(8,128)(2,1)S(1)} %fusion.44), channel_id=1, source_target_pairs={{0,16},{16,0},{1,17},{17,1},{2,18},{18,2},{3,19},{19,3},{4,20},{20... | collective-permute-start | bytes 1572872 | tf_op jit(solution)/shard_map/ppermute | solution.py:42
  431.3 23.6 %collective-permute-start.50 = (bf16[256,1024]{1,0:T(8,128)(2,1)S(1)}, bf16[256,1024]{1,0:T(8,128)(2,1)S(1)}, u32[]{:S(2)}, u32[]{:S(2)}) collective-permute-start(bf16[256,1024]{1,0:T(8,128)(2,1)S(1)} %get-tuple-element.122), channel_id=1, source_target_pairs={{0,4},{4,8},{8,12},{12,14},{14,10},{10,6},{6,2},{2,0},{1,5},{5,9},... | collective-permute-start | bytes 1572872 | tf_op jit(solution)/shard_map/ppermute | solution.py:47
  431.6 27.0 %collective-permute-start.58 = (bf16[1,8,32,384]{3,2,1,0:T(8,128)(2,1)S(1)}, bf16[1,8,32,384]{3,2,1,0:T(8,128)(2,1)S(1)}, u32[]{:S(2)}, u32[]{:S(2)}) collective-permute-start(bf16[1,8,32,384]{3,2,1,0:T(8,128)(2,1)S(1)} %fusion.50), channel_id=1, source_target_pairs={{0,16},{16,0},{1,17},{17,1},{2,18},{18,2},{3,19},{19,3},{4,20},{20... | collective-permute-start | bytes 589832 | tf_op jit(solution)/shard_map/ppermute | solution.py:42
  445.4 26.3 %collective-permute-start.68 = (bf16[32,1024]{1,0:T(8,128)(2,1)S(1)}, bf16[32,1024]{1,0:T(8,128)(2,1)S(1)}, u32[]{:S(2)}, u32[]{:S(2)}) collective-permute-start(bf16[32,1024]{1,0:T(8,128)(2,1)S(1)} %get-tuple-element.128), channel_id=1, source_target_pairs={{0,4},{4,8},{8,12},{12,14},{14,10},{10,6},{6,2},{2,0},{1,5},{5,9},... | collective-permute-start | bytes 196616 | tf_op jit(solution)/shard_map/ppermute | solution.py:47
  445.5 26.4 %collective-permute-start.73 = (bf16[32,1024]{1,0:T(8,128)(2,1)S(1)}, bf16[32,1024]{1,0:T(8,128)(2,1)S(1)}, u32[]{:S(2)}, u32[]{:S(2)}) collective-permute-start(bf16[32,1024]{1,0:T(8,128)(2,1)S(1)} %get-tuple-element.129), channel_id=1, source_target_pairs={{0,6},{4,2},{8,0},{12,4},{14,8},{10,12},{6,14},{2,10},{1,7},{5,3},... | collective-permute-start | bytes 196616 | tf_op jit(solution)/shard_map/ppermute | solution.py:47
  449.7 23.7 %collective-permute-start.72 = (bf16[32,1024]{1,0:T(8,128)(2,1)S(1)}, bf16[32,1024]{1,0:T(8,128)(2,1)S(1)}, u32[]{:S(2)}, u32[]{:S(2)}) collective-permute-start(bf16[32,1024]{1,0:T(8,128)(2,1)S(1)} %get-tuple-element.130), channel_id=1, source_target_pairs={{0,10},{4,6},{8,2},{12,0},{14,4},{10,8},{6,12},{2,14},{1,11},{5,7}... | collective-permute-start | bytes 196616 | tf_op jit(solution)/shard_map/ppermute | solution.py:47
  454.9 20.5 %collective-permute-start.71 = (bf16[32,1024]{1,0:T(8,128)(2,1)S(1)}, bf16[32,1024]{1,0:T(8,128)(2,1)S(1)}, u32[]{:S(2)}, u32[]{:S(2)}) collective-permute-start(bf16[32,1024]{1,0:T(8,128)(2,1)S(1)} %get-tuple-element.131), channel_id=1, source_target_pairs={{0,14},{4,10},{8,6},{12,2},{14,0},{10,4},{6,8},{2,12},{1,15},{5,11... | collective-permute-start | bytes 196616 | tf_op jit(solution)/shard_map/ppermute | solution.py:47
  458.6 19.6 %collective-permute-start.70 = (bf16[32,1024]{1,0:T(8,128)(2,1)S(1)}, bf16[32,1024]{1,0:T(8,128)(2,1)S(1)}, u32[]{:S(2)}, u32[]{:S(2)}) collective-permute-start(bf16[32,1024]{1,0:T(8,128)(2,1)S(1)} %get-tuple-element.132), channel_id=1, source_target_pairs={{0,12},{4,14},{8,10},{12,6},{14,2},{10,0},{6,4},{2,8},{1,13},{5,15... | collective-permute-start | bytes 196616 | tf_op jit(solution)/shard_map/ppermute | solution.py:47
  471.8 7.5 %collective-permute-start.69 = (bf16[32,1024]{1,0:T(8,128)(2,1)S(1)}, bf16[32,1024]{1,0:T(8,128)(2,1)S(1)}, u32[]{:S(2)}, u32[]{:S(2)}) collective-permute-start(bf16[32,1024]{1,0:T(8,128)(2,1)S(1)} %get-tuple-element.133), channel_id=1, source_target_pairs={{0,8},{4,12},{8,14},{12,10},{14,6},{10,2},{6,0},{2,4},{1,9},{5,13}... | collective-permute-start | bytes 196616 | tf_op jit(solution)/shard_map/ppermute | solution.py:47
  471.9 7.4 %collective-permute-start.74 = (bf16[32,1024]{1,0:T(8,128)(2,1)S(1)}, bf16[32,1024]{1,0:T(8,128)(2,1)S(1)}, u32[]{:S(2)}, u32[]{:S(2)}) collective-permute-start(bf16[32,1024]{1,0:T(8,128)(2,1)S(1)} %get-tuple-element.134), channel_id=1, source_target_pairs={{0,2},{4,0},{8,4},{12,8},{14,12},{10,14},{6,10},{2,6},{1,3},{5,1},... | collective-permute-start | bytes 196616 | tf_op jit(solution)/shard_map/ppermute | solution.py:47
  473.4 50.4 %collective-permute-start.54 = (bf16[256,1024]{1,0:T(8,128)(2,1)S(1)}, bf16[256,1024]{1,0:T(8,128)(2,1)S(1)}, u32[]{:S(2)}, u32[]{:S(2)}) collective-permute-start(bf16[256,1024]{1,0:T(8,128)(2,1)S(1)} %get-tuple-element.123), channel_id=1, source_target_pairs={{0,2},{4,0},{8,4},{12,8},{14,12},{10,14},{6,10},{2,6},{1,3},{5,1},... | collective-permute-start | bytes 1572872 | tf_op jit(solution)/shard_map/ppermute | solution.py:47
  475.4 48.4 %collective-permute-start.51 = (bf16[256,1024]{1,0:T(8,128)(2,1)S(1)}, bf16[256,1024]{1,0:T(8,128)(2,1)S(1)}, u32[]{:S(2)}, u32[]{:S(2)}) collective-permute-start(bf16[256,1024]{1,0:T(8,128)(2,1)S(1)} %fusion.26), channel_id=1, source_target_pairs={{0,4},{4,8},{8,12},{12,14},{14,10},{10,6},{6,2},{2,0},{1,5},{5,9},... | collective-permute-start | bytes 1572872 | tf_op jit(solution)/shard_map/ppermute | solution.py:47
  478.3 21.4 %collective-permute-start.59 = (bf16[32,384]{1,0:T(8,128)(2,1)S(1)}, bf16[32,384]{1,0:T(8,128)(2,1)S(1)}, u32[]{:S(2)}, u32[]{:S(2)}) collective-permute-start(bf16[32,384]{1,0:T(8,128)(2,1)S(1)} %get-tuple-element.181), channel_id=1, source_target_pairs={{0,4},{4,8},{8,12},{12,14},{14,10},{10,6},{6,2},{2,0},{1,5},{5,9},... | collective-permute-start | bytes 73736 | tf_op jit(solution)/shard_map/ppermute | solution.py:47
  480.0 43.5 %collective-permute-start.65 = (bf16[32,384]{1,0:T(8,128)(2,1)S(1)}, bf16[32,384]{1,0:T(8,128)(2,1)S(1)}, u32[]{:S(2)}, u32[]{:S(2)}) collective-permute-start(bf16[32,384]{1,0:T(8,128)(2,1)S(1)} %get-tuple-element.175), channel_id=1, source_target_pairs={{0,2},{4,0},{8,4},{12,8},{14,12},{10,14},{6,10},{2,6},{1,3},{5,1},... | collective-permute-start | bytes 73736 | tf_op jit(solution)/shard_map/ppermute | solution.py:47
  484.0 39.5 %collective-permute-start.64 = (bf16[32,384]{1,0:T(8,128)(2,1)S(1)}, bf16[32,384]{1,0:T(8,128)(2,1)S(1)}, u32[]{:S(2)}, u32[]{:S(2)}) collective-permute-start(bf16[32,384]{1,0:T(8,128)(2,1)S(1)} %get-tuple-element.176), channel_id=1, source_target_pairs={{0,6},{4,2},{8,0},{12,4},{14,8},{10,12},{6,14},{2,10},{1,7},{5,3},... | collective-permute-start | bytes 73736 | tf_op jit(solution)/shard_map/ppermute | solution.py:47
  510.0 7.0 %collective-permute-start.62 = (bf16[32,384]{1,0:T(8,128)(2,1)S(1)}, bf16[32,384]{1,0:T(8,128)(2,1)S(1)}, u32[]{:S(2)}, u32[]{:S(2)}) collective-permute-start(bf16[32,384]{1,0:T(8,128)(2,1)S(1)} %get-tuple-element.178), channel_id=1, source_target_pairs={{0,14},{4,10},{8,6},{12,2},{14,0},{10,4},{6,8},{2,12},{1,15},{5,11... | collective-permute-start | bytes 73736 | tf_op jit(solution)/shard_map/ppermute | solution.py:47
  525.6 16.9 %collective-permute-start.52 = (bf16[256,1024]{1,0:T(8,128)(2,1)S(1)}, bf16[256,1024]{1,0:T(8,128)(2,1)S(1)}, u32[]{:S(2)}, u32[]{:S(2)}) collective-permute-start(bf16[256,1024]{1,0:T(8,128)(2,1)S(1)} %get-tuple-element.120), channel_id=1, source_target_pairs={{0,4},{4,8},{8,12},{12,14},{14,10},{10,6},{6,2},{2,0},{1,5},{5,9},... | collective-permute-start | bytes 1572872 | tf_op jit(solution)/shard_map/ppermute | solution.py:47
  525.7 19.5 %collective-permute-start.55 = (bf16[256,1024]{1,0:T(8,128)(2,1)S(1)}, bf16[256,1024]{1,0:T(8,128)(2,1)S(1)}, u32[]{:S(2)}, u32[]{:S(2)}) collective-permute-start(bf16[256,1024]{1,0:T(8,128)(2,1)S(1)} %get-tuple-element.121), channel_id=1, source_target_pairs={{0,2},{4,0},{8,4},{12,8},{14,12},{10,14},{6,10},{2,6},{1,3},{5,1},... | collective-permute-start | bytes 1572872 | tf_op jit(solution)/shard_map/ppermute | solution.py:47
  545.6 12.7 %collective-permute-start.53 = (bf16[256,1024]{1,0:T(8,128)(2,1)S(1)}, bf16[256,1024]{1,0:T(8,128)(2,1)S(1)}, u32[]{:S(2)}, u32[]{:S(2)}) collective-permute-start(bf16[256,1024]{1,0:T(8,128)(2,1)S(1)} %get-tuple-element.118), channel_id=1, source_target_pairs={{0,4},{4,8},{8,12},{12,14},{14,10},{10,6},{6,2},{2,0},{1,5},{5,9},... | collective-permute-start | bytes 1572872 | tf_op jit(solution)/shard_map/ppermute | solution.py:47
  547.1 12.3 %collective-permute-start.56 = (bf16[256,1024]{1,0:T(8,128)(2,1)S(1)}, bf16[256,1024]{1,0:T(8,128)(2,1)S(1)}, u32[]{:S(2)}, u32[]{:S(2)}) collective-permute-start(bf16[256,1024]{1,0:T(8,128)(2,1)S(1)} %get-tuple-element.119), channel_id=1, source_target_pairs={{0,2},{4,0},{8,4},{12,8},{14,12},{10,14},{6,10},{2,6},{1,3},{5,1},... | collective-permute-start | bytes 1572872 | tf_op jit(solution)/shard_map/ppermute | solution.py:47
  (71 other events, 545.9 us)
Sparse Core Ops, SparseCore 0:
  21.7 117.6 all-gather.2
  409.7 131.8 reduce-scatter.1

commit v2 on v1

v2 whole, which is shorter than its diff:
```python
import functools
import math

import jax
import jax.numpy as jnp
from jax import lax
from jax.experimental import pallas as pl
from jax.experimental.pallas import tpu as pltpu
from jax.sharding import Mesh
from jax.sharding import PartitionSpec as P

D = 1024
FF = 2816
HEADS = 8
HEAD_DIM = 128
QUERY_BLOCK = 128
MEM_ROWS = 256
EPSILON = 1e-05
NEGATIVE = -1e30
SCALE = 1.0 / math.sqrt(HEAD_DIM)
LOG2 = SCALE * math.log2(math.e)
LOW = jnp.bfloat16
WIDE = jnp.float32

RING = [2 * i for i in range(HEADS // 2)] + [2 * i + 1 for i in reversed(range(HEADS // 2))]


def dot_nn(a, b):
    return lax.dot_general(a, b, (((1,), (0,)), ((), ())), preferred_element_type=WIDE)


def dot_nt(a, b):
    return lax.dot_general(a, b, (((1,), (1,)), ((), ())), preferred_element_type=WIDE)


def dot_tn(a, b):
    return lax.dot_general(a, b, (((0,), (0,)), ((), ())), preferred_element_type=WIDE)


def swap(block, axis):
    return lax.ppermute(block, axis, [(0, 1), (1, 0)])


def turn(block, distance):
    route = [(RING[i], RING[(i + distance) % HEADS]) for i in range(HEADS)]
    return lax.ppermute(block, "h", route)


def at_place(place):
    place = lax.rem(place + 2 * HEADS, HEADS)
    return jnp.where(place < HEADS // 2, 2 * place, 2 * (HEADS - 1 - place) + 1)


def exchange(blocks):
    return lax.all_to_all(blocks, "h", 0, 0)


def pick(flag, first, second):
    return jnp.where(flag == 0, first, second)


def vmem():
    return pl.BlockSpec(memory_space=pltpu.VMEM)


def qkv_kernel(parts, tab, *refs):
    xs, (gain_ref, w_ref, cos_ref, sin_ref) = refs[: sum(parts)], refs[sum(parts) : sum(parts) + 4]
    q_ref, kv_ref, n_ref, x_ref = refs[-4:]
    i = pl.program_id(0)
    first = 0
    for step, number in enumerate(parts):

        @pl.when(i == step)
        def _(blocks=xs[first : first + number]):
            row = 0
            for block in blocks:
                x_ref[row : row + block.shape[0], :] = block[...]
                row += block.shape[0]

        first += number
    x = x_ref[...].astype(WIDE)
    r = lax.rsqrt(jnp.mean(x * x, axis=-1, keepdims=True) + EPSILON)
    normed = (x * r * gain_ref[...].astype(WIDE)).astype(LOW)
    n_ref[0] = normed
    out = dot_nn(normed, w_ref[...])
    c, s = cos_ref[0], sin_ref[0]

    def rot(v):
        return v * c + pltpu.roll(v, HEAD_DIM // 2, 1) * s

    q_ref[0] = rot(out[:, :HEAD_DIM]).astype(LOW)
    kv_ref[0, 0] = rot(out[:, HEAD_DIM : 2 * HEAD_DIM]).astype(LOW)
    kv_ref[1, 0] = out[:, 2 * HEAD_DIM :].astype(LOW)


def qkv_blocks(chips, xs, gain, w, cos, sin, held):
    count = cos.shape[1]
    flat = [piece for block in xs for piece in block]

    def whole(shape):
        return pl.BlockSpec(shape, lambda i, t: (0, 0))

    def block(*shape):
        return pl.BlockSpec((1, *shape), lambda i, t: (t[i], 0, 0))

    spec = pltpu.PrefetchScalarGridSpec(
        num_scalar_prefetch=1,
        grid=(len(xs),),
        in_specs=[whole(piece.shape) for piece in flat]
        + [whole((1, D)), whole((D, 3 * HEAD_DIM)), block(count, HEAD_DIM), block(count, HEAD_DIM)]
        + [pl.BlockSpec(memory_space=pl.ANY)] * len(held),
        out_specs=[
            block(count, HEAD_DIM),
            pl.BlockSpec((2, 1, count, HEAD_DIM), lambda i, t: (0, t[i], 0, 0)),
            block(count, D),
        ],
        scratch_shapes=[pltpu.VMEM((count, D), LOW)],
    )
    return pl.pallas_call(
        functools.partial(qkv_kernel, [len(block) for block in xs]),
        grid_spec=spec,
        out_shape=[
            jax.ShapeDtypeStruct((HEADS, count, HEAD_DIM), LOW),
            jax.ShapeDtypeStruct((2, HEADS, count, HEAD_DIM), LOW),
            jax.ShapeDtypeStruct((HEADS, count, D), LOW),
        ],
        input_output_aliases={len(flat) + 5 + i: i for i in range(len(held))},
        cost_estimate=pl.CostEstimate(
            flops=2 * len(xs) * count * D * 3 * HEAD_DIM,
            bytes_accessed=5 * len(xs) * count * D,
            transcendentals=0,
        ),
        name=f"qkv{len(xs)}",
    )(chips, *flat, gain, w, cos, sin, *held)


def causal(count):
    rows = lax.broadcasted_iota(jnp.int32, (count, count), 0)
    return lax.broadcasted_iota(jnp.int32, (count, count), 1) <= rows


def attend_kernel(
    tab, q_ref, own_ref, oth_ref, segq_ref, sego_ref, segt_ref, idx_ref, ck_ref, cv_ref,
    o_ref, low_ref, lse_ref, mem_ref,
):
    i = pl.program_id(0)
    parity = tab[40]
    count = q_ref.shape[1]
    q = q_ref[0]
    segq = segq_ref[0]

    s1 = dot_nt(q, own_ref[0, i]) * LOG2
    s2 = dot_nt(q, oth_ref[0, i]) * LOG2
    s1 = jnp.where((sego_ref[i] == segq) & causal(count), s1, NEGATIVE)
    s2 = jnp.where(segt_ref[i] == segq + 64 * (1 - parity), s2, NEGATIVE)
    memory = []
    for b in range(count // QUERY_BLOCK):
        rows = slice(b * QUERY_BLOCK, (b + 1) * QUERY_BLOCK)
        doc = tab[2 * i + b]
        mate = tab[16 + 2 * i + b]
        idx = idx_ref[0, rows, :]
        lane = lax.broadcasted_iota(jnp.int32, (QUERY_BLOCK, MEM_ROWS), 1)
        first = jnp.where(idx == lane, 1.0, 0.0).astype(LOW)
        second = jnp.where(idx == lane + MEM_ROWS, 1.0, 0.0).astype(LOW)
        here = pl.ds(pl.multiple_of(doc * MEM_ROWS, MEM_ROWS), MEM_ROWS)
        there = pl.ds(pl.multiple_of(mate * MEM_ROWS, MEM_ROWS), MEM_ROWS)
        mk = (dot_nn(first, ck_ref[here, :]) + dot_nn(second, ck_ref[there, :])).astype(LOW)
        mv = (dot_nn(first, cv_ref[here, :]) + dot_nn(second, cv_ref[there, :])).astype(LOW)
        mem_ref[0, 0, rows, :] = mk
        mem_ref[1, 0, rows, :] = mv
        s = jnp.where(segq[rows] == doc, dot_nt(q[rows], mk) * LOG2, NEGATIVE)
        memory.append((s, mv))
    sm = jnp.concatenate([s for s, _ in memory], axis=0)
    top = jnp.maximum(
        jnp.max(jnp.maximum(s1, s2), axis=-1, keepdims=True), jnp.max(sm, axis=-1, keepdims=True)
    )
    p1 = jnp.exp2(s1 - top)
    p2 = jnp.exp2(s2 - top)
    pm = jnp.exp2(sm - top)
    total = jnp.sum(p1 + p2, axis=-1, keepdims=True) + jnp.sum(pm, axis=-1, keepdims=True)
    pm = pm.astype(LOW)
    acc = jnp.concatenate(
        [
            dot_nn(pm[b * QUERY_BLOCK : (b + 1) * QUERY_BLOCK], mv)
            for b, (_, mv) in enumerate(memory)
        ],
        axis=0,
    )
    acc = acc + dot_nn(p1.astype(LOW), own_ref[1, i]) + dot_nn(p2.astype(LOW), oth_ref[1, i])

    def body(j, state):
        top, total, acc = state
        s1 = dot_nt(q, own_ref[0, j]) * LOG2
        s2 = dot_nt(q, oth_ref[0, j]) * LOG2
        s1 = jnp.where(sego_ref[j] == segq, s1, NEGATIVE)
        s2 = jnp.where(segt_ref[j] == segq, s2, NEGATIVE)
        fresh = jnp.maximum(top, jnp.max(jnp.maximum(s1, s2), axis=-1, keepdims=True))
        p1 = jnp.exp2(s1 - fresh)
        p2 = jnp.exp2(s2 - fresh)
        decay = jnp.exp2(top - fresh)
        total = total * decay + jnp.sum(p1 + p2, axis=-1, keepdims=True)
        acc = (
            acc * decay
            + dot_nn(p1.astype(LOW), own_ref[1, j])
            + dot_nn(p2.astype(LOW), oth_ref[1, j])
        )
        return fresh, total, acc

    top, total, acc = lax.fori_loop(tab[32 + i], i, body, (top, total, acc))
    out = acc / total
    o_ref[0] = out
    low_ref[0] = out.astype(LOW)
    lse_ref[0] = top + jnp.log2(total)


def attend(tab, q, own, oth, segq, sego, segt, idx, ck, cv):
    count = q.shape[1]
    block = pl.BlockSpec((1, count, HEAD_DIM), lambda i, t: (i, 0, 0))
    thin = pl.BlockSpec((1, count, 1), lambda i, t: (i, 0, 0))
    whole = pl.BlockSpec((2, HEADS, count, HEAD_DIM), lambda i, t: (0, 0, 0, 0))
    segs = pl.BlockSpec((HEADS, 1, count), lambda i, t: (0, 0, 0))
    cache = pl.BlockSpec((ck.shape[0], HEAD_DIM), lambda i, t: (0, t[41]))
    mem = pl.BlockSpec((2, 1, count, HEAD_DIM), lambda i, t: (0, i, 0, 0))
    return pl.pallas_call(
        attend_kernel,
        grid_spec=pltpu.PrefetchScalarGridSpec(
            num_scalar_prefetch=1,
            grid=(HEADS,),
            in_specs=[block, whole, whole, thin, segs, segs, thin, cache, cache],
            out_specs=[block, block, thin, mem],
        ),
        out_shape=[
            jax.ShapeDtypeStruct((HEADS, count, HEAD_DIM), WIDE),
            jax.ShapeDtypeStruct((HEADS, count, HEAD_DIM), LOW),
            jax.ShapeDtypeStruct((HEADS, count, 1), WIDE),
            jax.ShapeDtypeStruct((2, HEADS, count, HEAD_DIM), LOW),
        ],
        cost_estimate=pl.CostEstimate(
            flops=25 * 10**9, bytes_accessed=6 * 2**20, transcendentals=3 * 10**6
        ),
        name="attend",
    )(tab, q, own, oth, segq, sego, segt, idx, ck, cv)


def attend_back_kernel(
    tab, q_ref, up_ref, o_ref, lse_ref, own_ref, oth_ref, mem_ref, segq_ref, sego_ref, segt_ref,
    dq_ref, down_ref, doth_ref, sum_ref,
):
    i = pl.program_id(0)

    @pl.when(i == 0)
    def _():
        sum_ref[...] = jnp.zeros_like(sum_ref)

    parity = tab[40]
    count = q_ref.shape[1]
    q = q_ref[0]
    up = up_ref[0]
    lse = lse_ref[0]
    segq = segq_ref[0]
    delta = jnp.sum(up.astype(WIDE) * o_ref[0], axis=-1, keepdims=True)
    partial = []
    for b in range(count // QUERY_BLOCK):
        rows = slice(b * QUERY_BLOCK, (b + 1) * QUERY_BLOCK)
        mk = mem_ref[0, 0, rows, :]
        mv = mem_ref[1, 0, rows, :]
        ok = segq[rows] == tab[2 * i + b]
        p = jnp.exp2(jnp.where(ok, dot_nt(q[rows], mk) * LOG2 - lse[rows], NEGATIVE))
        ds = (p * (dot_nt(up[rows], mv) - delta[rows])).astype(LOW)
        partial.append(dot_nn(ds, mk))

    def tile(side, ref, j, ok, dq):
        k = ref[0, j]
        v = ref[1, j]
        p = jnp.exp2(jnp.where(ok, dot_nt(q, k) * LOG2 - lse, NEGATIVE))
        ds = (p * (dot_nt(up, v) - delta)).astype(LOW)
        sum_ref[side, 0, j] += dot_tn(ds, q)
        sum_ref[side, 1, j] += dot_tn(p.astype(LOW), up)
        return dq + dot_nn(ds, k)

    dq = jnp.concatenate(partial, axis=0)
    dq = tile(0, own_ref, i, (sego_ref[i] == segq) & causal(count), dq)
    dq = tile(1, oth_ref, i, segt_ref[i] == segq + 64 * (1 - parity), dq)

    def body(j, dq):
        dq = tile(0, own_ref, j, sego_ref[j] == segq, dq)
        return tile(1, oth_ref, j, segt_ref[j] == segq, dq)

    dq_ref[0] = lax.fori_loop(tab[32 + i], i, body, dq)

    @pl.when(i == HEADS - 1)
    def _():
        down_ref[...] = sum_ref[0]
        doth_ref[...] = sum_ref[1].astype(LOW)


def attend_back(tab, q, up, o, lse, own, oth, mem, segq, sego, segt):
    count = q.shape[1]
    block = pl.BlockSpec((1, count, HEAD_DIM), lambda i, t: (i, 0, 0))
    thin = pl.BlockSpec((1, count, 1), lambda i, t: (i, 0, 0))
    whole = pl.BlockSpec((2, HEADS, count, HEAD_DIM), lambda i, t: (0, 0, 0, 0))
    segs = pl.BlockSpec((HEADS, 1, count), lambda i, t: (0, 0, 0))
    memory = pl.BlockSpec((2, 1, count, HEAD_DIM), lambda i, t: (0, i, 0, 0))
    return pl.pallas_call(
        attend_back_kernel,
        grid_spec=pltpu.PrefetchScalarGridSpec(
            num_scalar_prefetch=1,
            grid=(HEADS,),
            in_specs=[block, block, block, thin, whole, whole, memory, thin, segs, segs],
            out_specs=[block, whole, whole],
            scratch_shapes=[pltpu.VMEM((2, 2, HEADS, count, HEAD_DIM), WIDE)],
        ),
        out_shape=[
            jax.ShapeDtypeStruct((HEADS, count, HEAD_DIM), WIDE),
            jax.ShapeDtypeStruct((2, HEADS, count, HEAD_DIM), WIDE),
            jax.ShapeDtypeStruct((2, HEADS, count, HEAD_DIM), LOW),
        ],
        cost_estimate=pl.CostEstimate(
            flops=30 * 10**9, bytes_accessed=10 * 2**20, transcendentals=3 * 10**6
        ),
        name="attend_back",
    )(tab, q, up, o, lse, own, oth, mem, segq, sego, segt)


def out_kernel(heads_ref, w_ref, x_ref, gain_ref, att_ref, mid_ref, n_ref):
    for h in range(HEADS):
        att_ref[:, h * HEAD_DIM : (h + 1) * HEAD_DIM] = heads_ref[h]
    mid = x_ref[...].astype(WIDE) + dot_nn(att_ref[...], w_ref[...])
    mid_ref[...] = mid
    r = lax.rsqrt(jnp.mean(mid * mid, axis=-1, keepdims=True) + EPSILON)
    n_ref[...] = (mid * r * gain_ref[...].astype(WIDE)).astype(LOW)


def out_block(heads, w, x, gain):
    count = x.shape[0]
    return pl.pallas_call(
        out_kernel,
        in_specs=[vmem()] * 4,
        out_specs=[vmem()] * 3,
        out_shape=[
            jax.ShapeDtypeStruct((count, D), LOW),
            jax.ShapeDtypeStruct((count, D), WIDE),
            jax.ShapeDtypeStruct((count, D), LOW),
        ],
        cost_estimate=pl.CostEstimate(
            flops=2 * count * D * D, bytes_accessed=4 * 2**20, transcendentals=0
        ),
        name="out_block",
    )(heads, w, x, gain)


def ffn_kernel(na, nb, ga, gb, g_ref, u_ref, d_ref, hid_ref, gg_ref, ug_ref, dn_ref):
    for t, (n_ref, c_ref) in enumerate(((na, ga), (nb, gb))):
        n = n_ref[...]
        gate = dot_nn(n, g_ref[...])
        upper = dot_nn(n, u_ref[...])
        sigma = jax.nn.sigmoid(gate)
        silu = gate * sigma
        hid_ref[t] = (silu * upper).astype(LOW)
        hg = dot_nt(c_ref[...], d_ref[...])
        gg = (hg * upper * sigma * (1.0 + gate * (1.0 - sigma))).astype(LOW)
        ug = (hg * silu).astype(LOW)
        gg_ref[t] = gg
        ug_ref[t] = ug
        dn_ref[t] = (dot_nt(gg, g_ref[...]) + dot_nt(ug, u_ref[...])).astype(LOW)


def ffn(na, nb, ga, gb, g, u, d):
    count = na.shape[0]
    units = g.shape[1]
    return pl.pallas_call(
        ffn_kernel,
        in_specs=[vmem()] * 7,
        out_specs=[vmem()] * 4,
        out_shape=[jax.ShapeDtypeStruct((2, count, units), LOW)] * 3
        + [jax.ShapeDtypeStruct((2, count, D), LOW)],
        cost_estimate=pl.CostEstimate(
            flops=20 * count * D * units,
            bytes_accessed=6 * D * units + 16 * count * D,
            transcendentals=2 * count * units,
        ),
        name="ffn",
    )(na, nb, ga, gb, g, u, d)


def mid_kernel(mid_ref, pa, pb, pc, up_ref, gain_ref, w_ref, mg_ref, bg_ref, ag_ref):
    mid = mid_ref[...]
    scaled = (pa[...].astype(WIDE) + pb[...].astype(WIDE) + pc[...].astype(WIDE)) * gain_ref[
        ...
    ].astype(WIDE)
    r = lax.rsqrt(jnp.mean(mid * mid, axis=-1, keepdims=True) + EPSILON)
    inner = jnp.mean(scaled * mid, axis=-1, keepdims=True)
    mid_grad = up_ref[...].astype(WIDE) + r * scaled - mid * (r * r * r * inner)
    mg_ref[...] = mid_grad
    branch = mid_grad.astype(LOW)
    bg_ref[...] = branch
    att = dot_nt(branch, w_ref[...]).astype(LOW)
    for h in range(HEADS):
        ag_ref[h] = att[:, h * HEAD_DIM : (h + 1) * HEAD_DIM]


def mid_block(mid, pa, pb, pc, up, gain, w):
    count = mid.shape[0]
    return pl.pallas_call(
        mid_kernel,
        in_specs=[vmem()] * 7,
        out_specs=[vmem()] * 3,
        out_shape=[
            jax.ShapeDtypeStruct((count, D), WIDE),
            jax.ShapeDtypeStruct((count, D), LOW),
            jax.ShapeDtypeStruct((HEADS, count, HEAD_DIM), LOW),
        ],
        cost_estimate=pl.CostEstimate(
            flops=2 * count * D * D, bytes_accessed=6 * 2**20, transcendentals=0
        ),
        name="mid_block",
    )(mid, pa, pb, pc, up, gain, w)


def qkv_back_kernel(tab, dq_ref, own_ref, got_ref, cos_ref, sin_ref, w_ref, dx_ref, g_ref):
    c, s = cos_ref[0], sin_ref[0]

    def rot(v):
        return v * c - pltpu.roll(v, HEAD_DIM // 2, 1) * s

    dq = rot(dq_ref[0] * SCALE).astype(LOW)
    dk = rot((own_ref[0, 0] + got_ref[0, 0].astype(WIDE)) * SCALE).astype(LOW)
    dv = (own_ref[1, 0] + got_ref[1, 0].astype(WIDE)).astype(LOW)
    grads = jnp.concatenate([dq, dk, dv], axis=1)
    g_ref[0] = grads
    dx_ref[0] = dot_nt(grads, w_ref[...]).astype(LOW)


def qkv_back(chips, dq, own, got, cos, sin, w):
    count = dq.shape[1]
    block = pl.BlockSpec((1, count, HEAD_DIM), lambda i, t: (t[i], 0, 0))
    pair = pl.BlockSpec((2, 1, count, HEAD_DIM), lambda i, t: (0, t[i], 0, 0))
    return pl.pallas_call(
        qkv_back_kernel,
        grid_spec=pltpu.PrefetchScalarGridSpec(
            num_scalar_prefetch=1,
            grid=(HEADS,),
            in_specs=[
                block, pair, pair, block, block,
                pl.BlockSpec((D, 3 * HEAD_DIM), lambda i, t: (0, 0)),
            ],
            out_specs=[
                pl.BlockSpec((1, count, D), lambda i, t: (i, 0, 0)),
                pl.BlockSpec((1, count, 3 * HEAD_DIM), lambda i, t: (t[i], 0, 0)),
            ],
        ),
        out_shape=[
            jax.ShapeDtypeStruct((HEADS, count, D), LOW),
            jax.ShapeDtypeStruct((HEADS, count, 3 * HEAD_DIM), LOW),
        ],
        cost_estimate=pl.CostEstimate(
            flops=2 * HEADS * count * D * 3 * HEAD_DIM,
            bytes_accessed=4 * HEADS * count * D,
            transcendentals=0,
        ),
        name="qkv_back",
    )(chips, dq, own, got, cos, sin, w)


def local(
    far,
    tokens,
    segment_ids,
    second_doc,
    memory_index,
    cache_keys,
    cache_values,
    first_gain,
    query_weight,
    key_weight,
    value_weight,
    out_weight,
    second_gain,
    gate_weight,
    up_weight,
    down_weight,
    cotangent,
):
    x = tokens[0]
    upstream = cotangent[0]
    count = x.shape[0]
    blocks = count // QUERY_BLOCK
    rows = query_weight.shape[0]
    share = down_weight.shape[0]
    units = far * HEADS * share
    chip, core, pair = lax.axis_index("h"), lax.axis_index("c"), lax.axis_index("dl")
    mine = jnp.where(chip % 2 == 0, chip // 2, HEADS - 1 - chip // 2)
    slots = jnp.arange(HEADS, dtype=jnp.int32)
    chips = at_place(mine - slots)
    group = ("dh", "h") if far > 1 else "h"

    def by_head(w):
        return w.reshape(rows, HEADS, HEAD_DIM).transpose(1, 0, 2)

    picked = memory_index[0].transpose(1, 0, 2)
    seg_rows = jnp.broadcast_to(
        segment_ids[0].astype(LOW).reshape(1, blocks, QUERY_BLOCK), (HEADS, blocks, QUERY_BLOCK)
    )
    gains = jnp.concatenate([first_gain, second_gain])
    gain_rows = jnp.broadcast_to(
        jnp.pad(gains, (0, HEAD_DIM - 2 * rows)).reshape(1, 1, HEAD_DIM), (HEADS, 1, HEAD_DIM)
    )
    pack = jnp.concatenate(
        [
            by_head(query_weight),
            by_head(key_weight),
            by_head(value_weight),
            seg_rows,
            (picked // MEM_ROWS).astype(LOW),
            (picked % MEM_ROWS).astype(LOW),
            gain_rows,
        ],
        axis=1,
    )
    height = pack.shape[1]
    pack = jnp.pad(pack, ((0, 0), (0, -height % 16), (0, 0)))

    forth, back = [x, turn(x, 1)], [x, turn(x, -1)]
    pack, forth[1], back[1] = lax.optimization_barrier((pack, forth[1], back[1]))
    got = exchange(pack)
    for step in range(HEADS // 2 - 2):
        forth.append(turn(forth[-1], 1))
        back.append(turn(back[-1], -1))
    got, forth[-1], back[-1] = lax.optimization_barrier((got, forth[-1], back[-1]))
    split = count // 2
    far_first, far_last = turn(forth[-1][:split], 1), turn(back[-1][split:], -1)
    x_slots = [(v,) for v in forth] + [(far_first, far_last)] + [(v,) for v in back[:0:-1]]
    got_c = swap(got, "c")
    got_y = swap(got, "dl")
    got_yc = swap(got_y, "c")
    near = pick(core, jnp.stack([got, got_c]), jnp.stack([got_c, got]))
    away = pick(core, jnp.stack([got_y, got_yc]), jnp.stack([got_yc, got_y]))
    every = pick(pair, jnp.stack([near, away]), jnp.stack([away, near]))
    every = every.transpose(2, 0, 1, 3, 4)
    if far > 1:
        every = lax.all_gather(every, "dh", axis=0)
    else:
        every = every[None]
    every = every.transpose(0, 2, 1, 3, 4, 5)
    w_qkv = jnp.concatenate(
        [every[..., i * rows : (i + 1) * rows, :].reshape(D, HEAD_DIM) for i in range(3)], axis=1
    )
    gain_all = every[..., 3 * rows + 3 * blocks, : 2 * rows].reshape(-1, 2, rows)
    gain_one = gain_all[:, 0].reshape(1, D)
    gain_two = gain_all[:, 1].reshape(1, D)

    def seg_of(blocks_of):
        return (
            blocks_of[:, 3 * rows : 3 * rows + blocks]
            .astype(WIDE)
            .astype(jnp.int32)
            .reshape(HEADS, count)
        )

    seg_own = seg_of(got)
    seg_oth = seg_of(got_c)
    idx = (
        got[:, 3 * rows + blocks : 3 * rows + 2 * blocks].astype(WIDE) * MEM_ROWS
        + got[:, 3 * rows + 2 * blocks : 3 * rows + 3 * blocks].astype(WIDE)
    ).astype(jnp.int32)
    idx = idx.reshape(HEADS, count, 1)

    block_docs = seg_own[:, ::QUERY_BLOCK]
    docs = second_doc.shape[1]
    doc_ids = jnp.arange(docs, dtype=jnp.int32)
    mates = jnp.sum(
        jnp.where(block_docs[:, :, None] == doc_ids, second_doc[0][None, None, :], 0), axis=-1
    )
    seg_all = jnp.concatenate([seg_own, seg_oth], axis=0)
    before = jnp.sum(
        (seg_all.reshape(1, -1) < block_docs[:, :1]).astype(jnp.int32), axis=1
    )
    tab = jnp.concatenate(
        [
            block_docs.reshape(-1),
            mates.reshape(-1),
            before // (2 * count),
            jnp.stack([core, chip]),
        ]
    ).astype(jnp.int32)

    half = HEAD_DIM // 2
    freqs = 10000.0 ** (-jnp.arange(half, dtype=WIDE) * 2.0 / (2 * half))
    positions = ((2 * slots + core) * count)[:, None] + jnp.arange(count, dtype=jnp.int32)[None]
    turned = positions.astype(WIDE)[:, :, None] * freqs
    cosine, sine = jnp.cos(turned), jnp.sin(turned)
    cosine = jnp.concatenate([cosine, cosine], axis=-1)
    sine = jnp.concatenate([-sine, sine], axis=-1)

    def by_owner(w):
        return w.reshape(rows, far, 2, HEADS, 2, share).transpose(2, 4, 0, 1, 3, 5).reshape(
            2, 2, rows, units
        )

    gu = jnp.concatenate([by_owner(gate_weight), by_owner(up_weight)], axis=-1)
    kept = pick(core, gu[:, 0], gu[:, 1])
    came = swap(pick(core, gu[:, 1], gu[:, 0]), "c")
    gu = pick(core, jnp.stack([kept, came], 1), jnp.stack([came, kept], 1))
    kept = pick(pair, gu[0], gu[1])
    came = swap(pick(pair, gu[1], gu[0]), "dl")
    gu = pick(pair, jnp.stack([kept, came]), jnp.stack([came, kept])).reshape(4 * rows, 2 * units)
    wide = 2 * units
    third = wide - D
    pieces = [out_weight[:, i * third : (i + 1) * third] for i in range(-(-D // third))]
    pieces[-1] = jnp.pad(pieces[-1], ((0, 0), (0, third - pieces[-1].shape[1])))
    pieces = jnp.concatenate(pieces, axis=0)
    deep = max(share, pieces.shape[0])
    lower = jnp.concatenate(
        [
            jnp.pad(down_weight, ((0, deep - share), (0, 0))),
            jnp.pad(pieces, ((0, deep - pieces.shape[0]), (0, 0))),
        ],
        axis=1,
    )
    bundle = jnp.concatenate([gu, lower], axis=0)
    bundle, *_ = lax.optimization_barrier((bundle, *x_slots[3], *x_slots[4], *x_slots[5]))
    gathered = lax.all_gather(bundle, group, axis=0)
    up_c = swap(upstream, "c")
    up_y = swap(upstream, "dl")
    up_yc = swap(up_y, "c")

    held = ()
    for order in ([0, 1, 7, 2, 6], [3, 5, 4]):
        held = qkv_blocks(
            at_place(mine - jnp.asarray(order, jnp.int32)).astype(jnp.int32),
            [x_slots[i] for i in order],
            gain_one,
            w_qkv,
            cosine,
            sine,
            held,
        )
    queries, own, normed_one = held
    other = swap(own, "c")

    seg_thin = seg_own.reshape(HEADS, count, 1)
    seg_own_row = seg_own.reshape(HEADS, 1, count)
    seg_oth_row = seg_oth.reshape(HEADS, 1, count)
    attention, attention_low, lse, memory = attend(
        tab,
        queries,
        own,
        other,
        seg_thin,
        seg_own_row,
        seg_oth_row,
        idx,
        cache_keys[0].reshape(-1, D),
        cache_values[0].reshape(-1, D),
    )

    heads = exchange(attention_low)
    gathered, heads = lax.optimization_barrier((gathered, heads))
    gathered = gathered.reshape(far, HEADS, 4 * rows + deep, wide)
    gu_w = (
        gathered[:, :, : 4 * rows]
        .reshape(far, HEADS, 2, 2 * rows, wide)
        .transpose(0, 2, 1, 3, 4)
        .reshape(D, wide)
    )
    gate_w, up_w = gu_w[:, :units], gu_w[:, units:]
    down_w = gathered[:, :, 4 * rows : 4 * rows + share, :D].reshape(units, D)
    outs = gathered[:, :, 4 * rows :, D:]
    outs = jnp.concatenate(
        [outs[:, :, i * rows : (i + 1) * rows] for i in range(pieces.shape[0] // rows)], axis=-1
    )[..., :D]
    outs_c = swap(outs, "c")
    outs_y = swap(outs, "dl")
    outs_yc = swap(outs_y, "c")
    near = pick(core, jnp.stack([outs, outs_c], 2), jnp.stack([outs_c, outs], 2))
    away = pick(core, jnp.stack([outs_y, outs_yc], 2), jnp.stack([outs_yc, outs_y], 2))
    out_w = pick(pair, jnp.stack([near, away], 1), jnp.stack([away, near], 1)).reshape(D, D)

    attended, mid, normed_two = out_block(heads, out_w, x, gain_two)

    n_c = swap(normed_two, "c")
    n_y = swap(normed_two, "dl")
    n_yc = swap(n_y, "c")
    hid_l, gg_l, ug_l, dn_l = ffn(normed_two, n_c, upstream, up_c, gate_w, up_w, down_w)
    hid_r, gg_r, ug_r, dn_r = ffn(n_y, n_yc, up_y, up_yc, gate_w, up_w, down_w)

    def sum_back(near, away):
        there = (away[0].astype(WIDE) + swap(away[1], "c").astype(WIDE)).astype(LOW)
        return near[0], swap(near[1], "c"), swap(there, "dl")

    parts = sum_back(dn_l, dn_r)
    mid_grad, branch, att_grad = mid_block(
        mid, *parts, upstream, gain_two, out_w
    )

    ups = exchange(att_grad)

    hid_l, gg_l, ug_l, hid_r, gg_r, ug_r, branch = lax.optimization_barrier(
        (hid_l, gg_l, ug_l, hid_r, gg_r, ug_r, branch)
    )

    def over_owner(w):
        w = w.reshape(far, 2, HEADS, 2, rows, D)
        kept = pick(core, w[:, :, :, 0], w[:, :, :, 1])
        came = swap(pick(core, w[:, :, :, 1], w[:, :, :, 0]), "c")
        w = kept.astype(WIDE) + came.astype(WIDE)
        kept = pick(pair, w[:, 0], w[:, 1])
        came = swap(pick(pair, w[:, 1], w[:, 0]).astype(LOW), "dl")
        return (kept + came.astype(WIDE)).astype(LOW).reshape(far * HEADS, rows, D)

    out_part = over_owner(
        jnp.einsum("td,te->de", attended, branch, preferred_element_type=WIDE).astype(LOW)
    )

    def over_tokens(a, b):
        return jnp.einsum("gtd,gtf->df", a, b, preferred_element_type=WIDE)

    n_l, n_r = jnp.stack([normed_two, n_c]), jnp.stack([n_y, n_yc])
    u_l, u_r = jnp.stack([upstream, up_c]), jnp.stack([up_y, up_yc])
    gate_part = (over_tokens(n_l, gg_l) + over_tokens(n_r, gg_r)).astype(LOW)
    up_part = (over_tokens(n_l, ug_l) + over_tokens(n_r, ug_r)).astype(LOW)
    down_part = (over_tokens(hid_l, u_l) + over_tokens(hid_r, u_r)).astype(LOW)

    def by_rows(w):
        return (
            w.reshape(far, 2, HEADS, 2 * rows, units)
            .transpose(0, 2, 1, 3, 4)
            .reshape(far * HEADS, 4 * rows, units)
        )

    strips = [out_part[:, :, i * third : (i + 1) * third] for i in range(-(-D // third))]
    strips[-1] = jnp.pad(strips[-1], ((0, 0), (0, 0), (0, third - strips[-1].shape[-1])))
    strips = jnp.concatenate(strips, axis=1)
    height = 4 * rows + deep
    parts = jnp.concatenate(
        [
            jnp.concatenate([by_rows(gate_part), by_rows(up_part)], axis=-1),
            jnp.concatenate(
                [
                    jnp.pad(
                        down_part.reshape(far * HEADS, share, D), ((0, 0), (0, deep - share), (0, 0))
                    ),
                    jnp.pad(strips, ((0, 0), (0, deep - strips.shape[1]), (0, 0))),
                ],
                axis=2,
            ),
        ],
        axis=1,
    )
    ups, parts = lax.optimization_barrier((ups, parts))
    summed = lax.psum_scatter(
        parts.reshape(far * HEADS * height, wide), group, scatter_dimension=0, tiled=True
    )
    down_w_grad = summed[4 * rows : 4 * rows + share, :D].astype(WIDE)
    out_w_grad = jnp.concatenate(
        [
            summed[4 * rows + i * rows : 4 * rows + (i + 1) * rows, D:]
            for i in range(-(-D // third))
        ],
        axis=1,
    )[:, :D].astype(WIDE)
    gu = summed[: 4 * rows].reshape(2, 2, rows, wide)
    kept = pick(core, gu[:, 0], gu[:, 1])
    came = swap(pick(core, gu[:, 1], gu[:, 0]), "c")
    gu = pick(core, jnp.stack([kept, came], 1), jnp.stack([came, kept], 1))
    kept = pick(pair, gu[0], gu[1])
    came = swap(pick(pair, gu[1], gu[0]), "dl")
    gu = pick(pair, jnp.stack([kept, came]), jnp.stack([came, kept]))
    gu = (
        gu.reshape(2, 2, rows, 2, far, HEADS, share)
        .transpose(3, 2, 4, 0, 5, 1, 6)
        .reshape(2, rows, FF)
        .astype(WIDE)
    )
    gate_w_grad, up_w_grad = gu[0], gu[1]

    out_l = jnp.einsum("gtf,fd->gtd", hid_l, down_w, preferred_element_type=WIDE).astype(LOW)
    out_r = jnp.einsum("gtf,fd->gtd", hid_r, down_w, preferred_element_type=WIDE).astype(LOW)
    output = mid
    for part in sum_back(out_l, out_r):
        output = output + part.astype(WIDE)
    output = output.astype(LOW)

    dq, d_own, d_oth = attend_back(
        tab, queries, ups, attention, lse, own, other, memory, seg_thin, seg_own_row, seg_oth_row
    )
    d_got = swap(d_oth, "c")
    dx, grads = qkv_back(chips.astype(jnp.int32), dq, d_own, d_got, cosine, sine, w_qkv)

    def plus(block, arrived, start):
        size = arrived.shape[0]
        total = block[start : start + size].astype(WIDE) + arrived.astype(WIDE)
        pieces = [block[:start], total.astype(LOW), block[start + size :]]
        return jnp.concatenate([piece for piece in pieces if piece.shape[0]], axis=0)

    middle = dx[HEADS // 2]
    forth, back = middle[:split], middle[split:]
    for step in range(1, HEADS // 2):
        forth = plus(dx[HEADS // 2 + step], turn(forth, 1), 0)
        back = plus(dx[HEADS // 2 - step], turn(back, -1), split if step == 1 else 0)
    forth, back = turn(forth, 1), turn(back, -1)
    normed_one_grad = dx[0].astype(WIDE) + forth.astype(WIDE) + back.astype(WIDE)

    dw = jnp.einsum("std,stg->dg", normed_one, grads, preferred_element_type=WIDE).astype(LOW)
    dw = dw.reshape(far, 2, HEADS, 2, rows, 3 * HEAD_DIM)
    kept = pick(core, dw[:, :, :, 0], dw[:, :, :, 1])
    came = swap(pick(core, dw[:, :, :, 1], dw[:, :, :, 0]), "c")
    dw = kept.astype(WIDE) + came.astype(WIDE)
    kept = pick(pair, dw[:, 0], dw[:, 1])
    came = swap(pick(pair, dw[:, 1], dw[:, 0]).astype(LOW), "dl")
    dw = (kept + came.astype(WIDE)).astype(LOW)
    if far > 1:
        dw = lax.psum_scatter(dw, "dh", scatter_dimension=0, tiled=True)
    qkv_grads = exchange(dw[0]).astype(WIDE)

    wide_x = x.astype(WIDE)
    r = lax.rsqrt(jnp.mean(wide_x * wide_x, axis=-1, keepdims=True) + EPSILON)
    scaled = normed_one_grad * gain_one.astype(WIDE)
    inner = jnp.mean(scaled * wide_x, axis=-1, keepdims=True)
    input_grad = mid_grad + r * scaled - wide_x * (r * r * r * inner)

    q_w_grad, k_w_grad, v_w_grad = (
        qkv_grads[:, :, i * HEAD_DIM : (i + 1) * HEAD_DIM].transpose(1, 0, 2).reshape(rows, D)
        for i in range(3)
    )

    def gain_grad(gain, pairs):
        total = 0.0
        for grad, weight in pairs:
            total = total + jnp.sum(grad * weight.astype(WIDE), axis=1)
        return total / gain.astype(WIDE)

    first_gain_grad = gain_grad(
        first_gain,
        ((q_w_grad, query_weight), (k_w_grad, key_weight), (v_w_grad, value_weight)),
    )
    second_gain_grad = gain_grad(
        second_gain, ((gate_w_grad, gate_weight), (up_w_grad, up_weight))
    )
    return (
        output[None],
        input_grad[None],
        first_gain_grad,
        q_w_grad,
        k_w_grad,
        v_w_grad,
        out_w_grad,
        second_gain_grad,
        gate_w_grad,
        up_w_grad,
        down_w_grad,
    )


def solution(mesh):
    far = mesh.shape["dp"] // 2
    cores = mesh.shape["seq"] // HEADS
    fine = Mesh(mesh.devices.reshape(far, 2, HEADS, cores), ("dh", "dl", "h", "c"))
    dp, seq, every = ("dh", "dl"), ("h", "c"), ("dh", "dl", "h", "c")
    rows = P(every, None)
    return jax.shard_map(
        functools.partial(local, far),
        mesh=fine,
        in_specs=(
            P(dp, seq, None),
            P(dp, seq),
            P(dp, None),
            P(dp, seq, None, None),
            P(dp, None, None, None),
            P(dp, None, None, None),
            P(every),
            rows,
            rows,
            rows,
            rows,
            P(every),
            rows,
            rows,
            rows,
            P(dp, seq, None),
        ),
        out_specs=(
            P(dp, seq, None),
            P(dp, seq, None),
            P(every),
            rows,
            rows,
            rows,
            rows,
            P(every),
            rows,
            rows,
            rows,
        ),
        check_vma=False,
    )
```

time: 592 us -> 464 us (0.78)
  starting transfers between devices: 111 us -> 49.6 us
  Pallas kernels: 137 us -> 96.4 us
  waiting for transfers between devices: 189 us -> 153 us
  blocking collectives: 0 us -> 32.3 us
  local copies, waits for them, and re-layouts: 61 us -> 48.2 us
  matrix products: 26.1 us -> 18 us
    ppermute x49 -> x16, starting transfers between devices: 95.6 us -> 17.2 us  [turn(): return lax.ppermute(block, 'h', route)]
    ppermute x49 -> x16, waiting for transfers between devices: 143 us -> 70 us  [turn(): return lax.ppermute(block, 'h', route)]
    all_to_all x0 -> x1, blocking collectives: none -> 32.3 us  [exchange(): return lax.all_to_all(blocks, 'h', 0, 0)]
    ppermute x28, waiting for transfers between devices: 45 us -> 63.4 us  [swap(): return lax.ppermute(block, axis, [(0, 1), (1, 0)])]
    pallas_call x1, Pallas kernels: 35.8 us -> 18.7 us  [attend(): pl.pallas_call(attend_kernel, grid_spec=pltpu.PrefetchScalarGridSpec(num_...]
    all_to_all x0 -> x3, starting transfers between devices: none -> 15.9 us  [exchange(): return lax.all_to_all(blocks, 'h', 0, 0)]
    all_to_all x0 -> x3, waiting for transfers between devices: none -> 13.7 us  [exchange(): return lax.all_to_all(blocks, 'h', 0, 0)]
    pallas_call x1, Pallas kernels: 40.2 us -> 27.1 us  [attend_back(): pl.pallas_call(attend_back_kernel, grid_spec=pltpu.PrefetchScalarGridSpec...]
  transfers between devices with their start and end apart: 79 -> 49, of which waited for: 35 -> 21; matrix products, arithmetic and copies ran while one was open for 19% -> 21% of each run, Pallas kernels for 24% -> 20%
where the time goes in v2:
time: 464 us; the launch traced here: 458 us
  waiting for transfers between devices  153 us (33%)
  Pallas kernels  96.4 us (21%)
  starting transfers between devices  49.6 us (11%)
  local copies, waits for them, and re-layouts  48.2 us (10%)
  other arithmetic  45.3 us (10%)
  blocking collectives  32.3 us (7%)
  matrix products  18 us (4%)
  between operations  15.6 us (3%)
    ppermute x16, waiting for transfers between devices, turn(): return lax.ppermute(block, 'h', route)  70 us
    ppermute x28, waiting for transfers between devices, swap(): return lax.ppermute(block, axis, [(0, 1), (1, 0)])  63.4 us
    all_to_all x1, blocking collectives, exchange(): return lax.all_to_all(blocks, 'h', 0, 0)  32.3 us
    pallas_call x1, Pallas kernels, attend_back(): pl.pallas_call(attend_back_kernel, grid_spec=pltpu.PrefetchScalarGridSpec...  27.1 us
    pallas_call x1, Pallas kernels, attend(): pl.pallas_call(attend_kernel, grid_spec=pltpu.PrefetchScalarGridSpec(num_...  18.7 us
    pallas_call x2, Pallas kernels, ffn(): pl.pallas_call(ffn_kernel, in_specs=[vmem()] * 7, out_specs=[vmem()] * 4,...  18.2 us
    ppermute x16, starting transfers between devices, turn(): return lax.ppermute(block, 'h', route)  17.2 us
    ppermute x28, starting transfers between devices, swap(): return lax.ppermute(block, axis, [(0, 1), (1, 0)])  16.4 us
  transfers between devices with their start and end apart: 49, of which 21 were waited for; matrix products, arithmetic and copies ran while one was open for 21% of the time, Pallas kernels for 20%

profile of v2, /device:TPU:0, one launch (start us, length us, event | category | flops | bytes accessed | tf_op | source)
XLA Modules:
  0.0 457.9 jit_solution(12038193946614955932)
XLA Ops:
  7.3 3.1 collective-permute-start.2
  14.5 7.9 %collective-permute-done.2.refs_1_ = bf16[256,1024]{1,0:T(8,128)(2,1)S(1)} collective-permute-done((bf16[256,1024]{1,0:T(8,128)(2,1)}, bf16[256,1024]{1,0:T(8,128)(2,1)S(1)}, u32[]{:S(2)}, u32[]{:S(2)}) %collective-permute-start.2) | collective-permute-done | bytes 524320 | tf_op jit(solution)/shard_map/ppermute | solution.py:46
  22.4 1.5 collective-permute-done.3.refs_2_
  24.0 1.6 collective-permute-start.4
  27.7 8.8 %collective-permute-done.4.refs_3_ = bf16[256,1024]{1,0:T(8,128)(2,1)S(1)} collective-permute-done((bf16[256,1024]{1,0:T(8,128)(2,1)S(1)}, bf16[256,1024]{1,0:T(8,128)(2,1)S(1)}, u32[]{:S(2)}, u32[]{:S(2)}) %collective-permute-start.4) | collective-permute-done | bytes 524320 | tf_op jit(solution)/shard_map/ppermute | solution.py:46
  36.5 1.6 collective-permute-start.5
  41.5 4.8 %all-to-all-start = ((bf16[8,112,128]{2,1,0:T(8,128)(2,1)}), bf16[8,112,128]{2,1,0:T(8,128)(2,1)S(1)}, u32[]{:S(2)}, u32[]{:S(2)}) async-start(bf16[8,112,128]{2,1,0:T(8,128)(2,1)} %copy.363), calls=%async_computation | async-start | bytes 458752 | tf_op jit(solution)/shard_map/all_to_all | solution.py:55
  46.4 9.3 %all-to-all-done = bf16[8,112,128]{2,1,0:T(8,128)(2,1)S(1)} async-done(((bf16[8,112,128]{2,1,0:T(8,128)(2,1)}), bf16[8,112,128]{2,1,0:T(8,128)(2,1)S(1)}, u32[]{:S(2)}, u32[]{:S(2)}) %all-to-all-start) | async-done | bytes 229408 | tf_op jit(solution)/shard_map/all_to_all | solution.py:55
  57.5 2.0 collective-permute-start.9
  60.6 1.8 fusion.46
  65.1 3.7 fusion.55
  69.0 1.6 collective-permute-start.11
  71.1 2.0 pad_maximum_fusion.1
  73.0 2.0 collective-permute-done.11
  78.9 8.2 %qkv5.1 = (bf16[8,256,128]{2,1,0:T(8,128)(2,1)}, bf16[2,8,256,128]{3,2,1,0:T(8,128)(2,1)}, bf16[8,256,1024]{2,1,0:T(8,128)(2,1)}) custom-call(s32[5]{0:T(128)} %compare_select_fusion.7.tab, bf16[256,1024]{1,0:T(8,128)(2,1)} %bitcast.352, bf16[256,1024]{1,0:T(8,128)(2,1)} %copy-done.36, bf16[256,1024]{1,0:T(8,128)(2,1)} %copy-done.37, ...), custom_call_target="tpu_custom_call" | custom-call | flops 1006632960 | bytes 6553600 | tf_op jit(solution)/shard_map/qkv5/pallas_call | solution.py:119
  87.0 6.1 %qkv3.1 = (bf16[8,256,128]{2,1,0:T(8,128)(2,1)}, bf16[2,8,256,128]{3,2,1,0:T(8,128)(2,1)}, bf16[8,256,1024]{2,1,0:T(8,128)(2,1)}) custom-call(s32[3]{0:T(128)} %compare_select_fusion.8.tab, bf16[256,1024]{1,0:T(8,128)(2,1)} %copy-done.22, bf16[256,1024]{1,0:T(8,128)(2,1)} %copy-done.23, ...), custom_call_target="tpu_custom_call", output_to_operand_aliasing={{0}: (9, {}), {1}: (10, {}), {2}: (11, {})} | custom-call | flops 603979776 | bytes 3932160 | tf_op jit(solution)/shard_map/qkv3/pallas_call | solution.py:119
  99.6 18.7 %attend.1 = (f32[8,256,128]{2,1,0:T(8,128)}, bf16[8,256,128]{2,1,0:T(8,128)(2,1)}, f32[8,256,1]{2,1,0:T(8,128)}, bf16[2,8,256,128]{3,2,1,0:T(8,128)(2,1)}) custom-call(s32[42]{0:T(128)} %concatenate.158.tab, bf16[8,256,128]{2,1,0:T(8,128)(2,1)} %get-tuple-element.68.q_ref, bf16[2,8,256,128]{3,2,1,0:T(8,128)(2,1)} %get-tuple-element.69.own_ref, ...), custom_call_target="tpu_custom_call" | custom-call | flops 24999999488 | bytes 6291456 | tf_op jit(solution)/shard_map/attend/pallas_call | solution.py:224
  118.3 32.3 %all_to_all.20.heads_ref = bf16[8,256,128]{2,1,0:T(8,128)(2,1)} all-to-all(bf16[8,256,128]{2,1,0:T(8,128)(2,1)} %get-tuple-element.70), channel_id=1, replica_groups=mesh['dh'=1,'dl'=2,'h'=8,'c'=2] {'h'}, dimensions={0} | all-to-all | bytes 1048576 | tf_op jit(solution)/shard_map/all_to_all | solution.py:55
  150.6 5.5 %all-gather.3.cloned.1.call-done = bf16[1792,1408]{1,0:T(8,128)(2,1)} async-done(((bf16[224,1408]{1,0:T(8,128)(2,1)}), bf16[1792,1408]{1,0:T(8,128)(2,1)}) %all-gather.3.cloned.1.call-update) | async-done | bytes 5046288 | tf_op jit(solution)/shard_map/all_gather | solution.py:622
  158.8 12.2 %collective-permute-done.15 = bf16[1,8,32,1024]{3,2,1,0:T(8,128)(2,1)S(1)} collective-permute-done((bf16[1,8,32,1024]{3,2,1,0:T(8,128)(2,1)S(1)}, bf16[1,8,32,1024]{3,2,1,0:T(8,128)(2,1)S(1)}, u32[]{:S(2)}, u32[]{:S(2)}) %collective-permute-start.15) | collective-permute-done | bytes 524320 | tf_op jit(solution)/shard_map/ppermute | solution.py:41
  173.5 1.6 maximum_select_fusion
  175.2 3.7 out_block.1
  179.8 6.1 %collective-permute-done.21.ga = bf16[256,1024]{1,0:T(8,128)(2,1)S(1)} collective-permute-done((bf16[256,1024]{1,0:T(8,128)(2,1)S(1)}, bf16[256,1024]{1,0:T(8,128)(2,1)S(1)}, u32[]{:S(2)}, u32[]{:S(2)}) %collective-permute-start.21) | collective-permute-done | bytes 524320 | tf_op jit(solution)/shard_map/ppermute | solution.py:41
  185.8 10.8 %collective-permute-done.19.na = bf16[256,1024]{1,0:T(8,128)(2,1)S(1)} collective-permute-done((bf16[256,1024]{1,0:T(8,128)(2,1)}, bf16[256,1024]{1,0:T(8,128)(2,1)S(1)}, u32[]{:S(2)}, u32[]{:S(2)}) %collective-permute-start.19) | collective-permute-done | bytes 524320 | tf_op jit(solution)/shard_map/ppermute | solution.py:41
  197.1 2.0 slice.362
  199.2 2.6 slice.365
  202.1 2.4 fusion.82
  206.0 9.1 %ffn.3 = (bf16[2,256,704]{2,1,0:T(8,128)(2,1)}, bf16[2,256,704]{2,1,0:T(8,128)(2,1)}, bf16[2,256,704]{2,1,0:T(8,128)(2,1)}, bf16[2,256,1024]{2,1,0:T(8,128)(2,1)}) custom-call(bf16[256,1024]{1,0:T(8,128)(2,1)} %copy-done.10, bf16[256,1024]{1,0:T(8,128)(2,1)} %copy-done.13, bf16[256,1024]{1,0:T(8,128)(2,1)} %copy-done.39, bf16[256,1024]{1,0:T(8,128)(2,1)} %copy-done.41, ...), custom_call_target="tpu_custom_call" | custom-call | flops 3690987520 | bytes 8519680 | tf_op jit(solution)/shard_map/ffn/pallas_call | solution.py:371
  217.6 9.1 %ffn.2 = (bf16[2,256,704]{2,1,0:T(8,128)(2,1)}, bf16[2,256,704]{2,1,0:T(8,128)(2,1)}, bf16[2,256,704]{2,1,0:T(8,128)(2,1)}, bf16[2,256,1024]{2,1,0:T(8,128)(2,1)}) custom-call(bf16[256,1024]{1,0:T(8,128)(2,1)} %get-tuple-element.74.na, bf16[256,1024]{1,0:T(8,128)(2,1)} %copy-done.16, bf16[256,1024]{1,0:T(8,128)(2,1)} %bitcast.365, ...), custom_call_target="tpu_custom_call" | custom-call | flops 3690987520 | bytes 8519680 | tf_op jit(solution)/shard_map/ffn/pallas_call | solution.py:371
  226.7 2.2 slice_bitcast_fusion.7
  231.6 12.9 %collective-permute-done.25.pc = bf16[256,1024]{1,0:T(8,128)(2,1)S(1)} collective-permute-done((bf16[256,1024]{1,0:T(8,128)(2,1)S(1)}, bf16[256,1024]{1,0:T(8,128)(2,1)S(1)}, u32[]{:S(2)}, u32[]{:S(2)}) %collective-permute-start.25) | collective-permute-done | bytes 524320 | tf_op jit(solution)/shard_map/ppermute | solution.py:41
  245.3 4.6 %mid_block.1 = (f32[256,1024]{1,0:T(8,128)}, bf16[256,1024]{1,0:T(8,128)(2,1)}, bf16[8,256,128]{2,1,0:T(8,128)(2,1)}) custom-call(f32[256,1024]{1,0:T(8,128)} %get-tuple-element.73.mid_ref, bf16[256,1024]{1,0:T(8,128)(2,1)} %get-tuple-element.131.pa, bf16[256,1024]{1,0:T(8,128)(2,1)} %copy-done.43, bf16[256,1024]{1,0:T(8,128)(2,1)} %copy-done.44, ...), custom_call_target="tpu_custom_call" | custom-call | flops 536870912 | bytes 6291456 | tf_op jit(solution)/shard_map/mid_block/pallas_call | solution.py:404
  250.0 1.9 convolution_convert_fusion
  255.5 1.6 copy.387
  257.1 2.8 copy.388
  262.4 1.6 copy.391
  264.0 2.7 copy.392
  266.7 4.1 all-to-all-start.2
  270.9 1.9 convert_add_fusion
  274.4 2.0 fusion.22
  277.5 9.9 %collective-permute-done.30 = bf16[1,8,32,1024]{3,2,1,0:T(8,128)(2,1)S(1)} collective-permute-done((bf16[1,8,32,1024]{3,2,1,0:T(8,128)(2,1)S(1)}, bf16[1,8,32,1024]{3,2,1,0:T(8,128)(2,1)S(1)}, u32[]{:S(2)}, u32[]{:S(2)}) %collective-permute-start.30) | collective-permute-done | bytes 524320 | tf_op jit(solution)/shard_map/ppermute | solution.py:41
  287.7 3.4 fusion.8
  291.2 27.1 %attend_back.1 = (f32[8,256,128]{2,1,0:T(8,128)}, f32[2,8,256,128]{3,2,1,0:T(8,128)}, bf16[2,8,256,128]{3,2,1,0:T(8,128)(2,1)}) custom-call(s32[42]{0:T(128)} %concatenate.158.tab, bf16[8,256,128]{2,1,0:T(8,128)(2,1)} %get-tuple-element.68.q_ref, bf16[8,256,128]{2,1,0:T(8,128)(2,1)} %all-to-all-done.2.up_ref, f32[8,256,128]{2,1,0:T(8,128)} %get-tuple-element.95.o_ref, ...), custom_call_target="tpu_custom_call" | custom-call | flops 30000001024 | bytes 10485760 | tf_op jit(solution)/shard_map/attend_back/pallas_call | solution.py:304
  319.1 2.1 convolution_convert_fusion.2
  322.6 2.0 convolution_convert_fusion.1
  325.6 9.8 %qkv_back.1 = (bf16[8,256,1024]{2,1,0:T(8,128)(2,1)}, bf16[8,256,384]{2,1,0:T(8,128)(2,1)}) custom-call(s32[8]{0:T(128)} %compare_select_fusion.6.tab, f32[8,256,128]{2,1,0:T(8,128)} %get-tuple-element.98.dq_ref, f32[2,8,256,128]{3,2,1,0:T(8,128)} %get-tuple-element.99.own_ref, bf16[2,8,256,128]{3,2,1,0:T(8,128)(2,1)} %copy-done.25, ...), custom_call_target="tpu_custom_call" | custom-call | flops 1610612736 | bytes 8388608 | tf_op jit(solution)/shard_map/qkv_back/pallas_call | solution.py:438
  336.6 1.7 collective-permute-start.32
  338.7 5.1 %bitcast_convert_fusion = bf16[1024,384]{1,0:T(8,128)(2,1)S(1)} fusion(bf16[8,256,1024]{2,1,0:T(8,128)(2,1)} %get-tuple-element.102, bf16[8,256,384]{2,1,0:T(8,128)(2,1)} %get-tuple-element.103), kind=kOutput, calls=%fused_computation.23 | convolution fusion | flops 1611005952 | bytes 6553600 | tf_op jit(solution)/shard_map/std,stg->dg/dot_general | solution.py:804
  344.0 5.9 %collective-permute-done.32 = bf16[128,1024]{1,0:T(8,128)(2,1)S(1)} collective-permute-done((bf16[128,1024]{1,0:T(8,128)(2,1)S(1)}, bf16[128,1024]{1,0:T(8,128)(2,1)S(1)}, u32[]{:S(2)}, u32[]{:S(2)}) %collective-permute-start.32) | collective-permute-done | bytes 262176 | tf_op jit(solution)/shard_map/ppermute | solution.py:46
  352.2 2.5 collective-permute-start.37
  354.9 16.4 %collective-permute-done.33 = bf16[256,1024]{1,0:T(8,128)(2,1)S(1)} collective-permute-done((bf16[256,1024]{1,0:T(8,128)(2,1)S(1)}, bf16[256,1024]{1,0:T(8,128)(2,1)S(1)}, u32[]{:S(2)}, u32[]{:S(2)}) %collective-permute-start.33) | collective-permute-done | bytes 524320 | tf_op jit(solution)/shard_map/ppermute | solution.py:46
  373.1 1.9 collective-permute-start.28
  375.0 5.5 %collective-permute-done.41 = bf16[1,8,32,384]{3,2,1,0:T(8,128)(2,1)S(1)} collective-permute-done((bf16[1,8,32,384]{3,2,1,0:T(8,128)(2,1)S(1)}, bf16[1,8,32,384]{3,2,1,0:T(8,128)(2,1)S(1)}, u32[]{:S(2)}, u32[]{:S(2)}) %collective-permute-start.41) | collective-permute-done | bytes 196640 | tf_op jit(solution)/shard_map/ppermute | solution.py:41
  381.2 7.0 %all-to-all-start.3 = ((bf16[8,32,384]{2,1,0:T(8,128)(2,1)}), bf16[8,32,384]{2,1,0:T(8,128)(2,1)S(1)}, u32[]{:S(2)}, u32[]{:S(2)}) async-start(bf16[8,32,384]{2,1,0:T(8,128)(2,1)} %fusion.57), calls=%async_computation.3 | async-start | bytes 393216 | tf_op jit(solution)/shard_map/all_to_all | solution.py:55
  388.2 3.0 fusion.32
  391.2 2.0 collective-permute-start.38
  393.2 2.4 fusion.49
  395.6 4.4 all-to-all-done.3
  401.6 16.3 %collective-permute-done.38 = bf16[256,1024]{1,0:T(8,128)(2,1)S(1)} collective-permute-done((bf16[256,1024]{1,0:T(8,128)(2,1)}, bf16[256,1024]{1,0:T(8,128)(2,1)S(1)}, u32[]{:S(2)}, u32[]{:S(2)}) %collective-permute-start.38) | collective-permute-done | bytes 524320 | tf_op jit(solution)/shard_map/ppermute | solution.py:46
  421.5 11.1 %collective-permute-done.39 = bf16[256,1024]{1,0:T(8,128)(2,1)S(1)} collective-permute-done((bf16[256,1024]{1,0:T(8,128)(2,1)S(1)}, bf16[256,1024]{1,0:T(8,128)(2,1)S(1)}, u32[]{:S(2)}, u32[]{:S(2)}) %collective-permute-start.39) | collective-permute-done | bytes 524320 | tf_op jit(solution)/shard_map/ppermute | solution.py:46
  434.1 2.4 fusion.21
  439.3 2.4 collective-permute-start.43
  441.6 1.7 slice_convert_fusion
  444.1 2.7 collective-permute-done.43
  (326 shorter events, 73.1 us)
Async XLA Ops:
  7.3 15.2 %collective-permute-start.2 = (bf16[256,1024]{1,0:T(8,128)(2,1)}, bf16[256,1024]{1,0:T(8,128)(2,1)S(1)}, u32[]{:S(2)}, u32[]{:S(2)}) collective-permute-start(bf16[256,1024]{1,0:T(8,128)(2,1)} %bitcast.350), channel_id=1, source_target_pairs={{0,4},{4,8},{8,12},{12,14},{14,10},{10,6},{6,2},{2,0},{1,5},{5,9},... | collective-permute-start | bytes 1572872 | tf_op jit(solution)/shard_map/ppermute | solution.py:46
  10.4 13.6 %collective-permute-start.3 = (bf16[256,1024]{1,0:T(8,128)(2,1)}, bf16[256,1024]{1,0:T(8,128)(2,1)S(1)}, u32[]{:S(2)}, u32[]{:S(2)}) collective-permute-start(bf16[256,1024]{1,0:T(8,128)(2,1)} %bitcast.351), channel_id=1, source_target_pairs={{0,2},{4,0},{8,4},{12,8},{14,12},{10,14},{6,10},{2,6},{1,3},{5,1},... | collective-permute-start | bytes 1572872 | tf_op jit(solution)/shard_map/ppermute | solution.py:46
  14.1 13.5 %collective-permute-start = (bf16[2,32,1408]{2,1,0:T(8,128)(2,1)S(1)}, bf16[2,32,1408]{2,1,0:T(8,128)(2,1)S(1)}, u32[]{:S(2)}, u32[]{:S(2)}) collective-permute-start(bf16[2,32,1408]{2,1,0:T(8,128)(2,1)S(1)} %select_bitcast_fusion.2), channel_id=1, source_target_pairs={{0,1},{1,0},{2,3},{3,2},{4,5},{5,4},{6,7},{7,6},{8,9},{9,8},{10,11... | collective-permute-start | bytes 540680 | tf_op jit(solution)/shard_map/ppermute | solution.py:41
  22.4 38.2 %copy-start.36 = (bf16[256,1024]{1,0:T(8,128)(2,1)}, bf16[256,1024]{1,0:T(8,128)(2,1)S(1)}, u32[]{:S(2)}) copy-start(bf16[256,1024]{1,0:T(8,128)(2,1)S(1)} %collective-permute-done.2.refs_1_) | copy-start | bytes 1572868
  24.0 36.7 %copy-start.37 = (bf16[256,1024]{1,0:T(8,128)(2,1)}, bf16[256,1024]{1,0:T(8,128)(2,1)S(1)}, u32[]{:S(2)}) copy-start(bf16[256,1024]{1,0:T(8,128)(2,1)S(1)} %collective-permute-done.3.refs_2_) | copy-start | bytes 1572868
  24.0 12.5 %collective-permute-start.4 = (bf16[256,1024]{1,0:T(8,128)(2,1)S(1)}, bf16[256,1024]{1,0:T(8,128)(2,1)S(1)}, u32[]{:S(2)}, u32[]{:S(2)}) collective-permute-start(bf16[256,1024]{1,0:T(8,128)(2,1)S(1)} %collective-permute-done.2.refs_1_), channel_id=1, source_target_pairs={{0,4},{4,8},{8,12},{12,14},{14,10},{10,6},{6,2},{2,0},{1,5},{5,9},... | collective-permute-start | bytes 1572872 | tf_op jit(solution)/shard_map/ppermute | solution.py:46
  25.5 12.5 %collective-permute-start.6 = (bf16[256,1024]{1,0:T(8,128)(2,1)S(1)}, bf16[256,1024]{1,0:T(8,128)(2,1)}, u32[]{:S(2)}, u32[]{:S(2)}) collective-permute-start(bf16[256,1024]{1,0:T(8,128)(2,1)S(1)} %collective-permute-done.3.refs_2_), channel_id=1, source_target_pairs={{0,2},{4,0},{8,4},{12,8},{14,12},{10,14},{6,10},{2,6},{1,3},{5,1},... | collective-permute-start | bytes 1572872 | tf_op jit(solution)/shard_map/ppermute | solution.py:46
  36.5 28.0 %copy-start.38 = (bf16[256,1024]{1,0:T(8,128)(2,1)}, bf16[256,1024]{1,0:T(8,128)(2,1)S(1)}, u32[]{:S(2)}) copy-start(bf16[256,1024]{1,0:T(8,128)(2,1)S(1)} %collective-permute-done.4.refs_3_) | copy-start | bytes 1572868
  36.5 19.2 %collective-permute-start.5 = (bf16[256,1024]{1,0:T(8,128)(2,1)S(1)}, bf16[256,1024]{1,0:T(8,128)(2,1)S(1)}, u32[]{:S(2)}, u32[]{:S(2)}) collective-permute-start(bf16[256,1024]{1,0:T(8,128)(2,1)S(1)} %collective-permute-done.4.refs_3_), channel_id=1, source_target_pairs={{0,4},{4,8},{8,12},{12,14},{14,10},{10,6},{6,2},{2,0},{1,5},{5,9},... | collective-permute-start | bytes 1572872 | tf_op jit(solution)/shard_map/ppermute | solution.py:46
  38.1 17.6 %collective-permute-start.7 = (bf16[256,1024]{1,0:T(8,128)(2,1)}, bf16[256,1024]{1,0:T(8,128)(2,1)S(1)}, u32[]{:S(2)}, u32[]{:S(2)}) collective-permute-start(bf16[256,1024]{1,0:T(8,128)(2,1)} %collective-permute-done.6.refs_4_), channel_id=1, source_target_pairs={{0,2},{4,0},{8,4},{12,8},{14,12},{10,14},{6,10},{2,6},{1,3},{5,1},... | collective-permute-start | bytes 1572872 | tf_op jit(solution)/shard_map/ppermute | solution.py:46
  39.2 25.3 %copy-start.63 = (s32[5]{0:T(128)S(1)}, s32[5]{0:T(128)}, u32[]{:S(2)}) copy-start(s32[5]{0:T(128)} %constant.152) | copy-start | bytes 64
  39.2 20.3 %collective-permute-start.1 = (bf16[2,32,1408]{2,1,0:T(8,128)(2,1)}, bf16[2,32,1408]{2,1,0:T(8,128)(2,1)}, u32[]{:S(2)}, u32[]{:S(2)}) collective-permute-start(bf16[2,32,1408]{2,1,0:T(8,128)(2,1)} %fusion.60), channel_id=1, source_target_pairs={{0,16},{16,0},{1,17},{17,1},{2,18},{18,2},{3,19},{19,3},{4,20},{20... | collective-permute-start | bytes 540680 | tf_op jit(solution)/shard_map/ppermute | solution.py:41
  41.5 14.3 %all-to-all-start = ((bf16[8,112,128]{2,1,0:T(8,128)(2,1)}), bf16[8,112,128]{2,1,0:T(8,128)(2,1)S(1)}, u32[]{:S(2)}, u32[]{:S(2)}) async-start(bf16[8,112,128]{2,1,0:T(8,128)(2,1)} %copy.363), calls=%async_computation | async-start | bytes 458752 | tf_op jit(solution)/shard_map/all_to_all | solution.py:55
  46.3 109.8 %all-gather.3.cloned.1.call-start = ((), (), s32[]{:S(2)}) async-start(), calls=%async_computation.6 | async-start | bytes 5677056 | tf_op jit(solution)/shard_map/all_gather | solution.py:622
  55.7 13.2 %copy-start.23 = (bf16[256,1024]{1,0:T(8,128)(2,1)}, bf16[256,1024]{1,0:T(8,128)(2,1)S(1)}, u32[]{:S(2)}) copy-start(bf16[256,1024]{1,0:T(8,128)(2,1)S(1)} %collective-permute-done.7.refs_1_) | copy-start | bytes 1572868
  56.5 6.6 %collective-permute-start.8 = (bf16[128,1024]{1,0:T(8,128)(2,1)}, bf16[128,1024]{1,0:T(8,128)(2,1)S(1)}, u32[]{:S(2)}, u32[]{:S(2)}) collective-permute-start(bf16[128,1024]{1,0:T(8,128)(2,1)} %slice.274), channel_id=1, source_target_pairs={{0,4},{4,8},{8,12},{12,14},{14,10},{10,6},{6,2},{2,0},{1,5},{5,9},... | collective-permute-start | bytes 786440 | tf_op jit(solution)/shard_map/ppermute | solution.py:46
  57.5 7.0 %collective-permute-start.9 = (bf16[128,1024]{1,0:T(8,128)(2,1)}, bf16[128,1024]{1,0:T(8,128)(2,1)}, u32[]{:S(2)}, u32[]{:S(2)}) collective-permute-start(bf16[128,1024]{1,0:T(8,128)(2,1)} %slice.275), channel_id=1, source_target_pairs={{0,2},{4,0},{8,4},{12,8},{14,12},{10,14},{6,10},{2,6},{1,3},{5,1},... | collective-permute-start | bytes 786440 | tf_op jit(solution)/shard_map/ppermute | solution.py:46
  69.0 6.1 %collective-permute-start.11 = (bf16[8,112,128]{2,0,1:T(8,128)(2,1)S(1)}, bf16[8,112,128]{2,0,1:T(8,128)(2,1)S(1)}, u32[]{:S(2)}, u32[]{:S(2)}) collective-permute-start(bf16[8,112,128]{2,0,1:T(8,128)(2,1)S(1)} %copy.445), channel_id=1, source_target_pairs={{0,16},{16,0},{1,17},{17,1},{2,18},{18,2},{3,19},{19,3},{4,20},{20... | collective-permute-start | bytes 688136 | tf_op jit(solution)/shard_map/ppermute | solution.py:41
  71.1 4.2 collective-permute-start.10
  75.0 1.5 collective-permute-start.12
  93.2 5.5 %collective-permute-start.13 = (bf16[2,8,256,128]{3,2,1,0:T(8,128)(2,1)}, bf16[2,8,256,128]{3,2,1,0:T(8,128)(2,1)S(1)}, u32[]{:S(2)}, u32[]{:S(2)}) collective-permute-start(bf16[2,8,256,128]{3,2,1,0:T(8,128)(2,1)} %get-tuple-element.69.own_ref), channel_id=1, source_target_pairs={{0,1},{1,0},{2,3},{3,2},{4,5},{5,4},{6,7},{7,6},{8,9},{9,8},{10,11... | collective-permute-start | bytes 3145736 | tf_op jit(solution)/shard_map/ppermute | solution.py:41
  118.3 52.7 %copy-start.5 = (bf16[1,256,1024]{2,1,0:T(8,128)(2,1)S(1)}, bf16[1,256,1024]{2,1,0:T(8,128)(2,1)}, u32[]{:S(2)}) copy-start(bf16[1,256,1024]{2,1,0:T(8,128)(2,1)} %param.33) | copy-start | bytes 1572868
  157.3 13.7 %collective-permute-start.15 = (bf16[1,8,32,1024]{3,2,1,0:T(8,128)(2,1)S(1)}, bf16[1,8,32,1024]{3,2,1,0:T(8,128)(2,1)S(1)}, u32[]{:S(2)}, u32[]{:S(2)}) collective-permute-start(bf16[1,8,32,1024]{3,2,1,0:T(8,128)(2,1)S(1)} %pad_maximum_fusion.12), channel_id=1, source_target_pairs={{0,16},{16,0},{1,17},{17,1},{2,18},{18,2},{3,19},{19,3},{4,20},{20... | collective-permute-start | bytes 1572872 | tf_op jit(solution)/shard_map/ppermute | solution.py:41
  158.8 14.3 %collective-permute-start.14 = (bf16[1,8,32,1024]{3,2,1,0:T(8,128)(2,1)S(1)}, bf16[1,8,32,1024]{3,2,1,0:T(8,128)(2,1)S(1)}, u32[]{:S(2)}, u32[]{:S(2)}) collective-permute-start(bf16[1,8,32,1024]{3,2,1,0:T(8,128)(2,1)S(1)} %pad_maximum_fusion.12), channel_id=1, source_target_pairs={{0,1},{1,0},{2,3},{3,2},{4,5},{5,4},{6,7},{7,6},{8,9},{9,8},{10,11... | collective-permute-start | bytes 1572872 | tf_op jit(solution)/shard_map/ppermute | solution.py:41
  171.0 2.4 collective-permute-start.16
  171.0 14.8 %collective-permute-start.21 = (bf16[256,1024]{1,0:T(8,128)(2,1)S(1)}, bf16[256,1024]{1,0:T(8,128)(2,1)S(1)}, u32[]{:S(2)}, u32[]{:S(2)}) collective-permute-start(bf16[256,1024]{1,0:T(8,128)(2,1)S(1)} %bitcast.367), channel_id=1, source_target_pairs={{0,16},{16,0},{1,17},{17,1},{2,18},{18,2},{3,19},{19,3},{4,20},{20... | collective-permute-start | bytes 1572872 | tf_op jit(solution)/shard_map/ppermute | solution.py:41
  178.9 17.8 %collective-permute-start.19 = (bf16[256,1024]{1,0:T(8,128)(2,1)}, bf16[256,1024]{1,0:T(8,128)(2,1)S(1)}, u32[]{:S(2)}, u32[]{:S(2)}) collective-permute-start(bf16[256,1024]{1,0:T(8,128)(2,1)} %get-tuple-element.74.na), channel_id=1, source_target_pairs={{0,16},{16,0},{1,17},{17,1},{2,18},{18,2},{3,19},{19,3},{4,20},{20... | collective-permute-start | bytes 1572872 | tf_op jit(solution)/shard_map/ppermute | solution.py:41
  185.8 13.3 %copy-start.39 = (bf16[256,1024]{1,0:T(8,128)(2,1)}, bf16[256,1024]{1,0:T(8,128)(2,1)S(1)}, u32[]{:S(2)}) copy-start(bf16[256,1024]{1,0:T(8,128)(2,1)S(1)} %collective-permute-done.21.ga) | copy-start | bytes 1572868
  185.8 18.6 %collective-permute-start.22 = (bf16[256,1024]{1,0:T(8,128)(2,1)S(1)}, bf16[256,1024]{1,0:T(8,128)(2,1)S(1)}, u32[]{:S(2)}, u32[]{:S(2)}) collective-permute-start(bf16[256,1024]{1,0:T(8,128)(2,1)S(1)} %collective-permute-done.21.ga), channel_id=1, source_target_pairs={{0,1},{1,0},{2,3},{3,2},{4,5},{5,4},{6,7},{7,6},{8,9},{9,8},{10,11... | collective-permute-start | bytes 1572872 | tf_op jit(solution)/shard_map/ppermute | solution.py:41
  196.6 7.8 %collective-permute-start.20 = (bf16[256,1024]{1,0:T(8,128)(2,1)S(1)}, bf16[256,1024]{1,0:T(8,128)(2,1)S(1)}, u32[]{:S(2)}, u32[]{:S(2)}) collective-permute-start(bf16[256,1024]{1,0:T(8,128)(2,1)S(1)} %collective-permute-done.19.na), channel_id=1, source_target_pairs={{0,1},{1,0},{2,3},{3,2},{4,5},{5,4},{6,7},{7,6},{8,9},{9,8},{10,11... | collective-permute-start | bytes 1572872 | tf_op jit(solution)/shard_map/ppermute | solution.py:41
  196.6 20.2 %collective-permute-start.18 = (bf16[256,1024]{1,0:T(8,128)(2,1)S(1)}, bf16[256,1024]{1,0:T(8,128)(2,1)}, u32[]{:S(2)}, u32[]{:S(2)}) collective-permute-start(bf16[256,1024]{1,0:T(8,128)(2,1)S(1)} %bitcast.368), channel_id=1, source_target_pairs={{0,1},{1,0},{2,3},{3,2},{4,5},{5,4},{6,7},{7,6},{8,9},{9,8},{10,11... | collective-permute-start | bytes 1572872 | tf_op jit(solution)/shard_map/ppermute | solution.py:41
  204.4 12.4 %collective-permute-start.17 = (bf16[256,1024]{1,0:T(8,128)(2,1)S(1)}, bf16[256,1024]{1,0:T(8,128)(2,1)S(1)}, u32[]{:S(2)}, u32[]{:S(2)}) collective-permute-start(bf16[256,1024]{1,0:T(8,128)(2,1)S(1)} %copy-done.7), channel_id=1, source_target_pairs={{0,1},{1,0},{2,3},{3,2},{4,5},{5,4},{6,7},{7,6},{8,9},{9,8},{10,11... | collective-permute-start | bytes 1572872 | tf_op jit(solution)/shard_map/ppermute | solution.py:41
  216.2 12.7 %collective-permute-start.24 = (bf16[256,1024]{1,0:T(8,128)(2,1)S(1)}, bf16[256,1024]{1,0:T(8,128)(2,1)S(1)}, u32[]{:S(2)}, u32[]{:S(2)}) collective-permute-start(bf16[256,1024]{1,0:T(8,128)(2,1)S(1)} %slice_bitcast_fusion.6), channel_id=1, source_target_pairs={{0,1},{1,0},{2,3},{3,2},{4,5},{5,4},{6,7},{7,6},{8,9},{9,8},{10,11... | collective-permute-start | bytes 1572872 | tf_op jit(solution)/shard_map/ppermute | solution.py:41
  228.9 2.7 collective-permute-start.23
  230.2 14.4 %collective-permute-start.25 = (bf16[256,1024]{1,0:T(8,128)(2,1)S(1)}, bf16[256,1024]{1,0:T(8,128)(2,1)S(1)}, u32[]{:S(2)}, u32[]{:S(2)}) collective-permute-start(bf16[256,1024]{1,0:T(8,128)(2,1)S(1)} %fusion.39), channel_id=1, source_target_pairs={{0,16},{16,0},{1,17},{17,1},{2,18},{18,2},{3,19},{19,3},{4,20},{20... | collective-permute-start | bytes 1572872 | tf_op jit(solution)/shard_map/ppermute | solution.py:41
  253.1 17.9 %collective-permute-start.29 = (bf16[1,2,8,32,1024]{4,3,2,1,0:T(8,128)(2,1)}, bf16[1,2,8,32,1024]{4,3,2,1,0:T(8,128)(2,1)}, u32[]{:S(2)}, u32[]{:S(2)}) collective-permute-start(bf16[1,2,8,32,1024]{4,3,2,1,0:T(8,128)(2,1)} %select_bitcast_fusion), channel_id=1, source_target_pairs={{0,1},{1,0},{2,3},{3,2},{4,5},{5,4},{6,7},{7,6},{8,9},{9,8},{10,11... | collective-permute-start | bytes 3145736 | tf_op jit(solution)/shard_map/ppermute | solution.py:41
  266.7 24.5 %all-to-all-start.2 = ((bf16[8,256,128]{2,1,0:T(8,128)(2,1)}), bf16[8,256,128]{2,1,0:T(8,128)(2,1)}, u32[]{:S(2)}, u32[]{:S(2)}) async-start(bf16[8,256,128]{2,1,0:T(8,128)(2,1)} %get-tuple-element.87), calls=%async_computation.2 | async-start | bytes 1048576 | tf_op jit(solution)/shard_map/all_to_all | solution.py:55
  270.9 165.6 %reduce-scatter.2.cloned.1.call-start = ((), (), s32[]{:S(2)}) async-start(), calls=%async_computation.5 | async-start | bytes 5677056 | tf_op jit(solution)/shard_map/reduce_scatter | solution.py:751
  273.0 14.4 %collective-permute-start.30 = (bf16[1,8,32,1024]{3,2,1,0:T(8,128)(2,1)S(1)}, bf16[1,8,32,1024]{3,2,1,0:T(8,128)(2,1)S(1)}, u32[]{:S(2)}, u32[]{:S(2)}) collective-permute-start(bf16[1,8,32,1024]{3,2,1,0:T(8,128)(2,1)S(1)} %fusion.47), channel_id=1, source_target_pairs={{0,16},{16,0},{1,17},{17,1},{2,18},{18,2},{3,19},{19,3},{4,20},{20... | collective-permute-start | bytes 1572872 | tf_op jit(solution)/shard_map/ppermute | solution.py:41
  291.2 27.9 %copy-start.21 = (bf16[1,8,88,1024]{3,2,1,0:T(8,128)(2,1)S(1)}, bf16[1,8,88,1024]{3,2,1,0:T(8,128)(2,1)}, u32[]{:S(2)}) copy-start(bf16[1,8,88,1024]{3,2,1,0:T(8,128)(2,1)} %slice.365) | copy-start | bytes 4325380
  318.4 6.3 %collective-permute-start.31 = (bf16[2,8,256,128]{3,2,1,0:T(8,128)(2,1)}, bf16[2,8,256,128]{3,2,1,0:T(8,128)(2,1)S(1)}, u32[]{:S(2)}, u32[]{:S(2)}) collective-permute-start(bf16[2,8,256,128]{3,2,1,0:T(8,128)(2,1)} %get-tuple-element.100), channel_id=1, source_target_pairs={{0,1},{1,0},{2,3},{3,2},{4,5},{5,4},{6,7},{7,6},{8,9},{9,8},{10,11... | collective-permute-start | bytes 3145736 | tf_op jit(solution)/shard_map/ppermute | solution.py:41
  322.1 71.1 %collective-permute-start.26 = (bf16[256,1024]{1,0:T(8,128)(2,1)}, bf16[256,1024]{1,0:T(8,128)(2,1)}, u32[]{:S(2)}, u32[]{:S(2)}) collective-permute-start(bf16[256,1024]{1,0:T(8,128)(2,1)} %slice_bitcast_fusion.4), channel_id=1, source_target_pairs={{0,1},{1,0},{2,3},{3,2},{4,5},{5,4},{6,7},{7,6},{8,9},{9,8},{10,11... | collective-permute-start | bytes 1572872 | tf_op jit(solution)/shard_map/ppermute | solution.py:41
  336.6 13.3 %collective-permute-start.32 = (bf16[128,1024]{1,0:T(8,128)(2,1)S(1)}, bf16[128,1024]{1,0:T(8,128)(2,1)S(1)}, u32[]{:S(2)}, u32[]{:S(2)}) collective-permute-start(bf16[128,1024]{1,0:T(8,128)(2,1)S(1)} %get-tuple-element.122), channel_id=1, source_target_pairs={{0,4},{4,8},{8,12},{12,14},{14,10},{10,6},{6,2},{2,0},{1,5},{5,9},... | collective-permute-start | bytes 786440 | tf_op jit(solution)/shard_map/ppermute | solution.py:46
  338.3 11.6 %collective-permute-start.36 = (bf16[128,1024]{1,0:T(8,128)(2,1)S(1)}, bf16[128,1024]{1,0:T(8,128)(2,1)S(1)}, u32[]{:S(2)}, u32[]{:S(2)}) collective-permute-start(bf16[128,1024]{1,0:T(8,128)(2,1)S(1)} %get-tuple-element.123), channel_id=1, source_target_pairs={{0,2},{4,0},{8,4},{12,8},{14,12},{10,14},{6,10},{2,6},{1,3},{5,1},... | collective-permute-start | bytes 786440 | tf_op jit(solution)/shard_map/ppermute | solution.py:46
  343.9 10.8 %collective-permute-start.40 = (bf16[1,2,8,32,384]{4,3,2,1,0:T(8,128)(2,1)S(1)}, bf16[1,2,8,32,384]{4,3,2,1,0:T(8,128)(2,1)S(1)}, u32[]{:S(2)}, u32[]{:S(2)}) collective-permute-start(bf16[1,2,8,32,384]{4,3,2,1,0:T(8,128)(2,1)S(1)} %fusion.52), channel_id=1, source_target_pairs={{0,1},{1,0},{2,3},{3,2},{4,5},{5,4},{6,7},{7,6},{8,9},{9,8},{10,11... | collective-permute-start | bytes 1179656 | tf_op jit(solution)/shard_map/ppermute | solution.py:41
  351.2 20.1 %collective-permute-start.33 = (bf16[256,1024]{1,0:T(8,128)(2,1)S(1)}, bf16[256,1024]{1,0:T(8,128)(2,1)S(1)}, u32[]{:S(2)}, u32[]{:S(2)}) collective-permute-start(bf16[256,1024]{1,0:T(8,128)(2,1)S(1)} %pad_maximum_fusion.14), channel_id=1, source_target_pairs={{0,4},{4,8},{8,12},{12,14},{14,10},{10,6},{6,2},{2,0},{1,5},{5,9},... | collective-permute-start | bytes 1572872 | tf_op jit(solution)/shard_map/ppermute | solution.py:46
  351.3 21.5 %collective-permute-start.27 = (bf16[256,1024]{1,0:T(8,128)(2,1)S(1)}, bf16[256,1024]{1,0:T(8,128)(2,1)S(1)}, u32[]{:S(2)}, u32[]{:S(2)}) collective-permute-start(bf16[256,1024]{1,0:T(8,128)(2,1)S(1)} %slice_bitcast_fusion.2), channel_id=1, source_target_pairs={{0,1},{1,0},{2,3},{3,2},{4,5},{5,4},{6,7},{7,6},{8,9},{9,8},{10,11... | collective-permute-start | bytes 1572872 | tf_op jit(solution)/shard_map/ppermute | solution.py:41
  352.2 35.9 %collective-permute-start.37 = (bf16[256,1024]{1,0:T(8,128)(2,1)}, bf16[256,1024]{1,0:T(8,128)(2,1)}, u32[]{:S(2)}, u32[]{:S(2)}) collective-permute-start(bf16[256,1024]{1,0:T(8,128)(2,1)} %pad_maximum_fusion.15), channel_id=1, source_target_pairs={{0,2},{4,0},{8,4},{12,8},{14,12},{10,14},{6,10},{2,6},{1,3},{5,1},... | collective-permute-start | bytes 1572872 | tf_op jit(solution)/shard_map/ppermute | solution.py:46
  372.5 15.7 %collective-permute-start.34 = (bf16[256,1024]{1,0:T(8,128)(2,1)S(1)}, bf16[256,1024]{1,0:T(8,128)(2,1)}, u32[]{:S(2)}, u32[]{:S(2)}) collective-permute-start(bf16[256,1024]{1,0:T(8,128)(2,1)S(1)} %fusion.31), channel_id=1, source_target_pairs={{0,4},{4,8},{8,12},{12,14},{14,10},{10,6},{6,2},{2,0},{1,5},{5,9},... | collective-permute-start | bytes 1572872 | tf_op jit(solution)/shard_map/ppermute | solution.py:46
  372.6 7.8 %collective-permute-start.41 = (bf16[1,8,32,384]{3,2,1,0:T(8,128)(2,1)S(1)}, bf16[1,8,32,384]{3,2,1,0:T(8,128)(2,1)S(1)}, u32[]{:S(2)}, u32[]{:S(2)}) collective-permute-start(bf16[1,8,32,384]{3,2,1,0:T(8,128)(2,1)S(1)} %fusion.56), channel_id=1, source_target_pairs={{0,16},{16,0},{1,17},{17,1},{2,18},{18,2},{3,19},{19,3},{4,20},{20... | collective-permute-start | bytes 589832 | tf_op jit(solution)/shard_map/ppermute | solution.py:41
  373.1 20.1 %copy-start.3 = (f32[256,1024]{1,0:T(8,128)S(1)}, f32[256,1024]{1,0:T(8,128)}, u32[]{:S(2)}) copy-start(f32[256,1024]{1,0:T(8,128)} %get-tuple-element.73.mid_ref) | copy-start | bytes 3145732
  373.1 20.1 %copy-start.28 = (bf16[2,256,1024]{2,1,0:T(8,128)(2,1)S(1)}, bf16[2,256,1024]{2,1,0:T(8,128)(2,1)}, u32[]{:S(2)}) copy-start(bf16[2,256,1024]{2,1,0:T(8,128)(2,1)} %copy-done.27) | copy-start | bytes 3145732
  373.1 20.1 %collective-permute-start.28 = (bf16[256,1024]{1,0:T(8,128)(2,1)S(1)}, bf16[256,1024]{1,0:T(8,128)(2,1)}, u32[]{:S(2)}, u32[]{:S(2)}) collective-permute-start(bf16[256,1024]{1,0:T(8,128)(2,1)S(1)} %fusion.35), channel_id=1, source_target_pairs={{0,16},{16,0},{1,17},{17,1},{2,18},{18,2},{3,19},{19,3},{4,20},{20... | collective-permute-start | bytes 1572872 | tf_op jit(solution)/shard_map/ppermute | solution.py:41
  381.2 18.7 %all-to-all-start.3 = ((bf16[8,32,384]{2,1,0:T(8,128)(2,1)}), bf16[8,32,384]{2,1,0:T(8,128)(2,1)S(1)}, u32[]{:S(2)}, u32[]{:S(2)}) async-start(bf16[8,32,384]{2,1,0:T(8,128)(2,1)} %fusion.57), calls=%async_computation.3 | async-start | bytes 393216 | tf_op jit(solution)/shard_map/all_to_all | solution.py:55
  391.2 28.2 %copy-start.51 = (bf16[32,1024]{1,0:T(8,128)(2,1)S(1)}, bf16[32,1024]{1,0:T(8,128)(2,1)}, u32[]{:S(2)}) copy-start(bf16[32,1024]{1,0:T(8,128)(2,1)} %param.25) | copy-start | bytes 196612
  391.2 26.6 %collective-permute-start.38 = (bf16[256,1024]{1,0:T(8,128)(2,1)}, bf16[256,1024]{1,0:T(8,128)(2,1)S(1)}, u32[]{:S(2)}, u32[]{:S(2)}) collective-permute-start(bf16[256,1024]{1,0:T(8,128)(2,1)} %get-tuple-element.119), channel_id=1, source_target_pairs={{0,2},{4,0},{8,4},{12,8},{14,12},{10,14},{6,10},{2,6},{1,3},{5,1},... | collective-permute-start | bytes 1572872 | tf_op jit(solution)/shard_map/ppermute | solution.py:46
  395.6 24.6 %copy-start.53 = (bf16[32,1024]{1,0:T(8,128)(2,1)S(1)}, bf16[32,1024]{1,0:T(8,128)(2,1)}, u32[]{:S(2)}) copy-start(bf16[32,1024]{1,0:T(8,128)(2,1)} %param.27) | copy-start | bytes 196612
  395.6 25.4 %copy-start.57 = (bf16[32]{0:T(256)(128)(2,1)S(1)}, bf16[32]{0:T(256)(128)(2,1)}, u32[]{:S(2)}) copy-start(bf16[32]{0:T(256)(128)(2,1)} %param.24) | copy-start | bytes 196
  395.6 37.0 %copy-start = (bf16[1,256,1024]{2,1,0:T(8,128)(2,1)S(1)}, bf16[1,256,1024]{2,1,0:T(8,128)(2,1)}, u32[]{:S(2)}) copy-start(bf16[1,256,1024]{2,1,0:T(8,128)(2,1)} %param.18) | copy-start | bytes 1572868
  400.1 34.1 %copy-start.24 = (f32[256,1024]{1,0:T(8,128)S(1)}, f32[256,1024]{1,0:T(8,128)}, u32[]{:S(2)}) copy-start(f32[256,1024]{1,0:T(8,128)} %get-tuple-element.86) | copy-start | bytes 3145732
  400.9 20.6 %collective-permute-start.35 = (bf16[256,1024]{1,0:T(8,128)(2,1)S(1)}, bf16[256,1024]{1,0:T(8,128)(2,1)S(1)}, u32[]{:S(2)}, u32[]{:S(2)}) collective-permute-start(bf16[256,1024]{1,0:T(8,128)(2,1)S(1)} %copy-done.46), channel_id=1, source_target_pairs={{0,4},{4,8},{8,12},{12,14},{14,10},{10,6},{6,2},{2,0},{1,5},{5,9},... | collective-permute-start | bytes 1572872 | tf_op jit(solution)/shard_map/ppermute | solution.py:46
  419.1 13.5 %collective-permute-start.39 = (bf16[256,1024]{1,0:T(8,128)(2,1)S(1)}, bf16[256,1024]{1,0:T(8,128)(2,1)S(1)}, u32[]{:S(2)}, u32[]{:S(2)}) collective-permute-start(bf16[256,1024]{1,0:T(8,128)(2,1)S(1)} %fusion.30), channel_id=1, source_target_pairs={{0,2},{4,0},{8,4},{12,8},{14,12},{10,14},{6,10},{2,6},{1,3},{5,1},... | collective-permute-start | bytes 1572872 | tf_op jit(solution)/shard_map/ppermute | solution.py:46
  437.6 1.5 collective-permute-start.42
  439.3 7.6 %collective-permute-start.43 = (bf16[2,32,1408]{2,1,0:T(8,128)(2,1)S(1)}, bf16[2,32,1408]{2,1,0:T(8,128)(2,1)S(1)}, u32[]{:S(2)}, u32[]{:S(2)}) collective-permute-start(bf16[2,32,1408]{2,1,0:T(8,128)(2,1)S(1)} %get-tuple-element.146), channel_id=1, source_target_pairs={{0,16},{16,0},{1,17},{17,1},{2,18},{18,2},{3,19},{19,3},{4,20},{20... | collective-permute-start | bytes 540680 | tf_op jit(solution)/shard_map/ppermute | solution.py:41
  (49 other events, 214.7 us)
Sparse Core Ops, SparseCore 0:
  64.6 91.4 all-gather.2
  291.3 122.9 reduce-scatter.1
